TPU v7x, 32 devices: a whole 2x2x4 slice. The times are simulated.
32 devices in a mesh: groups: 2 (over x), pairs: 16 (over z, y, core).
Axes of the slice: x: 2, y: 2, z: 4, core: 2. Of those that a mesh axis runs over, the one named last changes fastest.
Arguments:
- traces: bfloat16 [128, 3, 4096], P(('groups', 'pairs')), parts along dimension 0, may hold values from -6 to 6
- gaps: int32 [128, 2], P(('groups', 'pairs')), parts along dimension 0, may hold values 0 or 1
- assign: int32 [128], P('groups'), parts along dimension 0, may hold values from 0 to 3, as said below
- target: int32 [32], P('groups'), parts along dimension 0, may hold values from 0 to 3, as said below
Outputs:
- correlations: bfloat16 [128, 16, 2, 9, 256], P(('groups', 'pairs')), parts along dimension 0
- energy: float32 [128, 9], P(('groups', 'pairs')), parts along dimension 0
There are 2 independent parts, one for each index of `groups`. A program takes and returns all parts, laid end to end along the dimension named above; each array names one. Nothing has to cross between parts.
Inputs may be any that keep to these rules, and one draw needn't show every extreme that they name: `assign`: the 4 stations of one owner name at most 2 stations of any block; in every draw one block takes exactly 2 stations of every owner. `target`: in every draw some owner names the block that takes 2 stations of every owner.
All inputs are finite; a program needn't handle non-finite values. No bound on the sum of `gaps` on one device may be relied on, other than what follows from the above.
Results may differ from a plain program's by a relative error of at most 0.0075.
Values may be sent and summed in bfloat16 or wider, within the bound.
No kernel may reach another device: no remote copies, remote signals or barrier semaphores. Data moves between devices by JAX's collectives and lax.ppermute only.
A program may use at most 128 MiB of HBM per device.

v0:
```python
import math

import jax
import jax.numpy as jnp
from jax import lax
from jax.sharding import PartitionSpec as P

SEG = 2048
FREQ = 512
FLO = 64
LAGS = 256
HALF = 21
CAP = 2


def dft_table():
    samples = jnp.arange(SEG, dtype=jnp.int32)[:, None]
    bins = FLO + jnp.arange(FREQ, dtype=jnp.int32)[None, :]
    phase = jnp.mod(samples * bins, SEG).astype(jnp.float32) * (2.0 * math.pi / SEG)
    return jnp.concatenate([jnp.cos(phase), -jnp.sin(phase)], axis=1).astype(jnp.bfloat16)


def lag_table():
    bins = FLO + jnp.arange(FREQ, dtype=jnp.int32)[:, None]
    shifts = jnp.arange(LAGS, dtype=jnp.int32)[None, :] - LAGS // 2
    phase = jnp.mod(bins * shifts, SEG).astype(jnp.float32) * (2.0 * math.pi / SEG)
    return jnp.concatenate([jnp.cos(phase), -jnp.sin(phase)], axis=0).astype(jnp.bfloat16)


def smooth_band():
    column = jnp.arange(FREQ, dtype=jnp.int32)
    band = (jnp.abs(column[:, None] - column[None, :]) <= HALF).astype(jnp.float32)
    return (band, jnp.sum(band, axis=0))


def whiten_all(traces, gaps):
    stations = traces.shape[0]
    windows = gaps.shape[1]
    segments = traces.reshape(stations * 3 * windows, SEG)
    spectra = jnp.dot(segments, dft_table(), preferred_element_type=jnp.float32)
    spectra = spectra.reshape(stations, 3, windows, 2, FREQ)
    power = jnp.sum(spectra * spectra, axis=(1, 3)) / 3.0
    band, bin_count = smooth_band()
    smooth = jnp.dot(power.reshape(-1, FREQ), band, precision=lax.Precision.HIGHEST)
    smooth = smooth.reshape(stations, windows, FREQ) / bin_count
    factor = gaps.astype(jnp.float32)[:, :, None] / jnp.sqrt(smooth + 1e-06)
    return (spectra * factor[:, None, :, None, :]).astype(jnp.bfloat16)


def station_ranks(owner_assign):
    own_count = owner_assign.shape[1]
    same = owner_assign[:, :, None] == owner_assign[:, None, :]
    order = jnp.arange(own_count, dtype=jnp.int32)
    before = order[:, None] < order[None, :]
    return jnp.sum((same & before[None, :, :]).astype(jnp.int32), axis=1)


def correlate_block(whitened, own_mask, partner, partner_mask, lag_tab):
    own_count = whitened.shape[0]
    slot_count = partner.shape[0]
    real_part = partner[:, :, :, 0]
    imag_part = partner[:, :, :, 1]
    quad = jnp.stack(
        [jnp.stack([real_part, imag_part], 3), jnp.stack([-imag_part, real_part], 3)], 4
    )
    cross = jnp.einsum("icwrf,jdwrof->ijcdof", whitened, quad, preferred_element_type=jnp.float32)
    cross = cross.astype(jnp.bfloat16)
    lagged = jnp.dot(cross.reshape(-1, 2 * FREQ), lag_tab, preferred_element_type=jnp.float32)
    lagged = lagged.reshape(own_count, slot_count, 9, LAGS)
    counts = jnp.dot(own_mask, partner_mask.T, precision=lax.Precision.HIGHEST)
    scale = 1.0 / (jnp.maximum(counts, 1.0) * math.sqrt(FREQ))
    return (lagged * scale[:, :, None, None]).astype(jnp.bfloat16)


def correlate_slots(whitened, own_mask, partner, partner_mask):
    own_count = whitened.shape[0]
    windows = whitened.shape[2]
    senders = partner.shape[0]
    width = partner.shape[1]
    stride = min(senders, 16)
    lag_tab = lag_table()
    initial = jnp.zeros((own_count, senders, width, 9, LAGS), jnp.bfloat16)

    def advance(position, filled):
        start = position * stride
        piece = lax.dynamic_slice_in_dim(partner, start, stride, 0)
        piece = piece.reshape(stride * width, 3, windows, 2, FREQ)
        mask_piece = lax.dynamic_slice_in_dim(partner_mask, start, stride, 0)
        mask_piece = mask_piece.reshape(stride * width, windows).astype(jnp.float32)
        result = correlate_block(whitened, own_mask, piece, mask_piece, lag_tab)
        result = result.reshape(own_count, stride, width, 9, LAGS)
        return lax.dynamic_update_slice_in_dim(filled, result, start, 1)

    return lax.fori_loop(0, senders // stride, advance, initial)


def on_device(traces, gaps, assign, target):
    whitened = whiten_all(traces, gaps)
    own_count = whitened.shape[0]
    owners = lax.axis_size("pairs")
    my_index = lax.axis_index("pairs")
    own_mask = gaps.astype(jnp.float32)
    station_rows = whitened.reshape(own_count, -1)
    mask_rows = gaps.astype(jnp.bfloat16)
    owner_assign = assign.reshape(owners, own_count)
    ranks = station_ranks(owner_assign)
    slot_ids = jnp.arange(CAP, dtype=jnp.int32)
    wanted = lax.dynamic_index_in_dim(target, my_index, 0, keepdims=False)
    select_in = (
        (owner_assign == wanted)[:, None, :] & (ranks[:, None, :] == slot_ids[None, :, None])
    ).astype(jnp.bfloat16)
    my_assign = lax.dynamic_index_in_dim(owner_assign, my_index, 0, keepdims=False)
    my_ranks = lax.dynamic_index_in_dim(ranks, my_index, 0, keepdims=False)
    select_out = (
        (my_assign[None, :] == target[:, None])[:, None, :]
        & (my_ranks[None, None, :] == slot_ids[None, :, None])
    ).astype(jnp.bfloat16)
    everyone, every_mask = (
        lax.all_gather(station_rows, "pairs", axis=0, tiled=True),
        lax.all_gather(mask_rows, "pairs", axis=0, tiled=True),
    )
    partner = jnp.einsum(
        "ecs,esr->ecr",
        select_in,
        everyone.reshape(owners, own_count, -1),
        preferred_element_type=jnp.float32,
    ).astype(jnp.bfloat16)
    partner_mask = jnp.einsum(
        "ecs,esw->ecw",
        select_in,
        every_mask.reshape(owners, own_count, -1),
        preferred_element_type=jnp.float32,
    ).astype(jnp.bfloat16)
    correlations = correlate_slots(whitened, own_mask, partner, partner_mask)
    slot_energy = jnp.sum(jnp.square(correlations.astype(jnp.float32)), axis=(0, 4))
    returned = lax.all_to_all(slot_energy, "pairs", split_axis=0, concat_axis=0, tiled=True)
    energy = jnp.einsum(
        "pcs,pcq->sq", select_out.astype(jnp.float32), returned, precision=lax.Precision.HIGHEST
    )
    energy = energy / float(owners * LAGS)
    return (correlations, energy)


def solution(mesh):
    in_specs = (
        P(("groups", "pairs"), None, None),
        P(("groups", "pairs"), None),
        P("groups"),
        P("groups"),
    )
    out_specs = (P(("groups", "pairs"), None, None, None, None), P(("groups", "pairs"), None))
    return jax.shard_map(
        on_device, mesh=mesh, in_specs=in_specs, out_specs=out_specs, check_vma=False
    )
```

profile of v0, /device:TPU:0, one launch (start us, length us, event | category | flops | bytes accessed | tf_op | source)
XLA Modules:
  0.0 122.6 jit_solution(12688342774132318976)
XLA Ops:
  0.7 0.1 convert_reduce_fusion
  0.8 1.0 copy.74
  1.7 0.1 reshape.137
  1.8 17.0 %cosine_convert_fusion = (bf16[2048,512]{1,0:T(8,128)(2,1)S(1)}, bf16[2048,512]{1,0:T(8,128)(2,1)S(1)}) fusion(s32[512]{0:T(512)S(1)} %iota_add_fusion), kind=kLoop, calls=%fused_computation.14 | loop fusion | flops 17825792 | bytes 4196352 | tf_op jit(solution)/shard_map/convert.2
  18.8 0.0 copy-start.1
  18.8 0.0 copy-start.2
  18.9 0.0 copy-start.3
  18.9 0.6 fusion.14
  19.5 0.1 reshape.139
  19.6 0.1 reshape.138
  19.7 0.1 reshape.136
  19.8 0.1 copy.71
  19.9 0.6 dynamic_slice.17
  20.5 0.6 broadcast_compare_fusion
  21.1 0.1 convert_reduce_fusion.1
  21.2 0.1 copy.73
  21.3 0.1 multiply_reduce_fusion.1
  21.4 0.3 fusion.19
  21.8 0.1 mul.96
  22.0 25.5 %all-gather = bf16[16,4,6144]{2,1,0:T(4,128)(2,1)S(1)} all-gather(bf16[1,4,6144]{2,1,0:T(4,128)(2,1)S(1)} %fusion.31), channel_id=1, replica_groups=mesh['groups'=2,'pairs'=16] {'pairs'}, dimensions={0}, use_global_device_ids=true | all-gather | bytes 835584 | tf_op jit(solution)/shard_map/all_gather | solution.py:119
  47.5 0.6 convolution_convert_fusion
  48.0 0.2 reshape.141
  48.3 0.2 stack.20
  48.5 0.5 iota_add_fusion.1
  49.1 17.4 %all-gather.1 = bf16[16,4,2]{1,2,0:T(2,128)(2,1)S(1)} all-gather(bf16[1,4,2]{1,2,0:T(2,128)(2,1)S(1)} %get-tuple-element.44), channel_id=1, replica_groups=mesh['groups'=2,'pairs'=16] {'pairs'}, dimensions={0}, use_global_device_ids=true | all-gather | bytes 272 | tf_op jit(solution)/shard_map/all_gather | solution.py:120
  66.5 0.1 convolution_convert_fusion.1
  66.7 0.8 fusion.22
  67.4 1.7 %copy.88 = bf16[4,3,2,2,512,1,1]{0,2,3,1,6,5,4:T(2,128)(2,1)S(1)} copy(bf16[4,3,2,2,512,1,1]{4,3,2,1,0,6,5:T(2,128)(2,1)S(1)} %fusion.32) | data formatting | bytes 98304 | tf_op jit(solution)/shard_map/convert_element_type | solution.py:47
  69.2 0.5 fusion.48
  69.7 0.1 copy.95
  69.8 0.1 copy_negate_fusion
  69.9 0.8 pad_maximum_fusion
  70.7 3.5 %copy.79 = bf16[32,3,2,2,512]{0,2,3,1,4:T(2,128)(2,1)S(1)} copy(bf16[32,3,2,2,512]{4,0,3,2,1:T(8,128)(2,1)} %pad_maximum_fusion) | data formatting | bytes 786432 | tf_op jit(solution)/shard_map/while/body/eval_jaxpr/stack | solution.py:64
  74.2 3.1 %copy.80 = bf16[32,3,2,2,1,512]{0,2,3,4,1,5:T(2,128)(2,1)} copy(bf16[32,3,2,2,1,512]{5,3,2,1,0,4:T(2,128)(2,1)S(1)} %stack.20) | data formatting | bytes 786432 | tf_op jit(solution)/shard_map/while/body/eval_jaxpr/stack | solution.py:63
  77.3 11.5 %fusion = bf16[4,32,3,3,2,512]{1,0,2,4,3,5:T(4,128)(2,1)} fusion(bf16[4,3,2,2,512,1,1]{0,2,3,1,6,5,4:T(2,128)(2,1)S(1)} %copy.88, bf16[32,3,2,2,1,512]{0,2,3,4,1,5:T(2,128)(2,1)S(1)} %bitcast.54, bf16[32,3,2,2,1,512]{0,2,3,4,1,5:T(2,128)(2,1)} %copy.80), kind=kOutput, calls=%fused_computation.1 | convolution fusion | flops 12189696 | bytes 3194880 | tf_op jit(solution)/shard_map/while/body/eval_jaxpr/icwrf,jdwrof->ijcdof/dot_general | solution.py:66
  88.8 14.3 %copy.82 = bf16[4,32,3,3,2,512]{5,4,1,3,2,0:T(2,128)(2,1)S(1)} copy(bf16[4,32,3,3,2,512]{1,0,2,4,3,5:T(4,128)(2,1)} %fusion) | data formatting | bytes 4718592 | tf_op jit(solution)/shard_map/while/body/eval_jaxpr/convert_element_type | solution.py:67
  103.1 0.0 copy-start.5
  103.1 2.9 %dot_general.36 = bf16[4,32,9,1024]{3,1,2,0:T(8,128)(2,1)} reshape(bf16[4,32,3,3,2,512]{5,4,1,3,2,0:T(2,128)(2,1)S(1)} %copy.82) | data formatting | bytes 4718592 | tf_op jit(solution)/shard_map/while/body/eval_jaxpr/dot_general | solution.py:68
  106.1 2.5 %cosine_convert_fusion.1 = (bf16[512,256]{1,0:T(8,128)(2,1)S(1)}, bf16[512,256]{1,0:T(8,128)(2,1)S(1)}) fusion(s32[256]{0:T(256)S(1)} %copy-done, s32[512]{0:T(512)S(1)} %iota_add_fusion), kind=kLoop, calls=%fused_computation.51 | loop fusion | flops 2228224 | bytes 527360 | tf_op jit(solution)/shard_map/convert
  108.6 2.5 %multiply_reduce_fusion = (f32[32,9]{0,1:T(8,128)S(1)}, bf16[4,32,9,256]{3,1,2,0:T(8,128)(2,1)S(1)}) fusion(f32[4,32]{1,0:T(4,128)S(1)} %copy-done.5, bf16[4,32,9,1024]{3,1,2,0:T(8,128)(2,1)} %dot_general.36, bf16[512,256]{1,0:T(8,128)(2,1)S(1)} %get-tuple-element.41, bf16[512,256]{1,0:T(8,128)(2,1)S(1)} %get-tuple-element.40), kind=kOutput, calls=%fused_computation.23 | convolution fusion | flops 606502656 | bytes 3475072 | tf_op jit(solution)/shard_map/while/body/eval_jaxpr/dot_general | solution.py:68
  111.1 0.7 copy.84
  111.8 3.5 %all-to-all-start = ((f32[16,2,9]{2,1,0:T(2,128)}), f32[16,2,9]{2,1,0:T(2,128)S(1)}, u32[]{:S(2)}, u32[]{:S(2)}) async-start(f32[16,2,9]{2,1,0:T(2,128)} %bitcast.17), calls=%async_computation | async-start | bytes 32768 | tf_op jit(solution)/shard_map/all_to_all | solution.py:136
  115.3 0.2 dynamic-slice_reduce_fusion
  115.5 0.1 broadcast_compare_fusion.1
  115.6 0.2 reshape.144
  115.8 1.2 copy.86
  117.0 4.7 %all-to-all-done = f32[16,2,9]{2,1,0:T(2,128)S(1)} async-done(((f32[16,2,9]{2,1,0:T(2,128)}), f32[16,2,9]{2,1,0:T(2,128)S(1)}, u32[]{:S(2)}, u32[]{:S(2)}) %all-to-all-start) | async-done | bytes 1184 | tf_op jit(solution)/shard_map/all_to_all | solution.py:136
  121.7 0.8 fusion.23
  (17 shorter events, 0.2 us)
Async XLA Ops:
  18.8 0.9 copy-start.1
  18.8 0.9 copy-start.2
  18.9 1.0 copy-start.3
  103.1 2.9 %copy-start = (s32[256]{0:T(256)S(1)}, s32[256]{0:T(256)}, u32[]{:S(2)}) copy-start(s32[256]{0:T(256)} %iota_add_fusion.1) | copy-start | bytes 3076
  103.1 5.4 %copy-start.5 = (f32[4,32]{1,0:T(4,128)S(1)}, f32[4,32]{1,0:T(4,128)}, u32[]{:S(2)}) copy-start(f32[4,32]{1,0:T(4,128)} %fusion.22) | copy-start | bytes 1540
  106.0 9.4 %copy-start.4 = (s32[16]{0:T(128)S(1)}, s32[16]{0:T(128)}, u32[]{:S(2)}) copy-start(s32[16]{0:T(128)} %param.7) | copy-start | bytes 196
  111.8 10.0 %all-to-all-start = ((f32[16,2,9]{2,1,0:T(2,128)}), f32[16,2,9]{2,1,0:T(2,128)S(1)}, u32[]{:S(2)}, u32[]{:S(2)}) async-start(f32[16,2,9]{2,1,0:T(2,128)} %bitcast.17), calls=%async_computation | async-start | bytes 32768 | tf_op jit(solution)/shard_map/all_to_all | solution.py:136
where the time goes:
time: 123 us
  blocking collectives  42.9 us (35%)
  local copies, waits for them, and re-layouts  31.3 us (25%)
  other arithmetic  21.9 us (18%)
  matrix products  17.3 us (14%)
  waiting for transfers between devices  4.73 us (4%)
  starting transfers between devices  3.49 us (3%)
    all_gather x1, blocking collectives, on_device(): lax.all_gather(station_rows, 'pairs', axis=0, tiled=True)  25.5 us
    another operation x2, other arithmetic  19.5 us
    all_gather x1, blocking collectives, on_device(): lax.all_gather(mask_rows, 'pairs', axis=0, tiled=True)  17.4 us
    convert_element_type x1, local copies, waits for them, and re-layouts, correlate_block(): cross = cross.astype(jnp.bfloat16)  14.3 us
    dot_general x1, matrix products, correlate_block(): jnp.einsum('icwrf,jdwrof->ijcdof', whitened, quad, preferred_element_type...  11.5 us
    all_to_all x1, waiting for transfers between devices, on_device(): lax.all_to_all(slot_energy, 'pairs', split_axis=0, concat_axis=0, tiled=T...  4.73 us
    another operation x1, local copies, waits for them, and re-layouts, correlate_block(): jnp.stack([-imag_part, real_part], 3)  3.52 us
    all_to_all x1, starting transfers between devices, on_device(): lax.all_to_all(slot_energy, 'pairs', split_axis=0, concat_axis=0, tiled=T...  3.49 us
  transfers between devices with their start and end apart: 1, of which 1 were waited for; matrix products, arithmetic and copies ran while one was open for 1% of the time, Pallas kernels for 0%

commit v1 on v0

v1 whole, which is shorter than its diff:
```python
import functools
import math

import jax
import jax.numpy as jnp
import numpy as np
from jax import lax
from jax.experimental import pallas as pl
from jax.experimental.pallas import tpu as pltpu
from jax.sharding import PartitionSpec as P

SEG = 2048
FREQ = 512
FLO = 64
LAGS = 256
HALF = 21
CAP = 2
COMP = 3
RADIX = 4
LANE = 128
NONE = -1000
PART = SEG // RADIX
PLANE = 2 * COMP * FREQ
WIDE = PLANE + LANE
GROUP = 4


def bin_order():
    spot = np.arange(FREQ)
    return RADIX * (spot % LANE) + spot // LANE


def dft_table():
    n1 = np.arange(PART)[:, None]
    blocks = []
    for r in (0, 2, 1, 3):
        k = FLO + RADIX * np.arange(LANE)[None, :] + r
        phase = np.mod(n1 * k, SEG) * (2.0 * math.pi / SEG)
        c, s = np.cos(phase), np.sin(phase)
        blocks.append(np.concatenate([c, -s], 1))
        if r == 1:
            blocks.append(np.concatenate([-s, -c], 1))
        if r == 3:
            blocks.append(np.concatenate([s, c], 1) * np.array([1.0]))
    return np.concatenate(blocks, 0).astype(jnp.bfloat16)


def band_table():
    f = bin_order()
    band = np.abs(f[:, None] - f[None, :]) <= HALF
    share = 1.0 / (float(COMP) * band.sum(0, keepdims=True))
    return band.astype(jnp.bfloat16), share.astype(np.float32)


def lag_table():
    bins = FLO + bin_order()[:, None]
    shifts = np.arange(LAGS)[None, :] - LAGS // 2
    phase = np.mod(bins * shifts, SEG) * (2.0 * math.pi / SEG)
    return np.concatenate([np.cos(phase), -np.sin(phase)], 0).astype(jnp.bfloat16)


def mm(a, b):
    return jnp.dot(a, b, preferred_element_type=jnp.float32)


def front_kernel(gaps_ref, x_ref, tab_ref, band_ref, share_ref, out_ref):
    windows, own = gaps_ref.shape
    rows = windows * own
    quarter = []
    for j in range(RADIX):
        per_comp = []
        for a in range(COMP):
            pieces = [
                x_ref[a, :, w * SEG + j * PART : w * SEG + (j + 1) * PART].astype(jnp.float32)
                for w in range(windows)
            ]
            per_comp.append(jnp.concatenate(pieces, 0))
        quarter.append(jnp.concatenate(per_comp, 0))
    x0, x1, x2, x3 = quarter
    even, odd = x0 + x2, x1 + x3

    def halves(y):
        low = y - y.astype(jnp.bfloat16).astype(jnp.float32)
        return jnp.concatenate([y, low], 0).astype(jnp.bfloat16)

    zero, two = halves(even + odd), halves(even - odd)
    u, v = halves(x0 - x2), halves(x1 - x3)
    tab = lambda i: tab_ref[i * PART : (i + 1) * PART, :]
    both = [
        mm(zero, tab(0)),
        mm(u, tab(2)) + mm(v, tab(3)),
        mm(two, tab(1)),
        mm(u, tab(4)) + mm(v, tab(5)),
    ]
    count = COMP * rows
    spec = [d[:count] + d[count:] for d in both]
    power = []
    for d in spec:
        total = jnp.zeros((rows, LANE), jnp.float32)
        for a in range(COMP):
            re = d[a * rows : (a + 1) * rows, :LANE]
            im = d[a * rows : (a + 1) * rows, LANE:]
            total = total + (re * re + im * im)
        power.append(total)
    power = jnp.concatenate(power, 1)
    p1 = power.astype(jnp.bfloat16).astype(jnp.float32)
    rest = power - p1
    p2 = rest.astype(jnp.bfloat16).astype(jnp.float32)
    p3 = rest - p2
    sums = mm(jnp.concatenate([p1, p2, p3], 0).astype(jnp.bfloat16), band_ref[...])
    smooth = (sums[:rows] + sums[rows : 2 * rows] + sums[2 * rows :]) * share_ref[...]
    row_at = lax.broadcasted_iota(jnp.int32, (rows, LANE), 0)
    flags = jnp.zeros((rows, LANE), jnp.float32)
    for w in range(windows):
        for s in range(own):
            flags = jnp.where(row_at == w * own + s, gaps_ref[w, s].astype(jnp.float32), flags)
    wide_flags = jnp.concatenate([flags] * RADIX, 1)
    factor = wide_flags / jnp.sqrt(smooth + 1e-06)
    for a in range(COMP):
        for part in range(2):
            whole = jnp.concatenate(
                [d[a * rows : (a + 1) * rows, part * LANE : (part + 1) * LANE] for d in spec], 1
            )
            start = (2 * a + part) * FREQ
            out_ref[:, start : start + FREQ] = (whole * factor).astype(jnp.bfloat16)
    out_ref[:, PLANE:] = flags.astype(jnp.bfloat16)


def front(traces, gaps):
    own, comps, length = traces.shape
    windows = gaps.shape[1]
    assert comps == COMP and length == windows * SEG
    band, share = band_table()
    vmem = pl.BlockSpec(memory_space=pltpu.VMEM)
    return pl.pallas_call(
        front_kernel,
        out_shape=jax.ShapeDtypeStruct((windows * own, WIDE), jnp.bfloat16),
        in_specs=[pl.BlockSpec(memory_space=pltpu.SMEM)] + [vmem] * 4,
        out_specs=vmem,
        name="front",
    )(
        gaps.T,
        traces.transpose(1, 0, 2),
        jnp.asarray(dft_table()),
        jnp.asarray(band),
        jnp.asarray(share),
    )


def exchange_masks(count):
    bits = int(count).bit_length() - 1
    assert count == 1 << bits and bits >= 3
    chips = [1 << b for b in range(bits - 1, 0, -1)]
    return [chips + [1], chips + [1]]


def slot_masks(masks):
    found = [0]
    for m in masks:
        found = found + [f ^ m for f in found]
    return found


def correlate_kernel(
    owners, own_rows, windows, assign_ref, target_ref, order_ref, all_ref, lag_ref, out_ref, energy_ref,
    self_f32, picked, pickx, picky, cross, result, outv, acc, sem,
):
    own = own_rows // windows
    me = lax.axis_index("pairs")
    chunk_rows = GROUP * own_rows
    pairs = GROUP * CAP
    stations = GROUP * own
    half = own * COMP * COMP * pairs
    self_f32[...] = all_ref[0:own_rows, :].astype(jnp.float32)
    acc[...] = jnp.zeros_like(acc)
    my_target = target_ref[me]

    def first_two(flags):
        found = [jnp.int32(NONE)] * CAP
        seen = jnp.int32(0)
        for s, flag in enumerate(flags):
            for c in range(CAP):
                found[c] = jnp.where(jnp.logical_and(flag, seen == c), s, found[c])
            seen = seen + flag.astype(jnp.int32)
        return found

    def one_chunk(ch, carry):
        slot = lax.rem(ch, 2)
        ids = [order_ref[ch * GROUP + j] for j in range(GROUP)]
        theirs, mine, yours = [], [], []
        for j in range(GROUP):
            theirs.append(first_two([assign_ref[ids[j] * own + s] == my_target for s in range(own)]))
            want = target_ref[ids[j]]
            mine.append(first_two([assign_ref[me * own + s] == want for s in range(own)]))
        chunk = all_ref[pl.ds(pl.multiple_of(ch * chunk_rows, chunk_rows), chunk_rows), :]

        def one_hot(row_count, cols, want):
            col = lax.broadcasted_iota(jnp.int32, (row_count, cols), 1)
            return jnp.where(col == want, 1.0, 0.0).astype(jnp.bfloat16)

        def iota(row_count, cols):
            return lax.broadcasted_iota(jnp.int32, (row_count, cols), 0)

        row = iota(windows * pairs, chunk_rows)
        within = row % pairs
        want = jnp.full(row.shape, NONE, jnp.int32)
        for j in range(GROUP):
            for c in range(CAP):
                want = jnp.where(within == j * CAP + c, theirs[j][c] + j * own_rows, want)
        sel = one_hot(windows * pairs, chunk_rows, want + (row // pairs) * own)
        row = iota(windows * stations, chunk_rows)
        within = row % stations
        want = (within // own) * own_rows + (row // stations) * own + within % own
        selx = one_hot(windows * stations, chunk_rows, want)
        moved = mm(jnp.concatenate([sel, selx], 0), chunk)
        picked[...] = moved[: windows * pairs]
        pickx[...] = moved[windows * pairs :]
        row = iota(CAP * windows * stations, own_rows)
        within = row % stations
        place = (row // (windows * stations)) * GROUP + within // own
        want = jnp.full(row.shape, NONE, jnp.int32)
        for c in range(CAP):
            for j in range(GROUP):
                want = jnp.where(place == c * GROUP + j, mine[j][c], want)
        w_at = (row // stations) % windows
        sely = one_hot(CAP * windows * stations, own_rows, want + w_at * own)
        picky[...] = mm(sely, all_ref[0:own_rows, :])

        def plane(a, part, lt):
            start = (2 * a + part) * FREQ + lt * LANE
            return pl.ds(pl.multiple_of(start, LANE), LANE)

        def product(left, right):
            re = im = None
            for w in range(windows):
                lr, li = left[w]
                rr, ri = right[w]
                r = lr * rr + li * ri
                i = li * rr - lr * ri
                re = r if re is None else re + r
                im = i if im is None else im + i
            return re, im

        def one_tile(lt, carry):
            re_at = pl.ds(pl.multiple_of(lt * LANE, LANE), LANE)
            im_at = pl.ds(pl.multiple_of(FREQ + lt * LANE, LANE), LANE)
            slots = [
                [
                    [picked[w * pairs : (w + 1) * pairs, plane(b, part, lt)] for part in range(2)]
                    for w in range(windows)
                ]
                for b in range(COMP)
            ]
            for yp in range(own // 2):
                for a in range(COMP):
                    left = []
                    for y in (2 * yp, 2 * yp + 1):
                        left.append(
                            [
                                [
                                    jnp.broadcast_to(
                                        self_f32[w * own + y : w * own + y + 1, plane(a, part, lt)],
                                        (pairs, LANE),
                                    )
                                    for part in range(2)
                                ]
                                for w in range(windows)
                            ]
                        )
                    for b in range(COMP):
                        at = ((yp * COMP + a) * COMP + b) * 2 * pairs
                        got = [product(left[y], slots[b]) for y in range(2)]
                        re = jnp.concatenate([g[0] for g in got], 0)
                        im = jnp.concatenate([g[1] for g in got], 0)
                        cross[at : at + 2 * pairs, re_at] = re.astype(jnp.bfloat16)
                        cross[at : at + 2 * pairs, im_at] = im.astype(jnp.bfloat16)
            lefts = [
                [
                    [pickx[w * stations : (w + 1) * stations, plane(a, part, lt)] for part in range(2)]
                    for w in range(windows)
                ]
                for a in range(COMP)
            ]
            for c in range(CAP):
                for b in range(COMP):
                    right = [
                        [
                            picky[
                                (c * windows + w) * stations : (c * windows + w + 1) * stations,
                                plane(b, part, lt),
                            ]
                            for part in range(2)
                        ]
                        for w in range(windows)
                    ]
                    for a in range(COMP):
                        re, im = product(lefts[a], right)
                        at = half + ((c * COMP + a) * COMP + b) * stations
                        cross[at : at + stations, re_at] = re.astype(jnp.bfloat16)
                        cross[at : at + stations, im_at] = im.astype(jnp.bfloat16)
            return carry

        lax.fori_loop(0, FREQ // LANE, one_tile, 0)
        result[...] = mm(cross[...], lag_ref[...])

        def scale_of(count):
            s = 1.0 / (jnp.maximum(count, 1.0) * math.sqrt(FREQ))
            return jnp.concatenate([s] * (LAGS // LANE), 1)

        def copies(which):
            return [
                pltpu.make_async_copy(outv.at[which, :, j], out_ref.at[:, ids[j]], sem.at[which])
                for j in range(GROUP)
            ]

        @pl.when(ch >= 2)
        def _():
            for cp in copies(slot):
                cp.wait()

        flag = lambda ref, lo, hi: ref[lo:hi, PLANE:]
        for y in range(own):
            count = None
            for w in range(windows):
                term = flag(self_f32, w * own + y, w * own + y + 1) * flag(picked, w * pairs, (w + 1) * pairs)
                count = term if count is None else count + term
            scale = scale_of(count)
            for q in range(COMP * COMP):
                at = ((y // 2) * COMP * COMP + q) * 2 * pairs + (y % 2) * pairs
                block = (result[at : at + pairs, :] * scale).astype(jnp.bfloat16)
                outv[slot, y, :, q, :, :] = block.reshape(GROUP, CAP, LAGS)
        for cp in copies(slot):
            cp.start()
        owner_row = lax.broadcasted_iota(jnp.int32, (stations, LANE), 0) // own
        for c in range(CAP):
            count = None
            for w in range(windows):
                lo = (c * windows + w) * stations
                term = flag(pickx, w * stations, (w + 1) * stations) * flag(picky, lo, lo + stations)
                count = term if count is None else count + term
            scale = scale_of(count)
            mask = []
            for y in range(own):
                m = jnp.zeros((stations, LANE), jnp.float32)
                for j in range(GROUP):
                    m = jnp.where(owner_row == j, (mine[j][c] == y).astype(jnp.float32), m)
                mask.append(m)
            for q in range(COMP * COMP):
                at = half + (c * COMP * COMP + q) * stations
                block = (result[at : at + stations, :] * scale).astype(jnp.bfloat16).astype(jnp.float32)
                square = block * block
                both = square[:, :LANE] + square[:, LANE:]
                for y in range(own):
                    acc[y * COMP * COMP + q] += both * mask[y]
        return carry

    chunks = owners // GROUP
    lax.fori_loop(0, chunks, one_chunk, 0)
    for last in range(max(chunks - 2, 0), chunks):
        for j in range(GROUP):
            pltpu.make_async_copy(
                outv.at[last % 2, :, j], out_ref.at[:, order_ref[last * GROUP + j]], sem.at[last % 2]
            ).wait()
    lane = lax.broadcasted_iota(jnp.int32, (1, LANE), 1)
    for y in range(own):
        line = jnp.zeros((1, LANE), jnp.float32)
        for q in range(COMP * COMP):
            total = jnp.sum(acc[y * COMP * COMP + q], keepdims=True).reshape(1, 1)
            line = jnp.where(lane == q, total, line)
        energy_ref[y : y + 1, :] = line[:, : COMP * COMP] / float(owners * LAGS)


def correlate(everyone, assign, target, order, own, windows):
    owners = target.shape[0]
    own_rows = own * windows
    stations, pairs = GROUP * own, GROUP * CAP
    rows = own * COMP * COMP * pairs + CAP * COMP * COMP * stations
    smem = pl.BlockSpec(memory_space=pltpu.SMEM)
    vmem = pl.BlockSpec(memory_space=pltpu.VMEM)
    f32 = jnp.float32
    return pl.pallas_call(
        functools.partial(correlate_kernel, owners, own_rows, windows),
        out_shape=(
            jax.ShapeDtypeStruct((own, owners, COMP * COMP, CAP, LAGS), jnp.bfloat16),
            jax.ShapeDtypeStruct((own, COMP * COMP), f32),
        ),
        in_specs=[smem] * 3 + [vmem] * 2,
        out_specs=(pl.BlockSpec(memory_space=pl.ANY), vmem),
        scratch_shapes=[
            pltpu.VMEM((own_rows, WIDE), f32),
            pltpu.VMEM((windows * pairs, WIDE), f32),
            pltpu.VMEM((windows * stations, WIDE), f32),
            pltpu.VMEM((CAP * windows * stations, WIDE), f32),
            pltpu.VMEM((rows, 2 * FREQ), jnp.bfloat16),
            pltpu.VMEM((rows, LAGS), f32),
            pltpu.VMEM((2, own, GROUP, COMP * COMP, CAP, LAGS), jnp.bfloat16),
            pltpu.VMEM((own * COMP * COMP, stations, LANE), f32),
            pltpu.SemaphoreType.DMA((2,)),
        ],
        compiler_params=pltpu.CompilerParams(vmem_limit_bytes=48 << 20),
        name="correlate",
    )(assign, target, order, everyone, jnp.asarray(lag_table()))


def on_device(traces, gaps, assign, target):
    own = traces.shape[0]
    windows = gaps.shape[1]
    owners = lax.axis_size("pairs")
    me = lax.axis_index("pairs")
    held = front(traces, gaps)
    masks = exchange_masks(owners)[0]
    for mask in masks:
        partner = [(i, i ^ mask) for i in range(owners)]
        held = jnp.concatenate([held, lax.ppermute(held, "pairs", partner)], 0)
    order = me ^ jnp.asarray(slot_masks(masks), jnp.int32)
    out, energy = correlate(held, assign, target, order, own, windows)
    return out.transpose(0, 1, 3, 2, 4), energy


def solution(mesh):
    in_specs = (
        P(("groups", "pairs"), None, None),
        P(("groups", "pairs"), None),
        P("groups"),
        P("groups"),
    )
    out_specs = (P(("groups", "pairs"), None, None, None, None), P(("groups", "pairs"), None))
    return jax.shard_map(
        on_device, mesh=mesh, in_specs=in_specs, out_specs=out_specs, check_vma=False
    )
```

time: 123 us -> 34.5 us (0.28)
  blocking collectives: 42.9 us -> 0 us
  local copies, waits for them, and re-layouts: 31.3 us -> 0.94 us
  other arithmetic: 21.9 us -> 2.48 us
  matrix products: 17.3 us -> 0 us
  Pallas kernels: 0 us -> 11.6 us
  waiting for transfers between devices: 4.73 us -> 11 us
  starting transfers between devices: 3.49 us -> 7.35 us
    all_gather x2 -> x0, blocking collectives: 42.9 us -> none  [the longest x1 25.5 us: on_device(): lax.all_gather(station_rows, 'pairs', axis=0, tiled=True)]
    another operation x3 -> x0, other arithmetic: 20.2 us -> none
    dot_general x8 -> x0, matrix products: 17.3 us -> none  [the longest x1 11.5 us: correlate_block(): jnp.einsum('icwrf,jdwrof->ijcdof', whitened, quad, preferred_element_type...]
    convert_element_type x2 -> x0, local copies, waits for them, and re-layouts: 16.1 us -> none  [the longest x1 14.3 us: correlate_block(): cross = cross.astype(jnp.bfloat16)]
    pallas_call x0 -> x2, Pallas kernels: none -> 11.6 us  [the longest x1 8.81 us: correlate(): pl.pallas_call(functools.partial(correlate_kernel, owners, own_rows, wind...]
    ppermute x0 -> x4, waiting for transfers between devices: none -> 11 us  [on_device(): held = jnp.concatenate([held, lax.ppermute(held, 'pairs', partner)], 0)]
    ppermute x0 -> x4, starting transfers between devices: none -> 7.35 us  [on_device(): held = jnp.concatenate([held, lax.ppermute(held, 'pairs', partner)], 0)]
    another operation x3 -> x0, local copies, waits for them, and re-layouts: 6.85 us -> none  [the longest x1 3.52 us: correlate_block(): jnp.stack([-imag_part, real_part], 3)]
  transfers between devices with their start and end apart: 1 -> 4, of which waited for: 1 -> 4; matrix products, arithmetic and copies ran while one was open for 1% -> 3% of each run, Pallas kernels for 0% -> 0%
where the time goes in v1:
time: 34.5 us; the launch traced here: 34.1 us
  Pallas kernels  11.6 us (34%)
  waiting for transfers between devices  11 us (32%)
  starting transfers between devices  7.35 us (21%)
  other arithmetic  2.48 us (7%)
  local copies, waits for them, and re-layouts  0.94 us (3%)
  between operations  0.69 us (2%)
    ppermute x4, waiting for transfers between devices, on_device(): held = jnp.concatenate([held, lax.ppermute(held, 'pairs', partner)], 0)  11 us
    pallas_call x1, Pallas kernels, correlate(): pl.pallas_call(functools.partial(correlate_kernel, owners, own_rows, wind...  8.81 us
    ppermute x4, starting transfers between devices, on_device(): held = jnp.concatenate([held, lax.ppermute(held, 'pairs', partner)], 0)  7.35 us
    pallas_call x1, Pallas kernels, front(): pl.pallas_call(front_kernel, out_shape=jax.ShapeDtypeStruct((windows * ow...  2.82 us
    concatenate x3, other arithmetic, on_device(): held = jnp.concatenate([held, lax.ppermute(held, 'pairs', partner)], 0)  2.48 us
    unnamed x12, local copies, waits for them, and re-layouts  0.91 us
  transfers between devices with their start and end apart: 4, of which 4 were waited for; matrix products, arithmetic and copies ran while one was open for 3% of the time, Pallas kernels for 0%

profile of v1, /device:TPU:0, one launch (start us, length us, event | category | flops | bytes accessed | tf_op | source)
XLA Modules:
  0.0 34.1 jit_solution(3598744644972255810)
XLA Ops:
  0.6 0.0 copy-start.3
  0.6 2.8 %front.1 = bf16[8,3200]{1,0:T(8,128)(2,1)} custom-call(s32[2,4]{1,0:T(2,128)} %bitcast.4, bf16[3,4,4096]{2,1,0:T(4,128)(2,1)} %bitcast.3, bf16[3072,256]{1,0:T(8,128)(2,1)} %constant.14.clone.tab_ref, bf16[512,512]{1,0:T(8,128)(2,1)} %constant.15.clone.band_ref, f32[1,512]{1,0:T(1,128)} %constant.16.clone.share_ref), custom_call_target="tpu_custom_call" | custom-call | tf_op jit(solution)/shard_map/front/pallas_call | solution.py:135
  3.5 0.0 copy-start
  3.5 0.0 copy-start.1
  3.5 0.0 copy-start.2
  3.5 4.1 %collective-permute-start = (bf16[8,3200]{1,0:T(8,128)(2,1)}, bf16[8,3200]{1,0:T(8,128)(2,1)S(1)}, u32[]{:S(2)}, u32[]{:S(2)}) collective-permute-start(bf16[8,3200]{1,0:T(8,128)(2,1)} %front.1), channel_id=1, source_target_pairs={{0,8},{1,9},{2,10},{3,11},{4,12},{5,13},{6,14},{7,15},{8,0},{9,1},... | collective-permute-start | bytes 153608 | tf_op jit(solution)/shard_map/ppermute | solution.py:414
  7.6 0.8 %constant_dynamic-update-slice_fusion.4 = bf16[128,3200]{1,0:T(8,128)(2,1)S(1)} fusion(bf16[8,3200]{1,0:T(8,128)(2,1)} %front.1), kind=kLoop, calls=%fused_computation.7 | loop fusion | bytes 102400
  8.4 0.0 copy-done.3
  8.4 2.0 %collective-permute-done = bf16[8,3200]{1,0:T(8,128)(2,1)S(1)} collective-permute-done((bf16[8,3200]{1,0:T(8,128)(2,1)}, bf16[8,3200]{1,0:T(8,128)(2,1)S(1)}, u32[]{:S(2)}, u32[]{:S(2)}) %collective-permute-start) | collective-permute-done | bytes 51232 | tf_op jit(solution)/shard_map/ppermute | solution.py:414
  10.5 0.8 %pad_maximum_fusion.2 = bf16[16,3200]{1,0:T(8,128)(2,1)S(1)} fusion(bf16[8,3200]{1,0:T(8,128)(2,1)S(1)} %collective-permute-done, bf16[8,3200]{1,0:T(8,128)(2,1)} %front.1), kind=kLoop, calls=%fused_computation.2 | loop fusion | flops 204800 | bytes 204800 | tf_op jit(solution)/shard_map/concatenate | solution.py:414
  11.3 1.4 %collective-permute-start.1 = (bf16[16,3200]{1,0:T(8,128)(2,1)S(1)}, bf16[16,3200]{1,0:T(8,128)(2,1)S(1)}, u32[]{:S(2)}, u32[]{:S(2)}) collective-permute-start(bf16[16,3200]{1,0:T(8,128)(2,1)S(1)} %pad_maximum_fusion.2), channel_id=1, source_target_pairs={{0,4},{1,5},{2,6},{3,7},{4,0},{5,1},{6,2},{7,3},{8,12},{9,13},{10,... | collective-permute-start | bytes 307208 | tf_op jit(solution)/shard_map/ppermute | solution.py:414
  12.6 3.3 %collective-permute-done.1 = bf16[16,3200]{1,0:T(8,128)(2,1)S(1)} collective-permute-done((bf16[16,3200]{1,0:T(8,128)(2,1)S(1)}, bf16[16,3200]{1,0:T(8,128)(2,1)S(1)}, u32[]{:S(2)}, u32[]{:S(2)}) %collective-permute-start.1) | collective-permute-done | bytes 102432 | tf_op jit(solution)/shard_map/ppermute | solution.py:414
  15.9 0.8 %pad_maximum_fusion.1 = bf16[32,3200]{1,0:T(8,128)(2,1)S(1)} fusion(bf16[16,3200]{1,0:T(8,128)(2,1)S(1)} %collective-permute-done.1, bf16[8,3200]{1,0:T(8,128)(2,1)S(1)} %collective-permute-done, bf16[8,3200]{1,0:T(8,128)(2,1)} %front.1), kind=kLoop, calls=%fused_computation.1 | loop fusion | flops 614400 | bytes 409600 | tf_op jit(solution)/shard_map/concatenate | solution.py:414
  16.8 1.8 %collective-permute-start.2 = (bf16[32,3200]{1,0:T(8,128)(2,1)S(1)}, bf16[32,3200]{1,0:T(8,128)(2,1)S(1)}, u32[]{:S(2)}, u32[]{:S(2)}) collective-permute-start(bf16[32,3200]{1,0:T(8,128)(2,1)S(1)} %pad_maximum_fusion.1), channel_id=1, source_target_pairs={{0,2},{1,3},{2,0},{3,1},{4,6},{5,7},{6,4},{7,5},{8,10},{9,11},{10,... | collective-permute-start | bytes 614408 | tf_op jit(solution)/shard_map/ppermute | solution.py:414
  18.6 4.0 %collective-permute-done.2 = bf16[32,3200]{1,0:T(8,128)(2,1)S(1)} collective-permute-done((bf16[32,3200]{1,0:T(8,128)(2,1)S(1)}, bf16[32,3200]{1,0:T(8,128)(2,1)S(1)}, u32[]{:S(2)}, u32[]{:S(2)}) %collective-permute-start.2) | collective-permute-done | bytes 204832 | tf_op jit(solution)/shard_map/ppermute | solution.py:414
  22.6 0.8 %pad_maximum_fusion = bf16[64,3200]{1,0:T(8,128)(2,1)S(1)} fusion(bf16[32,3200]{1,0:T(8,128)(2,1)S(1)} %collective-permute-done.2, bf16[16,3200]{1,0:T(8,128)(2,1)S(1)} %collective-permute-done.1, bf16[8,3200]{1,0:T(8,128)(2,1)S(1)} %collective-permute-done, bf16[8,3200]{1,0:T(8,128)(2,1)} %front.1), kind=kLoop, calls=%fused_computation | loop fusion | flops 1638400 | bytes 819200 | tf_op jit(solution)/shard_map/concatenate | solution.py:414
  23.4 0.1 collective-permute-start.3
  23.5 1.7 %collective-permute-done.3 = bf16[64,3200]{1,0:T(8,128)(2,1)S(1)} collective-permute-done((bf16[64,3200]{1,0:T(8,128)(2,1)S(1)}, bf16[64,3200]{1,0:T(8,128)(2,1)S(1)}, u32[]{:S(2)}, u32[]{:S(2)}) %collective-permute-start.3) | collective-permute-done | bytes 409632 | tf_op jit(solution)/shard_map/ppermute | solution.py:414
  25.3 0.0 copy-done
  25.3 0.0 copy-done.1
  25.3 0.0 copy-done.2
  25.3 8.8 %correlate.1 = (bf16[4,16,9,2,256]{4,3,2,1,0:T(2,128)(2,1)}, f32[4,9]{1,0:T(4,128)}) custom-call(s32[64]{0:T(128)S(1)} %copy-done.1, s32[16]{0:T(128)S(1)} %copy-done.2, s32[16]{0:T(128)S(1)} %broadcast_xor_fusion.order_ref, bf16[128,3200]{1,0:T(8,128)(2,1)S(1)} %constant_dynamic-update-slice_fusion.all_ref, bf16[1024,256]{1,0:T(8,128)(2,1)S(1)} %copy-done), custom_call_target="tpu_custom_call" | custom-call | tf_op jit(solution)/shard_map/correlate/pallas_call | solution.py:381
  (5 shorter events, 0.1 us)
Async XLA Ops:
  0.6 7.8 %copy-start.3 = (s32[16]{0:T(128)S(1)}, s32[16]{0:T(128)}, u32[]{:S(2)}) copy-start(s32[16]{0:T(128)} %constant.17.clone) | copy-start | bytes 196
  3.5 21.8 %copy-start = (bf16[1024,256]{1,0:T(8,128)(2,1)S(1)}, bf16[1024,256]{1,0:T(8,128)(2,1)}, u32[]{:S(2)}) copy-start(bf16[1024,256]{1,0:T(8,128)(2,1)} %constant.18.clone.lag_ref) | copy-start | bytes 1572868
  3.5 21.8 %copy-start.1 = (s32[64]{0:T(128)S(1)}, s32[64]{0:T(128)}, u32[]{:S(2)}) copy-start(s32[64]{0:T(128)} %assign_ref.1) | copy-start | bytes 772
  3.5 21.8 %copy-start.2 = (s32[16]{0:T(128)S(1)}, s32[16]{0:T(128)}, u32[]{:S(2)}) copy-start(s32[16]{0:T(128)} %target_ref.1) | copy-start | bytes 196
  3.5 7.0 %collective-permute-start = (bf16[8,3200]{1,0:T(8,128)(2,1)}, bf16[8,3200]{1,0:T(8,128)(2,1)S(1)}, u32[]{:S(2)}, u32[]{:S(2)}) collective-permute-start(bf16[8,3200]{1,0:T(8,128)(2,1)} %front.1), channel_id=1, source_target_pairs={{0,8},{1,9},{2,10},{3,11},{4,12},{5,13},{6,14},{7,15},{8,0},{9,1},... | collective-permute-start | bytes 153608 | tf_op jit(solution)/shard_map/ppermute | solution.py:414
  11.3 4.7 %collective-permute-start.1 = (bf16[16,3200]{1,0:T(8,128)(2,1)S(1)}, bf16[16,3200]{1,0:T(8,128)(2,1)S(1)}, u32[]{:S(2)}, u32[]{:S(2)}) collective-permute-start(bf16[16,3200]{1,0:T(8,128)(2,1)S(1)} %pad_maximum_fusion.2), channel_id=1, source_target_pairs={{0,4},{1,5},{2,6},{3,7},{4,0},{5,1},{6,2},{7,3},{8,12},{9,13},{10,... | collective-permute-start | bytes 307208 | tf_op jit(solution)/shard_map/ppermute | solution.py:414
  16.8 5.8 %collective-permute-start.2 = (bf16[32,3200]{1,0:T(8,128)(2,1)S(1)}, bf16[32,3200]{1,0:T(8,128)(2,1)S(1)}, u32[]{:S(2)}, u32[]{:S(2)}) collective-permute-start(bf16[32,3200]{1,0:T(8,128)(2,1)S(1)} %pad_maximum_fusion.1), channel_id=1, source_target_pairs={{0,2},{1,3},{2,0},{3,1},{4,6},{5,7},{6,4},{7,5},{8,10},{9,11},{10,... | collective-permute-start | bytes 614408 | tf_op jit(solution)/shard_map/ppermute | solution.py:414
  23.4 1.8 %collective-permute-start.3 = (bf16[64,3200]{1,0:T(8,128)(2,1)S(1)}, bf16[64,3200]{1,0:T(8,128)(2,1)S(1)}, u32[]{:S(2)}, u32[]{:S(2)}) collective-permute-start(bf16[64,3200]{1,0:T(8,128)(2,1)S(1)} %pad_maximum_fusion), channel_id=1, source_target_pairs={{0,1},{1,0},{2,3},{3,2},{4,5},{5,4},{6,7},{7,6},{8,9},{9,8},{10,11... | collective-permute-start | bytes 1228808 | tf_op jit(solution)/shard_map/ppermute | solution.py:414

commit v2 on v1

v2 whole, which is shorter than its diff:
```python
import functools
import math

import jax
import jax.numpy as jnp
import numpy as np
from jax import lax
from jax.experimental import pallas as pl
from jax.experimental.pallas import tpu as pltpu
from jax.sharding import PartitionSpec as P


SEG = 2048
FREQ = 512
FLO = 64
LAGS = 256
HALF = 21
CAP = 2
COMP = 3
RADIX = 4
LANE = 128
NONE = -1000
PART = SEG // RADIX
PLANE = 2 * COMP * FREQ
WINDOWS = 2
WIDE = WINDOWS * (PLANE + LANE)
GROUP = 4


def bin_order():
    spot = np.arange(FREQ)
    return RADIX * (spot % LANE) + spot // LANE


def dft_table():
    n1 = np.arange(PART)[:, None]
    blocks = []
    for r in (0, 2, 1, 3):
        k = FLO + RADIX * np.arange(LANE)[None, :] + r
        phase = np.mod(n1 * k, SEG) * (2.0 * math.pi / SEG)
        c, s = np.cos(phase), np.sin(phase)
        blocks.append(np.concatenate([c, -s], 1))
        if r == 1:
            blocks.append(np.concatenate([-s, -c], 1))
        if r == 3:
            blocks.append(np.concatenate([s, c], 1) * np.array([1.0]))
    return np.concatenate(blocks, 0).astype(jnp.bfloat16)


def band_table():
    f = bin_order()
    band = np.abs(f[:, None] - f[None, :]) <= HALF
    share = 1.0 / (float(COMP) * band.sum(0, keepdims=True))
    return band.astype(jnp.bfloat16), share.astype(np.float32)


def lag_table():
    bins = FLO + bin_order()[:, None]
    shifts = np.arange(LAGS)[None, :] - LAGS // 2
    phase = np.mod(bins * shifts, SEG) * (2.0 * math.pi / SEG)
    return np.concatenate([np.cos(phase), -np.sin(phase)], 0).astype(jnp.bfloat16)


def mm(a, b):
    return jnp.dot(a, b, preferred_element_type=jnp.float32)


def front_kernel(gaps_ref, x_ref, tab_ref, band_ref, share_ref, out_ref):
    windows, own = gaps_ref.shape
    rows = windows * own
    quarter = []
    for j in range(RADIX):
        per_comp = []
        for a in range(COMP):
            pieces = [
                x_ref[a, :, w * SEG + j * PART : w * SEG + (j + 1) * PART].astype(jnp.float32)
                for w in range(windows)
            ]
            per_comp.append(jnp.concatenate(pieces, 0))
        quarter.append(jnp.concatenate(per_comp, 0))
    x0, x1, x2, x3 = quarter
    even, odd = x0 + x2, x1 + x3

    def halves(y):
        low = y - y.astype(jnp.bfloat16).astype(jnp.float32)
        return jnp.concatenate([y, low], 0).astype(jnp.bfloat16)

    zero, two = halves(even + odd), halves(even - odd)
    u, v = halves(x0 - x2), halves(x1 - x3)
    tab = lambda i: tab_ref[i * PART : (i + 1) * PART, :]
    both = [
        mm(zero, tab(0)),
        mm(u, tab(2)) + mm(v, tab(3)),
        mm(two, tab(1)),
        mm(u, tab(4)) + mm(v, tab(5)),
    ]
    count = COMP * rows
    spec = [d[:count] + d[count:] for d in both]
    power = []
    for d in spec:
        total = jnp.zeros((rows, LANE), jnp.float32)
        for a in range(COMP):
            re = d[a * rows : (a + 1) * rows, :LANE]
            im = d[a * rows : (a + 1) * rows, LANE:]
            total = total + (re * re + im * im)
        power.append(total)
    power = jnp.concatenate(power, 1)
    p1 = power.astype(jnp.bfloat16).astype(jnp.float32)
    rest = power - p1
    p2 = rest.astype(jnp.bfloat16).astype(jnp.float32)
    p3 = rest - p2
    sums = mm(jnp.concatenate([p1, p2, p3], 0).astype(jnp.bfloat16), band_ref[...])
    smooth = (sums[:rows] + sums[rows : 2 * rows] + sums[2 * rows :]) * share_ref[...]
    row_at = lax.broadcasted_iota(jnp.int32, (rows, LANE), 0)
    flags = jnp.zeros((rows, LANE), jnp.float32)
    for w in range(windows):
        for s in range(own):
            flags = jnp.where(row_at == w * own + s, gaps_ref[w, s].astype(jnp.float32), flags)
    wide_flags = jnp.concatenate([flags] * RADIX, 1)
    factor = wide_flags / jnp.sqrt(smooth + 1e-06)
    for a in range(COMP):
        for part in range(2):
            whole = jnp.concatenate(
                [d[a * rows : (a + 1) * rows, part * LANE : (part + 1) * LANE] for d in spec], 1
            )
            white = whole * factor
            for w in range(windows):
                start = w * PLANE + (2 * a + part) * FREQ
                out_ref[:, start : start + FREQ] = white[w * own : (w + 1) * own].astype(jnp.bfloat16)
    for w in range(windows):
        start = windows * PLANE + w * LANE
        out_ref[:, start : start + LANE] = flags[w * own : (w + 1) * own].astype(jnp.bfloat16)


def front(traces, gaps):
    own, comps, length = traces.shape
    windows = gaps.shape[1]
    assert comps == COMP and length == windows * SEG
    band, share = band_table()
    vmem = pl.BlockSpec(memory_space=pltpu.VMEM)
    return pl.pallas_call(
        front_kernel,
        out_shape=jax.ShapeDtypeStruct((own, windows * (PLANE + LANE)), jnp.bfloat16),
        in_specs=[pl.BlockSpec(memory_space=pltpu.SMEM)] + [vmem] * 4,
        out_specs=vmem,
        compiler_params=room(0),
        name="front",
    )(
        gaps.T,
        traces.transpose(1, 0, 2),
        jnp.asarray(dft_table()),
        jnp.asarray(band),
        jnp.asarray(share),
    )


def exchange_plan(count):
    bits = int(count).bit_length() - 1
    assert count == 1 << bits and bits >= 3
    chips = [1 << b for b in range(bits - 1, 0, -1)]
    return [chips, chips[-1:] + chips[:-1]]


def owner_masks(plan):
    own_core = []
    for chips in plan:
        found = [0]
        for m in chips:
            found = found + [f ^ m for f in found]
        own_core.append(found)
    return np.asarray(
        [own_core[p] + [1 ^ f for f in own_core[1 - p]] for p in range(2)], np.int32
    )


def room(operand_bytes):
    return pltpu.CompilerParams(vmem_limit_bytes=(8 << 20) + operand_bytes)


def first_two(flags):
    found = [jnp.int32(NONE)] * CAP
    seen = jnp.int32(0)
    for s, flag in enumerate(flags):
        for c in range(CAP):
            found[c] = jnp.where(jnp.logical_and(flag, seen == c), s, found[c])
        seen = seen + flag.astype(jnp.int32)
    return found


def iota(rows, cols, dim):
    return lax.broadcasted_iota(jnp.int32, (rows, cols), dim)


def one_hot(want, cols):
    return jnp.where(iota(want.shape[0], cols, 1) == want, 1.0, 0.0).astype(jnp.bfloat16)


def own_slots(assign_ref, target_ref, me, own, owner):
    want = target_ref[owner]
    return first_two([assign_ref[me * own + s] == want for s in range(own)])


def spread_kernel(own, assign_ref, target_ref, mask_ref, self_ref, rows_ref, partner_ref):
    me = lax.axis_index("pairs")
    parity = lax.rem(me, 2)
    pairs = GROUP * CAP
    stations = GROUP * own
    mine_rows = self_ref[...]
    rows_ref[...] = mm(one_hot(iota(own * pairs, own, 0) // pairs, own), mine_rows).astype(
        jnp.bfloat16
    )
    place = iota(CAP * stations, own, 0)
    place = (place // stations) * GROUP + (place % stations) // own

    def one_chunk(ch, carry):
        want = jnp.full(place.shape, NONE, jnp.int32)
        for j in range(GROUP):
            owner = me ^ mask_ref[parity, ch * GROUP + j]
            for c, s in enumerate(own_slots(assign_ref, target_ref, me, own, owner)):
                want = jnp.where(place == c * GROUP + j, s, want)
        partner_ref[ch] = mm(one_hot(want, own), mine_rows).astype(jnp.bfloat16)
        return carry

    lax.fori_loop(0, partner_ref.shape[0], one_chunk, 0)


def spread(held, assign, target, masks):
    own = held.shape[0]
    chunks = masks.shape[1] // GROUP
    smem = pl.BlockSpec(memory_space=pltpu.SMEM)
    vmem = pl.BlockSpec(memory_space=pltpu.VMEM)
    made = own * GROUP * CAP + chunks * CAP * GROUP * own
    return pl.pallas_call(
        functools.partial(spread_kernel, own),
        out_shape=(
            jax.ShapeDtypeStruct((own * GROUP * CAP, WIDE), jnp.bfloat16),
            jax.ShapeDtypeStruct((chunks, CAP * GROUP * own, WIDE), jnp.bfloat16),
        ),
        in_specs=[smem] * 3 + [vmem],
        out_specs=(vmem, vmem),
        compiler_params=room(2 * made * WIDE),
        cost_estimate=pl.CostEstimate(
            flops=2 * made * own * WIDE, bytes_accessed=2 * made * WIDE, transcendentals=0
        ),
        name="spread",
    )(assign, target, masks, held)


def correlate_kernel(
    owners, own, windows, base, first, last, assign_ref, target_ref, mask_ref, chunk_ref, rows_ref,
    partner_ref, lag_ref, *rest,
):
    if not first:
        sum_in, rest = rest[0], rest[2:]
    out_ref, sum_ref, picked, cross, result, outv, sem = rest
    me = lax.axis_index("pairs")
    parity = lax.rem(me, 2)
    pairs = GROUP * CAP
    stations = GROUP * own
    nine = COMP * COMP
    half = own * nine * pairs
    chunks = chunk_ref.shape[0] // stations
    my_target = target_ref[me]
    total = jnp.zeros((own, nine * LANE), jnp.float32) if first else sum_in[...]

    def owner_of(ch, j):
        return me ^ mask_ref[parity, base + ch * GROUP + j]

    def copies(ch):
        which = lax.rem(ch, 2)
        return [
            pltpu.make_async_copy(outv.at[which, :, j], out_ref.at[:, owner_of(ch, j)], sem.at[which])
            for j in range(GROUP)
        ]

    def one_chunk(ch, total):
        slot = lax.rem(ch, 2)
        first_row = ch * stations if isinstance(ch, int) else pl.multiple_of(ch * stations, stations)
        here = pl.ds(first_row, stations)
        row = iota(2 * pairs, stations, 0) % pairs
        want = jnp.full(row.shape, NONE, jnp.int32)
        mine = []
        for j in range(GROUP):
            owner = owner_of(ch, j)
            theirs = first_two([assign_ref[owner * own + s] == my_target for s in range(own)])
            for c, s in enumerate(theirs):
                want = jnp.where(row == j * CAP + c, s + j * own, want)
            mine.append(own_slots(assign_ref, target_ref, me, own, owner))
        picked[...] = mm(one_hot(want, stations), chunk_ref[here, :]).astype(jnp.bfloat16)

        def product(left, right):
            re = im = None
            for (lr, li), (rr, ri) in zip(left, right):
                r = lr * rr + li * ri
                i = li * rr - lr * ri
                re = r if re is None else re + r
                im = i if im is None else im + i
            return re, im

        def one_tile(lt, carry):
            re_at = pl.ds(pl.multiple_of(lt * LANE, LANE), LANE)
            im_at = pl.ds(pl.multiple_of(FREQ + lt * LANE, LANE), LANE)

            def tile(load, a):
                got = []
                for w in range(windows):
                    both = []
                    for part in range(2):
                        start = ((w * COMP + a) * 2 + part) * FREQ + lt * LANE
                        both.append(load(pl.ds(pl.multiple_of(start, LANE), LANE)))
                    got.append(both)
                return got

            slots = [tile(lambda d: picked[:, d], b) for b in range(COMP)]
            for yp in range(own // 2):
                for a in range(COMP):
                    left = tile(lambda d: rows_ref[yp * 2 * pairs : (yp + 1) * 2 * pairs, d], a)
                    for b in range(COMP):
                        at = ((yp * COMP + a) * COMP + b) * 2 * pairs
                        re, im = product(left, slots[b])
                        cross[at : at + 2 * pairs, re_at] = re
                        cross[at : at + 2 * pairs, im_at] = im
            lefts = [tile(lambda d: chunk_ref[here, d], a) for a in range(COMP)]
            for c in range(CAP):
                for b in range(COMP):
                    right = tile(
                        lambda d: partner_ref[base // GROUP + ch, c * stations : (c + 1) * stations, d], b
                    )
                    for a in range(COMP):
                        re, im = product(lefts[a], right)
                        at = half + ((c * COMP + a) * COMP + b) * stations
                        cross[at : at + stations, re_at] = re
                        cross[at : at + stations, im_at] = im
            return carry

        lax.fori_loop(0, FREQ // LANE, one_tile, 0)
        result[...] = mm(cross[...], lag_ref[...])

        def flag(ref, rows, w):
            return ref[rows, PLANE * windows + w * LANE : PLANE * windows + (w + 1) * LANE]

        if not isinstance(ch, int):

            @pl.when(ch >= 2)
            def _():
                for cp in copies(ch):
                    cp.wait()

        for yp in range(own // 2):
            count = None
            for w in range(windows):
                left = flag(rows_ref, slice(yp * 2 * pairs, (yp + 1) * 2 * pairs), w)
                term = left.astype(jnp.float32) * flag(picked, slice(None), w).astype(jnp.float32)
                count = term if count is None else count + term
            scale = 1.0 / (jnp.maximum(count, 1.0) * math.sqrt(FREQ))
            scale = jnp.concatenate([scale] * (LAGS // LANE), 1)
            for q in range(nine):
                at = (yp * nine + q) * 2 * pairs
                block = (result[at : at + 2 * pairs, :] * scale).astype(jnp.bfloat16)
                outv[slot, 2 * yp : 2 * yp + 2, :, q, :, :] = block.reshape(2, GROUP, CAP, LAGS)
        for cp in copies(ch):
            cp.start()
        weights, squares = [], []
        col = iota(own, stations, 1) // own
        y_row = iota(own, stations, 0)
        for c in range(CAP):
            weight = jnp.zeros((own, stations), jnp.float32)
            for j in range(GROUP):
                hit = jnp.logical_and(col == j, y_row == mine[j][c])
                weight = jnp.where(hit, 1.0, weight)
            weights.append(weight)
            count = None
            for w in range(windows):
                left = flag(chunk_ref, here, w).astype(jnp.float32)
                part_rows = slice(c * stations, (c + 1) * stations)
                lanes = slice(PLANE * windows + w * LANE, PLANE * windows + (w + 1) * LANE)
                right = partner_ref[base // GROUP + ch, part_rows, lanes].astype(jnp.float32)
                term = left * right
                count = term if count is None else count + term
            most = jnp.maximum(count, 1.0)
            share = 1.0 / (most * most * float(FREQ))
            tiles = []
            for q in range(nine):
                at = half + (c * nine + q) * stations
                block = result[at : at + stations, :]
                square = block * block
                both = square[:, :LANE]
                for lt in range(1, LAGS // LANE):
                    both = both + square[:, lt * LANE : (lt + 1) * LANE]
                tiles.append(both * share)
            squares.append(jnp.concatenate(tiles, 1))
        weights = jnp.concatenate(weights, 1).astype(jnp.bfloat16)
        return total + mm(weights, jnp.concatenate(squares, 0).astype(jnp.bfloat16))

    if chunks == 1:
        total = one_chunk(0, total)
    else:
        total = lax.fori_loop(0, chunks, one_chunk, total)
    if last:
        lane = iota(own, nine, 1)
        energy = jnp.zeros((own, nine), jnp.float32)
        for q in range(nine):
            part = jnp.sum(total[:, q * LANE : (q + 1) * LANE], axis=1, keepdims=True)
            energy = jnp.where(lane == q, part, energy)
        sum_ref[...] = energy / float(owners * LAGS)
    else:
        sum_ref[...] = total
    for ch in range(max(chunks - 2, 0), chunks):
        for cp in copies(ch):
            cp.wait()


def correlate(chunk, base, spreads, carried, last, assign, target, masks, lags):
    rows, partners = spreads
    owners = target.shape[0]
    own = assign.shape[0] // owners
    windows = (rows.shape[1] - 0) // (PLANE + LANE)
    nine = COMP * COMP
    stations, pairs = GROUP * own, GROUP * CAP
    lines = own * nine * pairs + CAP * nine * stations
    smem = pl.BlockSpec(memory_space=pltpu.SMEM)
    vmem = pl.BlockSpec(memory_space=pltpu.VMEM)
    anywhere = pl.BlockSpec(memory_space=pl.ANY)
    f32, bf16 = jnp.float32, jnp.bfloat16
    first = carried is None
    operands = [assign, target, masks, chunk, rows, partners, lags]
    specs = [smem] * 3 + [vmem] * 4
    aliases = {}
    if not first:
        out_so_far, sums = carried
        operands += [sums, out_so_far]
        specs += [vmem, anywhere]
        aliases = {len(operands) - 1: 0}
    sum_shape = (own, nine) if last else (own, nine * LANE)
    chunks = chunk.shape[0] // stations
    return pl.pallas_call(
        functools.partial(correlate_kernel, owners, own, windows, base, first, last),
        out_shape=(
            jax.ShapeDtypeStruct((own, owners, nine, CAP, LAGS), bf16),
            jax.ShapeDtypeStruct(sum_shape, f32),
        ),
        in_specs=specs,
        out_specs=(anywhere, vmem),
        input_output_aliases=aliases,
        scratch_shapes=[
            pltpu.VMEM((2 * pairs, WIDE), bf16),
            pltpu.VMEM((lines, 2 * FREQ), bf16),
            pltpu.VMEM((lines, LAGS), f32),
            pltpu.VMEM((2, own, GROUP, nine, CAP, LAGS), bf16),
            pltpu.SemaphoreType.DMA((2,)),
        ],
        compiler_params=room(2 * (chunk.size + rows.size + partners.size)),
        cost_estimate=pl.CostEstimate(
            flops=chunks * 4 * lines * FREQ * LAGS,
            bytes_accessed=chunks * 2 * lines * LAGS,
            transcendentals=0,
        ),
        name="correlate",
    )(*operands)


def steps_of(traces, gaps, assign, target):
    owners = lax.axis_size("pairs")
    plan = exchange_plan(owners)
    masks = jnp.asarray(owner_masks(plan))
    lags = jnp.asarray(lag_table())

    def swap(block, masks_of):
        return lax.ppermute(block, "pairs", [(i, i ^ masks_of[i % 2]) for i in range(owners)])

    steps = [tuple(m) for m in zip(*plan)]
    held = front(traces, gaps)
    spreads = spread(held, assign, target, masks)
    for step in steps[:2]:
        got = swap(held, step)
        held = jnp.concatenate([held, got], 0)
    blocks = [held]
    for step in steps[2:]:
        sent = jnp.concatenate(blocks, 0) if len(blocks) > 1 else held
        blocks.append(swap(sent, step))
    other = []
    for block in blocks:
        other.append(swap(block, (1, 1)))
    base = 0
    order = []
    for block in blocks + other:
        order.append((block, base))
        base += block.shape[0] // traces.shape[0]
    count = len(blocks)
    ranked = [order[i + side * count] for i in range(count) for side in range(2)]
    carried = None
    for at, (block, start) in enumerate(ranked):
        last = at == len(ranked) - 1
        carried = correlate(block, start, spreads, carried, last, assign, target, masks, lags)
    out, energy = carried
    return out.transpose(0, 1, 3, 2, 4), energy


def solution(mesh):
    in_specs = (
        P(("groups", "pairs"), None, None),
        P(("groups", "pairs"), None),
        P("groups"),
        P("groups"),
    )
    out_specs = (P(("groups", "pairs"), None, None, None, None), P(("groups", "pairs"), None))
    return jax.shard_map(
        steps_of, mesh=mesh, in_specs=in_specs, out_specs=out_specs, check_vma=False
    )
```

time: 34.5 us -> 37 us (1.072)
  local copies, waits for them, and re-layouts: 0.94 us -> 4.77 us
  Pallas kernels: 11.6 us -> 14.3 us
  other arithmetic: 2.48 us -> 0.14 us
  waiting for transfers between devices: 11 us -> 8.76 us
  starting transfers between devices: 7.35 us -> 8.02 us
    unnamed x12 -> x18, local copies, waits for them, and re-layouts: 0.91 us -> 4.77 us
    pallas_call x2 -> x6, Pallas kernels: 11.6 us -> 14.3 us  [the longest x4 11.2 us: correlate(): pl.pallas_call(functools.partial(correlate_kernel, owners, own, windows,...]
    concatenate x3 -> x2, other arithmetic: 2.48 us -> 0.14 us  [steps_of(): held = jnp.concatenate([held, got], 0)]
    ppermute x4 -> x5, waiting for transfers between devices: 11 us -> 8.76 us  [swap(): lax.ppermute(block, 'pairs', [(i, i ^ masks_of[i % 2]) for i in range(own...]
    ppermute x4 -> x5, starting transfers between devices: 7.35 us -> 8.02 us  [swap(): lax.ppermute(block, 'pairs', [(i, i ^ masks_of[i % 2]) for i in range(own...]
  transfers between devices with their start and end apart: 4 -> 5, of which waited for: 4 -> 3; matrix products, arithmetic and copies ran while one was open for 3% -> 0% of each run, Pallas kernels for 0% -> 27%
where the time goes in v2:
time: 37 us; the launch traced here: 36.7 us
  Pallas kernels  14.3 us (39%)
  waiting for transfers between devices  8.76 us (24%)
  starting transfers between devices  8.02 us (22%)
  local copies, waits for them, and re-layouts  4.77 us (13%)
  between operations  0.75 us (2%)
    pallas_call x4, Pallas kernels, correlate(): pl.pallas_call(functools.partial(correlate_kernel, owners, own, windows,...  11.2 us
    ppermute x5, waiting for transfers between devices, swap(): lax.ppermute(block, 'pairs', [(i, i ^ masks_of[i % 2]) for i in range(own...  8.76 us
    ppermute x5, starting transfers between devices, swap(): lax.ppermute(block, 'pairs', [(i, i ^ masks_of[i % 2]) for i in range(own...  8.02 us
    unnamed x18, local copies, waits for them, and re-layouts  4.77 us
    pallas_call x1, Pallas kernels, spread(): pl.pallas_call(functools.partial(spread_kernel, own), out_shape=(jax.Shap...  1.94 us
    pallas_call x1, Pallas kernels, front(): pl.pallas_call(front_kernel, out_shape=jax.ShapeDtypeStruct((own, windows...  1.19 us
  transfers between devices with their start and end apart: 5, of which 3 were waited for; matrix products, arithmetic and copies ran while one was open for 0% of the time, Pallas kernels for 27%

profile of v2, /device:TPU:0, one launch (start us, length us, event | category | flops | bytes accessed | tf_op | source)
XLA Modules:
  0.0 36.7 jit_solution(16005288281085191326)
XLA Ops:
  0.6 0.0 copy-start.4
  0.6 0.0 copy-start
  0.7 0.0 copy-start.1
  0.7 1.5 %copy-done.1 = bf16[3072,256]{1,0:T(8,128)(2,1)S(1)} copy-done((bf16[3072,256]{1,0:T(8,128)(2,1)S(1)}, bf16[3072,256]{1,0:T(8,128)(2,1)}, u32[]{:S(2)}) %copy-start.1) | copy-done | bytes 1572888
  2.1 0.0 copy-start.2
  2.1 1.0 %copy-done.2 = bf16[512,512]{1,0:T(8,128)(2,1)S(1)} copy-done((bf16[512,512]{1,0:T(8,128)(2,1)S(1)}, bf16[512,512]{1,0:T(8,128)(2,1)}, u32[]{:S(2)}) %copy-start.2) | copy-done | bytes 524312
  3.2 0.0 copy-start.3
  3.2 0.9 %copy-done.3 = bf16[4,3,4096]{2,0,1:T(4,128)(2,1)S(1)} copy-done((bf16[4,3,4096]{2,0,1:T(4,128)(2,1)S(1)}, bf16[4,3,4096]{2,0,1:T(4,128)(2,1)}, u32[]{:S(2)}) %copy-start.3) | copy-done | bytes 98328
  4.1 0.0 copy-start.7
  4.1 0.7 %copy-done.7 = f32[1,512]{1,0:T(1,128)S(1)} copy-done((f32[1,512]{1,0:T(1,128)S(1)}, f32[1,512]{1,0:T(1,128)}, u32[]{:S(2)}) %copy-start.7) | copy-done | bytes 2072
  4.7 0.0 copy-start.8
  4.7 0.7 %copy-done.8 = s32[4,2]{0,1:T(2,128)S(1)} copy-done((s32[4,2]{0,1:T(2,128)S(1)}, s32[4,2]{0,1:T(2,128)}, u32[]{:S(2)}) %copy-start.8) | copy-done | bytes 56
  5.4 0.0 copy-start.5
  5.4 0.0 copy-start.6
  5.4 1.2 %front.1.self_ref = bf16[4,6400]{1,0:T(4,128)(2,1)S(1)} custom-call(s32[2,4]{1,0:T(2,128)S(1)} %bitcast.4, bf16[3,4,4096]{2,1,0:T(4,128)(2,1)S(1)} %bitcast.3, bf16[3072,256]{1,0:T(8,128)(2,1)S(1)} %copy-done.1, bf16[512,512]{1,0:T(8,128)(2,1)S(1)} %copy-done.2, f32[1,512]{1,0:T(1,128)S(1)} %copy-done.7), custom_call_target="tpu_custom_call" | custom-call | tf_op jit(solution)/shard_map/front/pallas_call | solution.py:141
  6.6 4.1 %collective-permute-start = (bf16[4,6400]{1,0:T(4,128)(2,1)S(1)}, bf16[4,6400]{1,0:T(4,128)(2,1)S(1)}, u32[]{:S(2)}, u32[]{:S(2)}) collective-permute-start(bf16[4,6400]{1,0:T(4,128)(2,1)S(1)} %front.1.self_ref), channel_id=1, source_target_pairs={{0,8},{1,3},{2,10},{3,1},{4,12},{5,7},{6,14},{7,5},{8,0},{9,11},{1... | collective-permute-start | bytes 153608 | tf_op jit(solution)/shard_map/ppermute | solution.py:469
  10.8 2.1 %collective-permute-done = bf16[4,6400]{1,0:T(4,128)(2,1)S(1)} collective-permute-done((bf16[4,6400]{1,0:T(4,128)(2,1)S(1)}, bf16[4,6400]{1,0:T(4,128)(2,1)S(1)}, u32[]{:S(2)}, u32[]{:S(2)}) %collective-permute-start) | collective-permute-done | bytes 51232 | tf_op jit(solution)/shard_map/ppermute | solution.py:469
  12.8 0.1 pad_maximum_fusion.1
  12.9 2.0 %collective-permute-start.1 = (bf16[8,6400]{1,0:T(8,128)(2,1)S(1)}, bf16[8,6400]{1,0:T(8,128)(2,1)S(1)}, u32[]{:S(2)}, u32[]{:S(2)}) collective-permute-start(bf16[8,6400]{1,0:T(8,128)(2,1)S(1)} %pad_maximum_fusion.1), channel_id=1, source_target_pairs={{0,4},{1,9},{2,6},{3,11},{4,0},{5,13},{6,2},{7,15},{8,12},{9,1},{1... | collective-permute-start | bytes 307208 | tf_op jit(solution)/shard_map/ppermute | solution.py:469
  14.9 2.8 %collective-permute-done.1 = bf16[8,6400]{1,0:T(8,128)(2,1)S(1)} collective-permute-done((bf16[8,6400]{1,0:T(8,128)(2,1)S(1)}, bf16[8,6400]{1,0:T(8,128)(2,1)S(1)}, u32[]{:S(2)}, u32[]{:S(2)}) %collective-permute-start.1) | collective-permute-done | bytes 102432 | tf_op jit(solution)/shard_map/ppermute | solution.py:469
  17.6 0.1 pad_maximum_fusion.chunk_ref
  17.7 1.9 %collective-permute-start.2 = (bf16[16,6400]{1,0:T(8,128)(2,1)S(1)}, bf16[16,6400]{1,0:T(8,128)(2,1)S(1)}, u32[]{:S(2)}, u32[]{:S(2)}) collective-permute-start(bf16[16,6400]{1,0:T(8,128)(2,1)S(1)} %pad_maximum_fusion.chunk_ref), channel_id=1, source_target_pairs={{0,2},{1,5},{2,0},{3,7},{4,6},{5,1},{6,4},{7,3},{8,10},{9,13},{10,... | collective-permute-start | bytes 614408 | tf_op jit(solution)/shard_map/ppermute | solution.py:469
  19.6 0.0 collective-permute-start.4
  19.6 3.9 %collective-permute-done.2.chunk_ref = bf16[16,6400]{1,0:T(8,128)(2,1)S(1)} collective-permute-done((bf16[16,6400]{1,0:T(8,128)(2,1)S(1)}, bf16[16,6400]{1,0:T(8,128)(2,1)S(1)}, u32[]{:S(2)}, u32[]{:S(2)}) %collective-permute-start.2) | collective-permute-done | bytes 204832 | tf_op jit(solution)/shard_map/ppermute | solution.py:469
  23.5 0.0 collective-permute-start.3
  23.5 0.0 copy-done.4
  23.6 0.0 copy-done.5
  23.6 0.0 copy-done.6
  23.6 1.9 %spread.1 = (bf16[32,6400]{1,0:T(8,128)(2,1)S(1)}, bf16[4,32,6400]{2,1,0:T(8,128)(2,1)S(1)}) custom-call(s32[64]{0:T(128)S(1)} %copy-done.5, s32[16]{0:T(128)S(1)} %copy-done.6, s32[2,16]{1,0:T(2,128)S(1)} %copy-done.4, bf16[4,6400]{1,0:T(4,128)(2,1)S(1)} %front.1.self_ref), custom_call_target="tpu_custom_call" | custom-call | flops 8192000 | bytes 2048000 | tf_op jit(solution)/shard_map/spread/pallas_call | solution.py:233
  25.5 0.0 copy-done
  25.5 2.6 %correlate.4 = (bf16[4,16,9,2,256]{4,3,2,1,0:T(2,128)(2,1)}, f32[4,1152]{1,0:T(4,128)S(1)}) custom-call(s32[64]{0:T(128)S(1)} %copy-done.5, s32[16]{0:T(128)S(1)} %copy-done.6, s32[2,16]{1,0:T(2,128)S(1)} %copy-done.4, bf16[16,6400]{1,0:T(8,128)(2,1)S(1)} %pad_maximum_fusion.chunk_ref, bf16[32,6400]{1,0:T(8,128)(2,1)S(1)} %get-tuple-element.12.rows_ref, ...), custom_call_target="tpu_custom_call" | custom-call | flops 301989888 | bytes 294912 | tf_op jit(solution)/shard_map/correlate/pallas_call | solution.py:436
  28.2 0.0 collective-permute-done.4.chunk_ref
  28.2 2.6 %correlate.5 = (bf16[4,16,9,2,256]{4,3,2,1,0:T(2,128)(2,1)}, f32[4,1152]{1,0:T(4,128)S(1)}) custom-call(s32[64]{0:T(128)S(1)} %copy-done.5, s32[16]{0:T(128)S(1)} %copy-done.6, s32[2,16]{1,0:T(2,128)S(1)} %copy-done.4, bf16[16,6400]{1,0:T(8,128)(2,1)S(1)} %collective-permute-done.4.chunk_ref, ...), custom_call_target="tpu_custom_call", output_to_operand_aliasing={{0}: (8, {})} | custom-call | flops 301989888 | bytes 294912 | tf_op jit(solution)/shard_map/correlate/pallas_call | solution.py:436
  30.8 2.6 %correlate.6 = (bf16[4,16,9,2,256]{4,3,2,1,0:T(2,128)(2,1)}, f32[4,1152]{1,0:T(4,128)S(1)}) custom-call(s32[64]{0:T(128)S(1)} %copy-done.5, s32[16]{0:T(128)S(1)} %copy-done.6, s32[2,16]{1,0:T(2,128)S(1)} %copy-done.4, bf16[16,6400]{1,0:T(8,128)(2,1)S(1)} %collective-permute-done.2.chunk_ref, ...), custom_call_target="tpu_custom_call", output_to_operand_aliasing={{0}: (8, {})} | custom-call | flops 301989888 | bytes 294912 | tf_op jit(solution)/shard_map/correlate/pallas_call | solution.py:436
  33.5 0.0 collective-permute-done.3.chunk_ref
  33.5 3.2 %correlate.7 = (bf16[4,16,9,2,256]{4,3,2,1,0:T(2,128)(2,1)}, f32[4,9]{1,0:T(4,128)}) custom-call(s32[64]{0:T(128)S(1)} %copy-done.5, s32[16]{0:T(128)S(1)} %copy-done.6, s32[2,16]{1,0:T(2,128)S(1)} %copy-done.4, bf16[16,6400]{1,0:T(8,128)(2,1)S(1)} %collective-permute-done.3.chunk_ref, ...), custom_call_target="tpu_custom_call", output_to_operand_aliasing={{0}: (8, {})} | custom-call | flops 301989888 | bytes 294912 | tf_op jit(solution)/shard_map/correlate/pallas_call | solution.py:436
Async XLA Ops:
  0.6 22.9 %copy-start.4 = (s32[2,16]{1,0:T(2,128)S(1)}, s32[2,16]{1,0:T(2,128)}, u32[]{:S(2)}) copy-start(s32[2,16]{1,0:T(2,128)} %constant.10.clone.mask_ref) | copy-start | bytes 388
  0.6 24.9 %copy-start = (bf16[1024,256]{1,0:T(8,128)(2,1)S(1)}, bf16[1024,256]{1,0:T(8,128)(2,1)}, u32[]{:S(2)}) copy-start(bf16[1024,256]{1,0:T(8,128)(2,1)} %constant.11.clone.lag_ref) | copy-start | bytes 1572868
  0.7 1.5 %copy-start.1 = (bf16[3072,256]{1,0:T(8,128)(2,1)S(1)}, bf16[3072,256]{1,0:T(8,128)(2,1)}, u32[]{:S(2)}) copy-start(bf16[3072,256]{1,0:T(8,128)(2,1)} %constant.12.clone.tab_ref) | copy-start | bytes 4718596
  2.1 1.0 %copy-start.2 = (bf16[512,512]{1,0:T(8,128)(2,1)S(1)}, bf16[512,512]{1,0:T(8,128)(2,1)}, u32[]{:S(2)}) copy-start(bf16[512,512]{1,0:T(8,128)(2,1)} %constant.13.clone.band_ref) | copy-start | bytes 1572868
  3.2 0.9 %copy-start.3 = (bf16[4,3,4096]{2,0,1:T(4,128)(2,1)S(1)}, bf16[4,3,4096]{2,0,1:T(4,128)(2,1)}, u32[]{:S(2)}) copy-start(bf16[4,3,4096]{2,0,1:T(4,128)(2,1)} %param.9) | copy-start | bytes 294916
  4.1 0.7 %copy-start.7 = (f32[1,512]{1,0:T(1,128)S(1)}, f32[1,512]{1,0:T(1,128)}, u32[]{:S(2)}) copy-start(f32[1,512]{1,0:T(1,128)} %constant.14.clone.share_ref) | copy-start | bytes 6148
  4.7 0.7 %copy-start.8 = (s32[4,2]{0,1:T(2,128)S(1)}, s32[4,2]{0,1:T(2,128)}, u32[]{:S(2)}) copy-start(s32[4,2]{0,1:T(2,128)} %param.10) | copy-start | bytes 100
  5.4 18.1 %copy-start.5 = (s32[64]{0:T(128)S(1)}, s32[64]{0:T(128)}, u32[]{:S(2)}) copy-start(s32[64]{0:T(128)} %assign_ref.9) | copy-start | bytes 772
  5.4 18.1 %copy-start.6 = (s32[16]{0:T(128)S(1)}, s32[16]{0:T(128)}, u32[]{:S(2)}) copy-start(s32[16]{0:T(128)} %target_ref.9) | copy-start | bytes 196
  6.6 6.2 %collective-permute-start = (bf16[4,6400]{1,0:T(4,128)(2,1)S(1)}, bf16[4,6400]{1,0:T(4,128)(2,1)S(1)}, u32[]{:S(2)}, u32[]{:S(2)}) collective-permute-start(bf16[4,6400]{1,0:T(4,128)(2,1)S(1)} %front.1.self_ref), channel_id=1, source_target_pairs={{0,8},{1,3},{2,10},{3,1},{4,12},{5,7},{6,14},{7,5},{8,0},{9,11},{1... | collective-permute-start | bytes 153608 | tf_op jit(solution)/shard_map/ppermute | solution.py:469
  12.9 4.7 %collective-permute-start.1 = (bf16[8,6400]{1,0:T(8,128)(2,1)S(1)}, bf16[8,6400]{1,0:T(8,128)(2,1)S(1)}, u32[]{:S(2)}, u32[]{:S(2)}) collective-permute-start(bf16[8,6400]{1,0:T(8,128)(2,1)S(1)} %pad_maximum_fusion.1), channel_id=1, source_target_pairs={{0,4},{1,9},{2,6},{3,11},{4,0},{5,13},{6,2},{7,15},{8,12},{9,1},{1... | collective-permute-start | bytes 307208 | tf_op jit(solution)/shard_map/ppermute | solution.py:469
  17.7 5.8 %collective-permute-start.2 = (bf16[16,6400]{1,0:T(8,128)(2,1)S(1)}, bf16[16,6400]{1,0:T(8,128)(2,1)S(1)}, u32[]{:S(2)}, u32[]{:S(2)}) collective-permute-start(bf16[16,6400]{1,0:T(8,128)(2,1)S(1)} %pad_maximum_fusion.chunk_ref), channel_id=1, source_target_pairs={{0,2},{1,5},{2,0},{3,7},{4,6},{5,1},{6,4},{7,3},{8,10},{9,13},{10,... | collective-permute-start | bytes 614408 | tf_op jit(solution)/shard_map/ppermute | solution.py:469
  19.6 8.5 %collective-permute-start.4 = (bf16[16,6400]{1,0:T(8,128)(2,1)S(1)}, bf16[16,6400]{1,0:T(8,128)(2,1)S(1)}, u32[]{:S(2)}, u32[]{:S(2)}) collective-permute-start(bf16[16,6400]{1,0:T(8,128)(2,1)S(1)} %pad_maximum_fusion.chunk_ref), channel_id=1, source_target_pairs={{0,1},{1,0},{2,3},{3,2},{4,5},{5,4},{6,7},{7,6},{8,9},{9,8},{10,11... | collective-permute-start | bytes 614408 | tf_op jit(solution)/shard_map/ppermute | solution.py:469
  23.5 9.9 %collective-permute-start.3 = (bf16[16,6400]{1,0:T(8,128)(2,1)S(1)}, bf16[16,6400]{1,0:T(8,128)(2,1)S(1)}, u32[]{:S(2)}, u32[]{:S(2)}) collective-permute-start(bf16[16,6400]{1,0:T(8,128)(2,1)S(1)} %collective-permute-done.2.chunk_ref), channel_id=1, source_target_pairs={{0,1},{1,0},{2,3},{3,2},{4,5},{5,4},{6,7},{7,6},{8,9},{9,8},{10,11... | collective-permute-start | bytes 614408 | tf_op jit(solution)/shard_map/ppermute | solution.py:469

commit v3 on v2

--- a/solution.py
+++ b/solution.py
@@ -19,6 +19,7 @@
 COMP = 3
 RADIX = 4
 LANE = 128
+TILE = 2 * LANE
 NONE = -1000
 PART = SEG // RADIX
 PLANE = 2 * COMP * FREQ
@@ -49,9 +50,7 @@
 
 def band_table():
     f = bin_order()
-    band = np.abs(f[:, None] - f[None, :]) <= HALF
-    share = 1.0 / (float(COMP) * band.sum(0, keepdims=True))
-    return band.astype(jnp.bfloat16), share.astype(np.float32)
+    return (np.abs(f[:, None] - f[None, :]) <= HALF).astype(jnp.bfloat16)
 
 
 def lag_table():
@@ -65,9 +64,26 @@
     return jnp.dot(a, b, preferred_element_type=jnp.float32)
 
 
-def front_kernel(gaps_ref, x_ref, tab_ref, band_ref, share_ref, out_ref):
+def front_kernel(gaps_hbm, x_hbm, tab_hbm, band_hbm, out_ref, gaps_ref, x_ref, tab_ref, band_ref, sem):
     windows, own = gaps_ref.shape
     rows = windows * own
+    parts = tab_ref.shape[0] // PART
+
+    def part_at(i):
+        return pl.ds(i * PART, PART)
+
+    loads = [
+        pltpu.make_async_copy(x_hbm, x_ref, sem.at[0]),
+        *[
+            pltpu.make_async_copy(tab_hbm.at[part_at(i)], tab_ref.at[part_at(i)], sem.at[1 + i])
+            for i in range(parts)
+        ],
+        pltpu.make_async_copy(band_hbm, band_ref, sem.at[1 + parts]),
+        pltpu.make_async_copy(gaps_hbm, gaps_ref, sem.at[2 + parts]),
+    ]
+    for load in loads:
+        load.start()
+    loads[0].wait()
     quarter = []
     for j in range(RADIX):
         per_comp = []
@@ -87,13 +103,16 @@
 
     zero, two = halves(even + odd), halves(even - odd)
     u, v = halves(x0 - x2), halves(x1 - x3)
-    tab = lambda i: tab_ref[i * PART : (i + 1) * PART, :]
-    both = [
-        mm(zero, tab(0)),
-        mm(u, tab(2)) + mm(v, tab(3)),
-        mm(two, tab(1)),
-        mm(u, tab(4)) + mm(v, tab(5)),
-    ]
+
+    def tab(i):
+        loads[1 + i].wait()
+        return tab_ref[part_at(i), :]
+
+    both0 = mm(zero, tab(0))
+    both2 = mm(two, tab(1))
+    both1 = mm(u, tab(2)) + mm(v, tab(3))
+    both3 = mm(u, tab(4)) + mm(v, tab(5))
+    both = [both0, both1, both2, both3]
     count = COMP * rows
     spec = [d[:count] + d[count:] for d in both]
     power = []
@@ -109,8 +128,14 @@
     rest = power - p1
     p2 = rest.astype(jnp.bfloat16).astype(jnp.float32)
     p3 = rest - p2
+    loads[1 + parts].wait()
     sums = mm(jnp.concatenate([p1, p2, p3], 0).astype(jnp.bfloat16), band_ref[...])
-    smooth = (sums[:rows] + sums[rows : 2 * rows] + sums[2 * rows :]) * share_ref[...]
+    spot = iota(rows, FREQ, 1)
+    f = RADIX * (spot % LANE) + spot // LANE
+    taken = jnp.minimum(f + HALF, FREQ - 1) - jnp.maximum(f - HALF, 0) + 1
+    share = 1.0 / (taken.astype(jnp.float32) * float(COMP))
+    smooth = (sums[:rows] + sums[rows : 2 * rows] + sums[2 * rows :]) * share
+    loads[2 + parts].wait()
     row_at = lax.broadcasted_iota(jnp.int32, (rows, LANE), 0)
     flags = jnp.zeros((rows, LANE), jnp.float32)
     for w in range(windows):
@@ -136,22 +161,25 @@
     own, comps, length = traces.shape
     windows = gaps.shape[1]
     assert comps == COMP and length == windows * SEG
-    band, share = band_table()
-    vmem = pl.BlockSpec(memory_space=pltpu.VMEM)
+    table, band = dft_table(), band_table()
+    operands = (gaps.T, traces.transpose(1, 0, 2), jnp.asarray(table), jnp.asarray(band))
+    hbm = pl.BlockSpec(memory_space=pltpu.HBM)
+    bf16 = jnp.bfloat16
     return pl.pallas_call(
         front_kernel,
-        out_shape=jax.ShapeDtypeStruct((own, windows * (PLANE + LANE)), jnp.bfloat16),
-        in_specs=[pl.BlockSpec(memory_space=pltpu.SMEM)] + [vmem] * 4,
-        out_specs=vmem,
+        out_shape=jax.ShapeDtypeStruct((own, windows * (PLANE + LANE)), bf16),
+        in_specs=[hbm] * 4,
+        out_specs=pl.BlockSpec(memory_space=pltpu.VMEM),
+        scratch_shapes=[
+            pltpu.SMEM((windows, own), jnp.int32),
+            pltpu.VMEM((comps, own, length), bf16),
+            pltpu.VMEM(table.shape, bf16),
+            pltpu.VMEM(band.shape, bf16),
+            pltpu.SemaphoreType.DMA((3 + table.shape[0] // PART,)),
+        ],
         compiler_params=room(0),
         name="front",
-    )(
-        gaps.T,
-        traces.transpose(1, 0, 2),
-        jnp.asarray(dft_table()),
-        jnp.asarray(band),
-        jnp.asarray(share),
-    )
+    )(*[pltpu.with_memory_space_constraint(v, pltpu.HBM) for v in operands])
 
 
 def exchange_plan(count):
@@ -298,16 +326,16 @@
             return re, im
 
         def one_tile(lt, carry):
-            re_at = pl.ds(pl.multiple_of(lt * LANE, LANE), LANE)
-            im_at = pl.ds(pl.multiple_of(FREQ + lt * LANE, LANE), LANE)
+            re_at = pl.ds(pl.multiple_of(lt * TILE, TILE), TILE)
+            im_at = pl.ds(pl.multiple_of(FREQ + lt * TILE, TILE), TILE)
 
             def tile(load, a):
                 got = []
                 for w in range(windows):
                     both = []
                     for part in range(2):
-                        start = ((w * COMP + a) * 2 + part) * FREQ + lt * LANE
-                        both.append(load(pl.ds(pl.multiple_of(start, LANE), LANE)))
+                        start = ((w * COMP + a) * 2 + part) * FREQ + lt * TILE
+                        both.append(load(pl.ds(pl.multiple_of(start, TILE), TILE)))
                     got.append(both)
                 return got
 
@@ -333,7 +361,7 @@
                         cross[at : at + stations, im_at] = im
             return carry
 
-        lax.fori_loop(0, FREQ // LANE, one_tile, 0)
+        lax.fori_loop(0, FREQ // TILE, one_tile, 0)
         result[...] = mm(cross[...], lag_ref[...])
 
         def flag(ref, rows, w):

time: 37 us -> 31.8 us (0.86)
  local copies, waits for them, and re-layouts: 4.77 us -> 0.02 us
    unnamed x18 -> x8, local copies, waits for them, and re-layouts: 4.77 us -> 0.02 us
    pallas_call x4, Pallas kernels: 11.2 us -> 9.74 us  [correlate(): pl.pallas_call(functools.partial(correlate_kernel, owners, own, windows,...]
    pallas_call x1, Pallas kernels: 1.19 us -> 2.32 us  [front(): pl.pallas_call(front_kernel, out_shape=jax.ShapeDtypeStruct((own, windows...]
  transfers between devices with their start and end apart: 5 -> 5, of which waited for: 3 -> 3; matrix products, arithmetic and copies ran while one was open for 0% -> 0% of each run, Pallas kernels for 27% -> 28%
where the time goes in v3:
time: 31.8 us; the launch traced here: 31.7 us
  Pallas kernels  14 us (44%)
  waiting for transfers between devices  8.76 us (28%)
  starting transfers between devices  8.02 us (25%)
  between operations  0.75 us (2%)
    pallas_call x4, Pallas kernels, correlate(): pl.pallas_call(functools.partial(correlate_kernel, owners, own, windows,...  9.74 us
    ppermute x5, waiting for transfers between devices, swap(): lax.ppermute(block, 'pairs', [(i, i ^ masks_of[i % 2]) for i in range(own...  8.76 us
    ppermute x5, starting transfers between devices, swap(): lax.ppermute(block, 'pairs', [(i, i ^ masks_of[i % 2]) for i in range(own...  8.02 us
    pallas_call x1, Pallas kernels, front(): pl.pallas_call(front_kernel, out_shape=jax.ShapeDtypeStruct((own, windows...  2.32 us
    pallas_call x1, Pallas kernels, spread(): pl.pallas_call(functools.partial(spread_kernel, own), out_shape=(jax.Shap...  1.94 us
  transfers between devices with their start and end apart: 5, of which 3 were waited for; matrix products, arithmetic and copies ran while one was open for 0% of the time, Pallas kernels for 28%

profile of v3, /device:TPU:0, one launch (start us, length us, event | category | flops | bytes accessed | tf_op | source)
XLA Modules:
  0.0 31.7 jit_solution(11656224189438436637)
XLA Ops:
  0.6 0.0 copy-start.1
  0.6 0.0 copy-start
  0.7 0.0 copy-start.2
  0.7 0.0 copy-start.3
  0.7 2.3 %front.1.self_ref = bf16[4,6400]{1,0:T(4,128)(2,1)S(1)} custom-call(s32[2,4]{1,0:T(2,128)} %bitcast.5, bf16[3,4,4096]{2,1,0:T(4,128)(2,1)} %bitcast.4, bf16[3072,256]{1,0:T(8,128)(2,1)} %constant.10.clone.tab_hbm, bf16[512,512]{1,0:T(8,128)(2,1)} %constant.11.clone.band_hbm), custom_call_target="tpu_custom_call" | custom-call | tf_op jit(solution)/shard_map/front/pallas_call | solution.py:168
  3.0 4.1 %collective-permute-start = (bf16[4,6400]{1,0:T(4,128)(2,1)S(1)}, bf16[4,6400]{1,0:T(4,128)(2,1)S(1)}, u32[]{:S(2)}, u32[]{:S(2)}) collective-permute-start(bf16[4,6400]{1,0:T(4,128)(2,1)S(1)} %front.1.self_ref), channel_id=1, source_target_pairs={{0,8},{1,3},{2,10},{3,1},{4,12},{5,7},{6,14},{7,5},{8,0},{9,11},{1... | collective-permute-start | bytes 153608 | tf_op jit(solution)/shard_map/ppermute | solution.py:497
  7.1 2.1 %collective-permute-done = bf16[4,6400]{1,0:T(4,128)(2,1)S(1)} collective-permute-done((bf16[4,6400]{1,0:T(4,128)(2,1)S(1)}, bf16[4,6400]{1,0:T(4,128)(2,1)S(1)}, u32[]{:S(2)}, u32[]{:S(2)}) %collective-permute-start) | collective-permute-done | bytes 51232 | tf_op jit(solution)/shard_map/ppermute | solution.py:497
  9.2 0.1 pad_maximum_fusion.1
  9.3 2.0 %collective-permute-start.1 = (bf16[8,6400]{1,0:T(8,128)(2,1)S(1)}, bf16[8,6400]{1,0:T(8,128)(2,1)S(1)}, u32[]{:S(2)}, u32[]{:S(2)}) collective-permute-start(bf16[8,6400]{1,0:T(8,128)(2,1)S(1)} %pad_maximum_fusion.1), channel_id=1, source_target_pairs={{0,4},{1,9},{2,6},{3,11},{4,0},{5,13},{6,2},{7,15},{8,12},{9,1},{1... | collective-permute-start | bytes 307208 | tf_op jit(solution)/shard_map/ppermute | solution.py:497
  11.3 2.8 %collective-permute-done.1 = bf16[8,6400]{1,0:T(8,128)(2,1)S(1)} collective-permute-done((bf16[8,6400]{1,0:T(8,128)(2,1)S(1)}, bf16[8,6400]{1,0:T(8,128)(2,1)S(1)}, u32[]{:S(2)}, u32[]{:S(2)}) %collective-permute-start.1) | collective-permute-done | bytes 102432 | tf_op jit(solution)/shard_map/ppermute | solution.py:497
  14.0 0.1 pad_maximum_fusion.chunk_ref
  14.1 1.9 %collective-permute-start.2 = (bf16[16,6400]{1,0:T(8,128)(2,1)S(1)}, bf16[16,6400]{1,0:T(8,128)(2,1)S(1)}, u32[]{:S(2)}, u32[]{:S(2)}) collective-permute-start(bf16[16,6400]{1,0:T(8,128)(2,1)S(1)} %pad_maximum_fusion.chunk_ref), channel_id=1, source_target_pairs={{0,2},{1,5},{2,0},{3,7},{4,6},{5,1},{6,4},{7,3},{8,10},{9,13},{10,... | collective-permute-start | bytes 614408 | tf_op jit(solution)/shard_map/ppermute | solution.py:497
  16.0 0.0 collective-permute-start.4
  16.0 3.9 %collective-permute-done.2.chunk_ref = bf16[16,6400]{1,0:T(8,128)(2,1)S(1)} collective-permute-done((bf16[16,6400]{1,0:T(8,128)(2,1)S(1)}, bf16[16,6400]{1,0:T(8,128)(2,1)S(1)}, u32[]{:S(2)}, u32[]{:S(2)}) %collective-permute-start.2) | collective-permute-done | bytes 204832 | tf_op jit(solution)/shard_map/ppermute | solution.py:497
  19.9 0.0 collective-permute-start.3
  19.9 0.0 copy-done.1
  19.9 0.0 copy-done.2
  19.9 0.0 copy-done.3
  19.9 1.9 %spread.1 = (bf16[32,6400]{1,0:T(8,128)(2,1)S(1)}, bf16[4,32,6400]{2,1,0:T(8,128)(2,1)S(1)}) custom-call(s32[64]{0:T(128)S(1)} %copy-done.2, s32[16]{0:T(128)S(1)} %copy-done.3, s32[2,16]{1,0:T(2,128)S(1)} %copy-done.1, bf16[4,6400]{1,0:T(4,128)(2,1)S(1)} %front.1.self_ref), custom_call_target="tpu_custom_call" | custom-call | flops 8192000 | bytes 2048000 | tf_op jit(solution)/shard_map/spread/pallas_call | solution.py:261
  21.9 0.0 copy-done
  21.9 2.3 %correlate.4 = (bf16[4,16,9,2,256]{4,3,2,1,0:T(2,128)(2,1)}, f32[4,1152]{1,0:T(4,128)S(1)}) custom-call(s32[64]{0:T(128)S(1)} %copy-done.2, s32[16]{0:T(128)S(1)} %copy-done.3, s32[2,16]{1,0:T(2,128)S(1)} %copy-done.1, bf16[16,6400]{1,0:T(8,128)(2,1)S(1)} %pad_maximum_fusion.chunk_ref, bf16[32,6400]{1,0:T(8,128)(2,1)S(1)} %get-tuple-element.12.rows_ref, ...), custom_call_target="tpu_custom_call" | custom-call | flops 301989888 | bytes 294912 | tf_op jit(solution)/shard_map/correlate/pallas_call | solution.py:464
  24.2 0.0 collective-permute-done.4.chunk_ref
  24.2 2.3 %correlate.5 = (bf16[4,16,9,2,256]{4,3,2,1,0:T(2,128)(2,1)}, f32[4,1152]{1,0:T(4,128)S(1)}) custom-call(s32[64]{0:T(128)S(1)} %copy-done.2, s32[16]{0:T(128)S(1)} %copy-done.3, s32[2,16]{1,0:T(2,128)S(1)} %copy-done.1, bf16[16,6400]{1,0:T(8,128)(2,1)S(1)} %collective-permute-done.4.chunk_ref, ...), custom_call_target="tpu_custom_call", output_to_operand_aliasing={{0}: (8, {})} | custom-call | flops 301989888 | bytes 294912 | tf_op jit(solution)/shard_map/correlate/pallas_call | solution.py:464
  26.5 2.3 %correlate.6 = (bf16[4,16,9,2,256]{4,3,2,1,0:T(2,128)(2,1)}, f32[4,1152]{1,0:T(4,128)S(1)}) custom-call(s32[64]{0:T(128)S(1)} %copy-done.2, s32[16]{0:T(128)S(1)} %copy-done.3, s32[2,16]{1,0:T(2,128)S(1)} %copy-done.1, bf16[16,6400]{1,0:T(8,128)(2,1)S(1)} %collective-permute-done.2.chunk_ref, ...), custom_call_target="tpu_custom_call", output_to_operand_aliasing={{0}: (8, {})} | custom-call | flops 301989888 | bytes 294912 | tf_op jit(solution)/shard_map/correlate/pallas_call | solution.py:464
  28.8 0.0 collective-permute-done.3.chunk_ref
  28.8 2.9 %correlate.7 = (bf16[4,16,9,2,256]{4,3,2,1,0:T(2,128)(2,1)}, f32[4,9]{1,0:T(4,128)}) custom-call(s32[64]{0:T(128)S(1)} %copy-done.2, s32[16]{0:T(128)S(1)} %copy-done.3, s32[2,16]{1,0:T(2,128)S(1)} %copy-done.1, bf16[16,6400]{1,0:T(8,128)(2,1)S(1)} %collective-permute-done.3.chunk_ref, ...), custom_call_target="tpu_custom_call", output_to_operand_aliasing={{0}: (8, {})} | custom-call | flops 301989888 | bytes 294912 | tf_op jit(solution)/shard_map/correlate/pallas_call | solution.py:464
Async XLA Ops:
  0.6 19.3 %copy-start.1 = (s32[2,16]{1,0:T(2,128)S(1)}, s32[2,16]{1,0:T(2,128)}, u32[]{:S(2)}) copy-start(s32[2,16]{1,0:T(2,128)} %constant.8.clone.mask_ref) | copy-start | bytes 388
  0.6 21.2 %copy-start = (bf16[1024,256]{1,0:T(8,128)(2,1)S(1)}, bf16[1024,256]{1,0:T(8,128)(2,1)}, u32[]{:S(2)}) copy-start(bf16[1024,256]{1,0:T(8,128)(2,1)} %constant.9.clone.lag_ref) | copy-start | bytes 1572868
  0.7 19.3 %copy-start.2 = (s32[64]{0:T(128)S(1)}, s32[64]{0:T(128)}, u32[]{:S(2)}) copy-start(s32[64]{0:T(128)} %assign_ref.9) | copy-start | bytes 772
  0.7 19.3 %copy-start.3 = (s32[16]{0:T(128)S(1)}, s32[16]{0:T(128)}, u32[]{:S(2)}) copy-start(s32[16]{0:T(128)} %target_ref.9) | copy-start | bytes 196
  3.0 6.2 %collective-permute-start = (bf16[4,6400]{1,0:T(4,128)(2,1)S(1)}, bf16[4,6400]{1,0:T(4,128)(2,1)S(1)}, u32[]{:S(2)}, u32[]{:S(2)}) collective-permute-start(bf16[4,6400]{1,0:T(4,128)(2,1)S(1)} %front.1.self_ref), channel_id=1, source_target_pairs={{0,8},{1,3},{2,10},{3,1},{4,12},{5,7},{6,14},{7,5},{8,0},{9,11},{1... | collective-permute-start | bytes 153608 | tf_op jit(solution)/shard_map/ppermute | solution.py:497
  9.3 4.7 %collective-permute-start.1 = (bf16[8,6400]{1,0:T(8,128)(2,1)S(1)}, bf16[8,6400]{1,0:T(8,128)(2,1)S(1)}, u32[]{:S(2)}, u32[]{:S(2)}) collective-permute-start(bf16[8,6400]{1,0:T(8,128)(2,1)S(1)} %pad_maximum_fusion.1), channel_id=1, source_target_pairs={{0,4},{1,9},{2,6},{3,11},{4,0},{5,13},{6,2},{7,15},{8,12},{9,1},{1... | collective-permute-start | bytes 307208 | tf_op jit(solution)/shard_map/ppermute | solution.py:497
  14.1 5.8 %collective-permute-start.2 = (bf16[16,6400]{1,0:T(8,128)(2,1)S(1)}, bf16[16,6400]{1,0:T(8,128)(2,1)S(1)}, u32[]{:S(2)}, u32[]{:S(2)}) collective-permute-start(bf16[16,6400]{1,0:T(8,128)(2,1)S(1)} %pad_maximum_fusion.chunk_ref), channel_id=1, source_target_pairs={{0,2},{1,5},{2,0},{3,7},{4,6},{5,1},{6,4},{7,3},{8,10},{9,13},{10,... | collective-permute-start | bytes 614408 | tf_op jit(solution)/shard_map/ppermute | solution.py:497
  16.0 8.2 %collective-permute-start.4 = (bf16[16,6400]{1,0:T(8,128)(2,1)S(1)}, bf16[16,6400]{1,0:T(8,128)(2,1)S(1)}, u32[]{:S(2)}, u32[]{:S(2)}) collective-permute-start(bf16[16,6400]{1,0:T(8,128)(2,1)S(1)} %pad_maximum_fusion.chunk_ref), channel_id=1, source_target_pairs={{0,1},{1,0},{2,3},{3,2},{4,5},{5,4},{6,7},{7,6},{8,9},{9,8},{10,11... | collective-permute-start | bytes 614408 | tf_op jit(solution)/shard_map/ppermute | solution.py:497
  19.9 8.9 %collective-permute-start.3 = (bf16[16,6400]{1,0:T(8,128)(2,1)S(1)}, bf16[16,6400]{1,0:T(8,128)(2,1)S(1)}, u32[]{:S(2)}, u32[]{:S(2)}) collective-permute-start(bf16[16,6400]{1,0:T(8,128)(2,1)S(1)} %collective-permute-done.2.chunk_ref), channel_id=1, source_target_pairs={{0,1},{1,0},{2,3},{3,2},{4,5},{5,4},{6,7},{7,6},{8,9},{9,8},{10,11... | collective-permute-start | bytes 614408 | tf_op jit(solution)/shard_map/ppermute | solution.py:497

commit v4 on v3

--- a/solution.py
+++ b/solution.py
@@ -57,7 +57,8 @@
     bins = FLO + bin_order()[:, None]
     shifts = np.arange(LAGS)[None, :] - LAGS // 2
     phase = np.mod(bins * shifts, SEG) * (2.0 * math.pi / SEG)
-    return np.concatenate([np.cos(phase), -np.sin(phase)], 0).astype(jnp.bfloat16)
+    both = np.stack([np.cos(phase), -np.sin(phase)], 0).reshape(2, FREQ // TILE, TILE, LAGS)
+    return both.transpose(1, 0, 2, 3).reshape(2 * FREQ, LAGS).astype(jnp.bfloat16)
 
 
 def mm(a, b):
@@ -280,13 +281,12 @@
 ):
     if not first:
         sum_in, rest = rest[0], rest[2:]
-    out_ref, sum_ref, picked, cross, result, outv, sem = rest
+    out_ref, sum_ref, picked, cross_e, result_e, cross, result, outv, sem = rest
     me = lax.axis_index("pairs")
     parity = lax.rem(me, 2)
     pairs = GROUP * CAP
     stations = GROUP * own
     nine = COMP * COMP
-    half = own * nine * pairs
     chunks = chunk_ref.shape[0] // stations
     my_target = target_ref[me]
     total = jnp.zeros((own, nine * LANE), jnp.float32) if first else sum_in[...]
@@ -325,47 +325,79 @@
                 im = i if im is None else im + i
             return re, im
 
-        def one_tile(lt, carry):
-            re_at = pl.ds(pl.multiple_of(lt * TILE, TILE), TILE)
-            im_at = pl.ds(pl.multiple_of(FREQ + lt * TILE, TILE), TILE)
-
-            def tile(load, a):
-                got = []
-                for w in range(windows):
-                    both = []
-                    for part in range(2):
-                        start = ((w * COMP + a) * 2 + part) * FREQ + lt * TILE
-                        both.append(load(pl.ds(pl.multiple_of(start, TILE), TILE)))
-                    got.append(both)
-                return got
-
-            slots = [tile(lambda d: picked[:, d], b) for b in range(COMP)]
+        def tile(load, a, lt):
+            got = []
+            for w in range(windows):
+                both = []
+                for part in range(2):
+                    start = ((w * COMP + a) * 2 + part) * FREQ + lt * TILE
+                    both.append(load(slice(start, start + TILE)))
+                got.append(both)
+            return got
+
+        def partner(rows, lanes):
+            return partner_ref[base // GROUP + ch, rows, lanes]
+
+        tiles = FREQ // TILE
+
+        def keep(ref, at, rows, lt, values):
+            for part in range(2):
+                start = (2 * lt + part) * TILE
+                ref[at : at + rows, start : start + TILE] = values[part]
+
+        for lt in range(tiles):
+            lefts = [tile(lambda d: chunk_ref[here, d], a, lt) for a in range(COMP)]
+            for c in range(CAP):
+                part_rows = slice(c * stations, (c + 1) * stations)
+                for b in range(COMP):
+                    right = tile(lambda d: partner(part_rows, d), b, lt)
+                    for a in range(COMP):
+                        at = ((c * COMP + a) * COMP + b) * stations
+                        keep(cross_e, at, stations, lt, product(lefts[a], right))
+        result_e[...] = mm(cross_e[...], lag_ref[...])
+        for lt in range(tiles):
+            slots = [tile(lambda d: picked[:, d], b, lt) for b in range(COMP)]
             for yp in range(own // 2):
+                y_rows = slice(yp * 2 * pairs, (yp + 1) * 2 * pairs)
                 for a in range(COMP):
-                    left = tile(lambda d: rows_ref[yp * 2 * pairs : (yp + 1) * 2 * pairs, d], a)
+                    left = tile(lambda d: rows_ref[y_rows, d], a, lt)
                     for b in range(COMP):
                         at = ((yp * COMP + a) * COMP + b) * 2 * pairs
-                        re, im = product(left, slots[b])
-                        cross[at : at + 2 * pairs, re_at] = re
-                        cross[at : at + 2 * pairs, im_at] = im
-            lefts = [tile(lambda d: chunk_ref[here, d], a) for a in range(COMP)]
-            for c in range(CAP):
-                for b in range(COMP):
-                    right = tile(
-                        lambda d: partner_ref[base // GROUP + ch, c * stations : (c + 1) * stations, d], b
-                    )
-                    for a in range(COMP):
-                        re, im = product(lefts[a], right)
-                        at = half + ((c * COMP + a) * COMP + b) * stations
-                        cross[at : at + stations, re_at] = re
-                        cross[at : at + stations, im_at] = im
-            return carry
-
-        lax.fori_loop(0, FREQ // TILE, one_tile, 0)
+                        keep(cross, at, 2 * pairs, lt, product(left, slots[b]))
         result[...] = mm(cross[...], lag_ref[...])
 
-        def flag(ref, rows, w):
-            return ref[rows, PLANE * windows + w * LANE : PLANE * windows + (w + 1) * LANE]
+        def flag_at(w):
+            return slice(PLANE * windows + w * LANE, PLANE * windows + (w + 1) * LANE)
+
+        weights, squares = [], []
+        col = iota(own, stations, 1) // own
+        y_row = iota(own, stations, 0)
+        for c in range(CAP):
+            part_rows = slice(c * stations, (c + 1) * stations)
+            weight = jnp.zeros((own, stations), jnp.float32)
+            for j in range(GROUP):
+                hit = jnp.logical_and(col == j, y_row == mine[j][c])
+                weight = jnp.where(hit, 1.0, weight)
+            weights.append(weight)
+            count = None
+            for w in range(windows):
+                left = chunk_ref[here, flag_at(w)].astype(jnp.float32)
+                term = left * partner(part_rows, flag_at(w)).astype(jnp.float32)
+                count = term if count is None else count + term
+            most = jnp.maximum(count, 1.0)
+            share = 1.0 / (most * most * float(FREQ))
+            lines = []
+            for q in range(nine):
+                at = (c * nine + q) * stations
+                block = result_e[at : at + stations, :]
+                square = block * block
+                both = square[:, :LANE]
+                for lt in range(1, LAGS // LANE):
+                    both = both + square[:, lt * LANE : (lt + 1) * LANE]
+                lines.append(both * share)
+            squares.append(jnp.concatenate(lines, 1))
+        weights = jnp.concatenate(weights, 1).astype(jnp.bfloat16)
+        total = total + mm(weights, jnp.concatenate(squares, 0).astype(jnp.bfloat16))
 
         if not isinstance(ch, int):
 
@@ -377,8 +409,8 @@
         for yp in range(own // 2):
             count = None
             for w in range(windows):
-                left = flag(rows_ref, slice(yp * 2 * pairs, (yp + 1) * 2 * pairs), w)
-                term = left.astype(jnp.float32) * flag(picked, slice(None), w).astype(jnp.float32)
+                left = rows_ref[yp * 2 * pairs : (yp + 1) * 2 * pairs, flag_at(w)].astype(jnp.float32)
+                term = left * picked[:, flag_at(w)].astype(jnp.float32)
                 count = term if count is None else count + term
             scale = 1.0 / (jnp.maximum(count, 1.0) * math.sqrt(FREQ))
             scale = jnp.concatenate([scale] * (LAGS // LANE), 1)
@@ -388,37 +420,7 @@
                 outv[slot, 2 * yp : 2 * yp + 2, :, q, :, :] = block.reshape(2, GROUP, CAP, LAGS)
         for cp in copies(ch):
             cp.start()
-        weights, squares = [], []
-        col = iota(own, stations, 1) // own
-        y_row = iota(own, stations, 0)
-        for c in range(CAP):
-            weight = jnp.zeros((own, stations), jnp.float32)
-            for j in range(GROUP):
-                hit = jnp.logical_and(col == j, y_row == mine[j][c])
-                weight = jnp.where(hit, 1.0, weight)
-            weights.append(weight)
-            count = None
-            for w in range(windows):
-                left = flag(chunk_ref, here, w).astype(jnp.float32)
-                part_rows = slice(c * stations, (c + 1) * stations)
-                lanes = slice(PLANE * windows + w * LANE, PLANE * windows + (w + 1) * LANE)
-                right = partner_ref[base // GROUP + ch, part_rows, lanes].astype(jnp.float32)
-                term = left * right
-                count = term if count is None else count + term
-            most = jnp.maximum(count, 1.0)
-            share = 1.0 / (most * most * float(FREQ))
-            tiles = []
-            for q in range(nine):
-                at = half + (c * nine + q) * stations
-                block = result[at : at + stations, :]
-                square = block * block
-                both = square[:, :LANE]
-                for lt in range(1, LAGS // LANE):
-                    both = both + square[:, lt * LANE : (lt + 1) * LANE]
-                tiles.append(both * share)
-            squares.append(jnp.concatenate(tiles, 1))
-        weights = jnp.concatenate(weights, 1).astype(jnp.bfloat16)
-        return total + mm(weights, jnp.concatenate(squares, 0).astype(jnp.bfloat16))
+        return total
 
     if chunks == 1:
         total = one_chunk(0, total)
@@ -472,8 +474,10 @@
         input_output_aliases=aliases,
         scratch_shapes=[
             pltpu.VMEM((2 * pairs, WIDE), bf16),
-            pltpu.VMEM((lines, 2 * FREQ), bf16),
-            pltpu.VMEM((lines, LAGS), f32),
+            pltpu.VMEM((CAP * nine * stations, 2 * FREQ), bf16),
+            pltpu.VMEM((CAP * nine * stations, LAGS), f32),
+            pltpu.VMEM((own * nine * pairs, 2 * FREQ), bf16),
+            pltpu.VMEM((own * nine * pairs, LAGS), f32),
             pltpu.VMEM((2, own, GROUP, nine, CAP, LAGS), bf16),
             pltpu.SemaphoreType.DMA((2,)),
         ],

time: 31.8 us -> 30.8 us (0.969)
  Pallas kernels: 14 us -> 12.9 us
    pallas_call x4, Pallas kernels: 9.74 us -> 8.68 us  [correlate(): pl.pallas_call(functools.partial(correlate_kernel, owners, own, windows,...]
  transfers between devices with their start and end apart: 5 -> 5, of which waited for: 3 -> 3; matrix products, arithmetic and copies ran while one was open for 0% -> 0% of each run, Pallas kernels for 28% -> 26%
where the time goes in v4:
time: 30.8 us; the launch traced here: 30.6 us
  Pallas kernels  12.9 us (42%)
  waiting for transfers between devices  8.76 us (28%)
  starting transfers between devices  8.02 us (26%)
  between operations  0.75 us (2%)
    ppermute x5, waiting for transfers between devices, swap(): lax.ppermute(block, 'pairs', [(i, i ^ masks_of[i % 2]) for i in range(own...  8.76 us
    pallas_call x4, Pallas kernels, correlate(): pl.pallas_call(functools.partial(correlate_kernel, owners, own, windows,...  8.68 us
    ppermute x5, starting transfers between devices, swap(): lax.ppermute(block, 'pairs', [(i, i ^ masks_of[i % 2]) for i in range(own...  8.02 us
    pallas_call x1, Pallas kernels, front(): pl.pallas_call(front_kernel, out_shape=jax.ShapeDtypeStruct((own, windows...  2.32 us
    pallas_call x1, Pallas kernels, spread(): pl.pallas_call(functools.partial(spread_kernel, own), out_shape=(jax.Shap...  1.94 us
  transfers between devices with their start and end apart: 5, of which 3 were waited for; matrix products, arithmetic and copies ran while one was open for 0% of the time, Pallas kernels for 26%

profile of v4, /device:TPU:0, one launch (start us, length us, event | category | flops | bytes accessed | tf_op | source)
XLA Modules:
  0.0 30.6 jit_solution(4689231014062223822)
XLA Ops:
  0.6 0.0 copy-start.1
  0.6 0.0 copy-start
  0.7 0.0 copy-start.2
  0.7 0.0 copy-start.3
  0.7 2.3 %front.1.self_ref = bf16[4,6400]{1,0:T(4,128)(2,1)S(1)} custom-call(s32[2,4]{1,0:T(2,128)} %bitcast.5, bf16[3,4,4096]{2,1,0:T(4,128)(2,1)} %bitcast.4, bf16[3072,256]{1,0:T(8,128)(2,1)} %constant.10.clone.tab_hbm, bf16[512,512]{1,0:T(8,128)(2,1)} %constant.11.clone.band_hbm), custom_call_target="tpu_custom_call" | custom-call | tf_op jit(solution)/shard_map/front/pallas_call | solution.py:169
  3.0 4.1 %collective-permute-start = (bf16[4,6400]{1,0:T(4,128)(2,1)S(1)}, bf16[4,6400]{1,0:T(4,128)(2,1)S(1)}, u32[]{:S(2)}, u32[]{:S(2)}) collective-permute-start(bf16[4,6400]{1,0:T(4,128)(2,1)S(1)} %front.1.self_ref), channel_id=1, source_target_pairs={{0,8},{1,3},{2,10},{3,1},{4,12},{5,7},{6,14},{7,5},{8,0},{9,11},{1... | collective-permute-start | bytes 153608 | tf_op jit(solution)/shard_map/ppermute | solution.py:501
  7.1 2.1 %collective-permute-done = bf16[4,6400]{1,0:T(4,128)(2,1)S(1)} collective-permute-done((bf16[4,6400]{1,0:T(4,128)(2,1)S(1)}, bf16[4,6400]{1,0:T(4,128)(2,1)S(1)}, u32[]{:S(2)}, u32[]{:S(2)}) %collective-permute-start) | collective-permute-done | bytes 51232 | tf_op jit(solution)/shard_map/ppermute | solution.py:501
  9.2 0.1 pad_maximum_fusion.1
  9.3 2.0 %collective-permute-start.1 = (bf16[8,6400]{1,0:T(8,128)(2,1)S(1)}, bf16[8,6400]{1,0:T(8,128)(2,1)S(1)}, u32[]{:S(2)}, u32[]{:S(2)}) collective-permute-start(bf16[8,6400]{1,0:T(8,128)(2,1)S(1)} %pad_maximum_fusion.1), channel_id=1, source_target_pairs={{0,4},{1,9},{2,6},{3,11},{4,0},{5,13},{6,2},{7,15},{8,12},{9,1},{1... | collective-permute-start | bytes 307208 | tf_op jit(solution)/shard_map/ppermute | solution.py:501
  11.3 2.8 %collective-permute-done.1 = bf16[8,6400]{1,0:T(8,128)(2,1)S(1)} collective-permute-done((bf16[8,6400]{1,0:T(8,128)(2,1)S(1)}, bf16[8,6400]{1,0:T(8,128)(2,1)S(1)}, u32[]{:S(2)}, u32[]{:S(2)}) %collective-permute-start.1) | collective-permute-done | bytes 102432 | tf_op jit(solution)/shard_map/ppermute | solution.py:501
  14.0 0.1 pad_maximum_fusion.chunk_ref
  14.1 1.9 %collective-permute-start.2 = (bf16[16,6400]{1,0:T(8,128)(2,1)S(1)}, bf16[16,6400]{1,0:T(8,128)(2,1)S(1)}, u32[]{:S(2)}, u32[]{:S(2)}) collective-permute-start(bf16[16,6400]{1,0:T(8,128)(2,1)S(1)} %pad_maximum_fusion.chunk_ref), channel_id=1, source_target_pairs={{0,2},{1,5},{2,0},{3,7},{4,6},{5,1},{6,4},{7,3},{8,10},{9,13},{10,... | collective-permute-start | bytes 614408 | tf_op jit(solution)/shard_map/ppermute | solution.py:501
  16.0 0.0 collective-permute-start.4
  16.0 3.9 %collective-permute-done.2.chunk_ref = bf16[16,6400]{1,0:T(8,128)(2,1)S(1)} collective-permute-done((bf16[16,6400]{1,0:T(8,128)(2,1)S(1)}, bf16[16,6400]{1,0:T(8,128)(2,1)S(1)}, u32[]{:S(2)}, u32[]{:S(2)}) %collective-permute-start.2) | collective-permute-done | bytes 204832 | tf_op jit(solution)/shard_map/ppermute | solution.py:501
  19.9 0.0 collective-permute-start.3
  19.9 0.0 copy-done.1
  19.9 0.0 copy-done.2
  19.9 0.0 copy-done.3
  19.9 1.9 %spread.1 = (bf16[32,6400]{1,0:T(8,128)(2,1)S(1)}, bf16[4,32,6400]{2,1,0:T(8,128)(2,1)S(1)}) custom-call(s32[64]{0:T(128)S(1)} %copy-done.2, s32[16]{0:T(128)S(1)} %copy-done.3, s32[2,16]{1,0:T(2,128)S(1)} %copy-done.1, bf16[4,6400]{1,0:T(4,128)(2,1)S(1)} %front.1.self_ref), custom_call_target="tpu_custom_call" | custom-call | flops 8192000 | bytes 2048000 | tf_op jit(solution)/shard_map/spread/pallas_call | solution.py:262
  21.9 0.0 copy-done
  21.9 2.0 %correlate.4 = (bf16[4,16,9,2,256]{4,3,2,1,0:T(2,128)(2,1)}, f32[4,1152]{1,0:T(4,128)S(1)}) custom-call(s32[64]{0:T(128)S(1)} %copy-done.2, s32[16]{0:T(128)S(1)} %copy-done.3, s32[2,16]{1,0:T(2,128)S(1)} %copy-done.1, bf16[16,6400]{1,0:T(8,128)(2,1)S(1)} %pad_maximum_fusion.chunk_ref, bf16[32,6400]{1,0:T(8,128)(2,1)S(1)} %get-tuple-element.12.rows_ref, ...), custom_call_target="tpu_custom_call" | custom-call | flops 301989888 | bytes 294912 | tf_op jit(solution)/shard_map/correlate/pallas_call | solution.py:466
  23.9 0.0 collective-permute-done.4.chunk_ref
  23.9 2.0 %correlate.5 = (bf16[4,16,9,2,256]{4,3,2,1,0:T(2,128)(2,1)}, f32[4,1152]{1,0:T(4,128)S(1)}) custom-call(s32[64]{0:T(128)S(1)} %copy-done.2, s32[16]{0:T(128)S(1)} %copy-done.3, s32[2,16]{1,0:T(2,128)S(1)} %copy-done.1, bf16[16,6400]{1,0:T(8,128)(2,1)S(1)} %collective-permute-done.4.chunk_ref, ...), custom_call_target="tpu_custom_call", output_to_operand_aliasing={{0}: (8, {})} | custom-call | flops 301989888 | bytes 294912 | tf_op jit(solution)/shard_map/correlate/pallas_call | solution.py:466
  26.0 2.0 %correlate.6 = (bf16[4,16,9,2,256]{4,3,2,1,0:T(2,128)(2,1)}, f32[4,1152]{1,0:T(4,128)S(1)}) custom-call(s32[64]{0:T(128)S(1)} %copy-done.2, s32[16]{0:T(128)S(1)} %copy-done.3, s32[2,16]{1,0:T(2,128)S(1)} %copy-done.1, bf16[16,6400]{1,0:T(8,128)(2,1)S(1)} %collective-permute-done.2.chunk_ref, ...), custom_call_target="tpu_custom_call", output_to_operand_aliasing={{0}: (8, {})} | custom-call | flops 301989888 | bytes 294912 | tf_op jit(solution)/shard_map/correlate/pallas_call | solution.py:466
  28.0 0.0 collective-permute-done.3.chunk_ref
  28.0 2.6 %correlate.7 = (bf16[4,16,9,2,256]{4,3,2,1,0:T(2,128)(2,1)}, f32[4,9]{1,0:T(4,128)}) custom-call(s32[64]{0:T(128)S(1)} %copy-done.2, s32[16]{0:T(128)S(1)} %copy-done.3, s32[2,16]{1,0:T(2,128)S(1)} %copy-done.1, bf16[16,6400]{1,0:T(8,128)(2,1)S(1)} %collective-permute-done.3.chunk_ref, ...), custom_call_target="tpu_custom_call", output_to_operand_aliasing={{0}: (8, {})} | custom-call | flops 301989888 | bytes 294912 | tf_op jit(solution)/shard_map/correlate/pallas_call | solution.py:466
Async XLA Ops:
  0.6 19.3 %copy-start.1 = (s32[2,16]{1,0:T(2,128)S(1)}, s32[2,16]{1,0:T(2,128)}, u32[]{:S(2)}) copy-start(s32[2,16]{1,0:T(2,128)} %constant.8.clone.mask_ref) | copy-start | bytes 388
  0.6 21.2 %copy-start = (bf16[1024,256]{1,0:T(8,128)(2,1)S(1)}, bf16[1024,256]{1,0:T(8,128)(2,1)}, u32[]{:S(2)}) copy-start(bf16[1024,256]{1,0:T(8,128)(2,1)} %constant.9.clone.lag_ref) | copy-start | bytes 1572868
  0.7 19.3 %copy-start.2 = (s32[64]{0:T(128)S(1)}, s32[64]{0:T(128)}, u32[]{:S(2)}) copy-start(s32[64]{0:T(128)} %assign_ref.9) | copy-start | bytes 772
  0.7 19.3 %copy-start.3 = (s32[16]{0:T(128)S(1)}, s32[16]{0:T(128)}, u32[]{:S(2)}) copy-start(s32[16]{0:T(128)} %target_ref.9) | copy-start | bytes 196
  3.0 6.2 %collective-permute-start = (bf16[4,6400]{1,0:T(4,128)(2,1)S(1)}, bf16[4,6400]{1,0:T(4,128)(2,1)S(1)}, u32[]{:S(2)}, u32[]{:S(2)}) collective-permute-start(bf16[4,6400]{1,0:T(4,128)(2,1)S(1)} %front.1.self_ref), channel_id=1, source_target_pairs={{0,8},{1,3},{2,10},{3,1},{4,12},{5,7},{6,14},{7,5},{8,0},{9,11},{1... | collective-permute-start | bytes 153608 | tf_op jit(solution)/shard_map/ppermute | solution.py:501
  9.3 4.7 %collective-permute-start.1 = (bf16[8,6400]{1,0:T(8,128)(2,1)S(1)}, bf16[8,6400]{1,0:T(8,128)(2,1)S(1)}, u32[]{:S(2)}, u32[]{:S(2)}) collective-permute-start(bf16[8,6400]{1,0:T(8,128)(2,1)S(1)} %pad_maximum_fusion.1), channel_id=1, source_target_pairs={{0,4},{1,9},{2,6},{3,11},{4,0},{5,13},{6,2},{7,15},{8,12},{9,1},{1... | collective-permute-start | bytes 307208 | tf_op jit(solution)/shard_map/ppermute | solution.py:501
  14.1 5.8 %collective-permute-start.2 = (bf16[16,6400]{1,0:T(8,128)(2,1)S(1)}, bf16[16,6400]{1,0:T(8,128)(2,1)S(1)}, u32[]{:S(2)}, u32[]{:S(2)}) collective-permute-start(bf16[16,6400]{1,0:T(8,128)(2,1)S(1)} %pad_maximum_fusion.chunk_ref), channel_id=1, source_target_pairs={{0,2},{1,5},{2,0},{3,7},{4,6},{5,1},{6,4},{7,3},{8,10},{9,13},{10,... | collective-permute-start | bytes 614408 | tf_op jit(solution)/shard_map/ppermute | solution.py:501
  16.0 7.9 %collective-permute-start.4 = (bf16[16,6400]{1,0:T(8,128)(2,1)S(1)}, bf16[16,6400]{1,0:T(8,128)(2,1)S(1)}, u32[]{:S(2)}, u32[]{:S(2)}) collective-permute-start(bf16[16,6400]{1,0:T(8,128)(2,1)S(1)} %pad_maximum_fusion.chunk_ref), channel_id=1, source_target_pairs={{0,1},{1,0},{2,3},{3,2},{4,5},{5,4},{6,7},{7,6},{8,9},{9,8},{10,11... | collective-permute-start | bytes 614408 | tf_op jit(solution)/shard_map/ppermute | solution.py:501
  19.9 8.1 %collective-permute-start.3 = (bf16[16,6400]{1,0:T(8,128)(2,1)S(1)}, bf16[16,6400]{1,0:T(8,128)(2,1)S(1)}, u32[]{:S(2)}, u32[]{:S(2)}) collective-permute-start(bf16[16,6400]{1,0:T(8,128)(2,1)S(1)} %collective-permute-done.2.chunk_ref), channel_id=1, source_target_pairs={{0,1},{1,0},{2,3},{3,2},{4,5},{5,4},{6,7},{7,6},{8,9},{9,8},{10,11... | collective-permute-start | bytes 614408 | tf_op jit(solution)/shard_map/ppermute | solution.py:501

commit v5 on v4

--- a/solution.py
+++ b/solution.py
@@ -190,16 +190,25 @@
     return [chips, chips[-1:] + chips[:-1]]
 
 
-def owner_masks(plan):
-    own_core = []
-    for chips in plan:
-        found = [0]
-        for m in chips:
-            found = found + [f ^ m for f in found]
-        own_core.append(found)
-    return np.asarray(
-        [own_core[p] + [1 ^ f for f in own_core[1 - p]] for p in range(2)], np.int32
-    )
+def owner_at(plan, me, place):
+    parity = lax.rem(me, 2)
+    bits = len(plan[0])
+    if isinstance(place, int):
+        found = []
+        for p in range(2):
+            far = place >> bits
+            mask = far
+            for i, m in enumerate(plan[p ^ far]):
+                mask ^= m * ((place >> i) & 1)
+            found.append(mask)
+        return me ^ jnp.where(parity == 0, found[0], found[1])
+    far = place >> bits
+    side = parity ^ far
+    mask = far
+    for i in range(bits):
+        step = jnp.where(side == 0, plan[0][i], plan[1][i])
+        mask = mask ^ (step * ((place >> i) & 1))
+    return me ^ mask
 
 
 def room(operand_bytes):
@@ -224,14 +233,8 @@
     return jnp.where(iota(want.shape[0], cols, 1) == want, 1.0, 0.0).astype(jnp.bfloat16)
 
 
-def own_slots(assign_ref, target_ref, me, own, owner):
-    want = target_ref[owner]
-    return first_two([assign_ref[me * own + s] == want for s in range(own)])
-
-
-def spread_kernel(own, assign_ref, target_ref, mask_ref, self_ref, rows_ref, partner_ref):
+def spread_kernel(plan, own, assign_ref, target_ref, self_ref, rows_ref, partner_ref, pick_ref, weight_ref):
     me = lax.axis_index("pairs")
-    parity = lax.rem(me, 2)
     pairs = GROUP * CAP
     stations = GROUP * own
     mine_rows = self_ref[...]
@@ -240,81 +243,101 @@
     )
     place = iota(CAP * stations, own, 0)
     place = (place // stations) * GROUP + (place % stations) // own
+    slot = iota(2 * pairs, stations, 0) % pairs
+    col = iota(own, CAP * stations, 1)
+    col = (col // stations) * GROUP + (col % stations) // own
+    y_row = iota(own, CAP * stations, 0)
+    my_target = target_ref[me]
 
     def one_chunk(ch, carry):
         want = jnp.full(place.shape, NONE, jnp.int32)
+        taken = jnp.full(slot.shape, NONE, jnp.int32)
+        weight = jnp.zeros(col.shape, jnp.float32)
         for j in range(GROUP):
-            owner = me ^ mask_ref[parity, ch * GROUP + j]
-            for c, s in enumerate(own_slots(assign_ref, target_ref, me, own, owner)):
-                want = jnp.where(place == c * GROUP + j, s, want)
+            owner = owner_at(plan, me, ch * GROUP + j)
+            wanted = target_ref[owner]
+            mine = first_two([assign_ref[me * own + s] == wanted for s in range(own)])
+            theirs = first_two([assign_ref[owner * own + s] == my_target for s in range(own)])
+            for c in range(CAP):
+                want = jnp.where(place == c * GROUP + j, mine[c], want)
+                hit = jnp.logical_and(col == c * GROUP + j, y_row == mine[c])
+                weight = jnp.where(hit, 1.0, weight)
+                taken = jnp.where(slot == j * CAP + c, theirs[c] + j * own, taken)
         partner_ref[ch] = mm(one_hot(want, own), mine_rows).astype(jnp.bfloat16)
+        pick_ref[ch] = one_hot(taken, stations)
+        weight_ref[ch] = weight.astype(jnp.bfloat16)
         return carry
 
     lax.fori_loop(0, partner_ref.shape[0], one_chunk, 0)
 
 
-def spread(held, assign, target, masks):
+def spread(plan, held, assign, target):
     own = held.shape[0]
-    chunks = masks.shape[1] // GROUP
+    chunks = target.shape[0] // GROUP
+    stations, pairs = GROUP * own, GROUP * CAP
     smem = pl.BlockSpec(memory_space=pltpu.SMEM)
     vmem = pl.BlockSpec(memory_space=pltpu.VMEM)
-    made = own * GROUP * CAP + chunks * CAP * GROUP * own
+    made = own * pairs + chunks * CAP * stations
+    bf16 = jnp.bfloat16
     return pl.pallas_call(
-        functools.partial(spread_kernel, own),
+        functools.partial(spread_kernel, plan, own),
         out_shape=(
-            jax.ShapeDtypeStruct((own * GROUP * CAP, WIDE), jnp.bfloat16),
-            jax.ShapeDtypeStruct((chunks, CAP * GROUP * own, WIDE), jnp.bfloat16),
+            jax.ShapeDtypeStruct((own * pairs, WIDE), bf16),
+            jax.ShapeDtypeStruct((chunks, CAP * stations, WIDE), bf16),
+            jax.ShapeDtypeStruct((chunks, 2 * pairs, stations), bf16),
+            jax.ShapeDtypeStruct((chunks, own, CAP * stations), bf16),
         ),
-        in_specs=[smem] * 3 + [vmem],
-        out_specs=(vmem, vmem),
+        in_specs=[smem] * 2 + [vmem],
+        out_specs=(vmem,) * 4,
         compiler_params=room(2 * made * WIDE),
         cost_estimate=pl.CostEstimate(
             flops=2 * made * own * WIDE, bytes_accessed=2 * made * WIDE, transcendentals=0
         ),
         name="spread",
-    )(assign, target, masks, held)
-
-
-def correlate_kernel(
-    owners, own, windows, base, first, last, assign_ref, target_ref, mask_ref, chunk_ref, rows_ref,
-    partner_ref, lag_ref, *rest,
-):
-    if not first:
-        sum_in, rest = rest[0], rest[2:]
-    out_ref, sum_ref, picked, cross_e, result_e, cross, result, outv, sem = rest
+    )(assign, target, held)
+
+
+def correlate_kernel(plan, owners, own, windows, base, kind, chunk_ref, *refs):
+    refs = list(refs)
+    rows_ref, partner_ref, pick_ref, weight_ref, lag_ref = refs[:5]
+    refs = refs[5:]
+    sum_in = refs.pop(0) if kind["sums"] else None
+    waiting = refs.pop(0) if kind["waiting"] is not None else None
+    if kind["out_in"]:
+        refs.pop(0)
+    out_ref = refs.pop(0) if kind["out"] else None
+    kept = refs.pop(0) if kind["keep"] else None
+    sum_ref = refs.pop(0)
+    picked, cross_e, result_e, cross, result, outv, energy_v, sem = refs
     me = lax.axis_index("pairs")
-    parity = lax.rem(me, 2)
     pairs = GROUP * CAP
     stations = GROUP * own
     nine = COMP * COMP
     chunks = chunk_ref.shape[0] // stations
-    my_target = target_ref[me]
-    total = jnp.zeros((own, nine * LANE), jnp.float32) if first else sum_in[...]
-
-    def owner_of(ch, j):
-        return me ^ mask_ref[parity, base + ch * GROUP + j]
-
-    def copies(ch):
-        which = lax.rem(ch, 2)
+    total = sum_in[...] if kind["sums"] else jnp.zeros((own, nine * LANE), jnp.float32)
+
+    def flush(source, place, which, ys=slice(None)):
         return [
-            pltpu.make_async_copy(outv.at[which, :, j], out_ref.at[:, owner_of(ch, j)], sem.at[which])
+            pltpu.make_async_copy(
+                source.at[ys, j], out_ref.at[ys, owner_at(plan, me, place + j)], sem.at[which]
+            )
             for j in range(GROUP)
         ]
+
+    def copies(ch):
+        return flush(outv.at[lax.rem(ch, 2)], base + ch * GROUP, lax.rem(ch, 2))
+
+    before = [] if waiting is None else flush(waiting, kind["waiting"], 2)
+    for cp in before:
+        cp.start()
+    started = []
 
     def one_chunk(ch, total):
         slot = lax.rem(ch, 2)
         first_row = ch * stations if isinstance(ch, int) else pl.multiple_of(ch * stations, stations)
         here = pl.ds(first_row, stations)
-        row = iota(2 * pairs, stations, 0) % pairs
-        want = jnp.full(row.shape, NONE, jnp.int32)
-        mine = []
-        for j in range(GROUP):
-            owner = owner_of(ch, j)
-            theirs = first_two([assign_ref[owner * own + s] == my_target for s in range(own)])
-            for c, s in enumerate(theirs):
-                want = jnp.where(row == j * CAP + c, s + j * own, want)
-            mine.append(own_slots(assign_ref, target_ref, me, own, owner))
-        picked[...] = mm(one_hot(want, stations), chunk_ref[here, :]).astype(jnp.bfloat16)
+        number = base // GROUP + ch
+        picked[...] = mm(pick_ref[number], chunk_ref[here, :]).astype(jnp.bfloat16)
 
         def product(left, right):
             re = im = None
@@ -336,7 +359,7 @@
             return got
 
         def partner(rows, lanes):
-            return partner_ref[base // GROUP + ch, rows, lanes]
+            return partner_ref[number, rows, lanes]
 
         tiles = FREQ // TILE
 
@@ -369,16 +392,9 @@
         def flag_at(w):
             return slice(PLANE * windows + w * LANE, PLANE * windows + (w + 1) * LANE)
 
-        weights, squares = [], []
-        col = iota(own, stations, 1) // own
-        y_row = iota(own, stations, 0)
+        squares = []
         for c in range(CAP):
             part_rows = slice(c * stations, (c + 1) * stations)
-            weight = jnp.zeros((own, stations), jnp.float32)
-            for j in range(GROUP):
-                hit = jnp.logical_and(col == j, y_row == mine[j][c])
-                weight = jnp.where(hit, 1.0, weight)
-            weights.append(weight)
             count = None
             for w in range(windows):
                 left = chunk_ref[here, flag_at(w)].astype(jnp.float32)
@@ -396,8 +412,9 @@
                     both = both + square[:, lt * LANE : (lt + 1) * LANE]
                 lines.append(both * share)
             squares.append(jnp.concatenate(lines, 1))
-        weights = jnp.concatenate(weights, 1).astype(jnp.bfloat16)
-        total = total + mm(weights, jnp.concatenate(squares, 0).astype(jnp.bfloat16))
+        total = total + mm(weight_ref[number], jnp.concatenate(squares, 0).astype(jnp.bfloat16))
+        if kind["last"] and chunks == 1:
+            finish(total)
 
         if not isinstance(ch, int):
 
@@ -414,87 +431,123 @@
                 count = term if count is None else count + term
             scale = 1.0 / (jnp.maximum(count, 1.0) * math.sqrt(FREQ))
             scale = jnp.concatenate([scale] * (LAGS // LANE), 1)
+            ys = slice(2 * yp, 2 * yp + 2)
             for q in range(nine):
                 at = (yp * nine + q) * 2 * pairs
                 block = (result[at : at + 2 * pairs, :] * scale).astype(jnp.bfloat16)
-                outv[slot, 2 * yp : 2 * yp + 2, :, q, :, :] = block.reshape(2, GROUP, CAP, LAGS)
-        for cp in copies(ch):
-            cp.start()
+                block = block.reshape(2, GROUP, CAP, LAGS)
+                if kind["keep"]:
+                    kept[ys, :, q, :, :] = block
+                else:
+                    outv[slot, ys, :, q, :, :] = block
+            if chunks == 1 and not kind["keep"]:
+                for cp in flush(outv.at[0], base, 0, ys):
+                    cp.start()
+                    started.append(cp)
+        if chunks > 1:
+            for cp in copies(ch):
+                cp.start()
         return total
 
-    if chunks == 1:
-        total = one_chunk(0, total)
-    else:
-        total = lax.fori_loop(0, chunks, one_chunk, total)
-    if last:
+    def finish(total):
         lane = iota(own, nine, 1)
         energy = jnp.zeros((own, nine), jnp.float32)
         for q in range(nine):
             part = jnp.sum(total[:, q * LANE : (q + 1) * LANE], axis=1, keepdims=True)
             energy = jnp.where(lane == q, part, energy)
-        sum_ref[...] = energy / float(owners * LAGS)
+        energy_v[...] = energy / float(owners * LAGS)
+        cp = pltpu.make_async_copy(energy_v, sum_ref, sem.at[3])
+        cp.start()
+        started.append(cp)
+
+    if chunks == 1:
+        total = one_chunk(0, total)
     else:
+        total = lax.fori_loop(0, chunks, one_chunk, total)
+        if kind["last"]:
+            finish(total)
+    if not kind["last"]:
         sum_ref[...] = total
-    for ch in range(max(chunks - 2, 0), chunks):
-        for cp in copies(ch):
-            cp.wait()
-
-
-def correlate(chunk, base, spreads, carried, last, assign, target, masks, lags):
-    rows, partners = spreads
-    owners = target.shape[0]
-    own = assign.shape[0] // owners
-    windows = (rows.shape[1] - 0) // (PLANE + LANE)
+    for cp in before + started:
+        cp.wait()
+    if chunks > 1:
+        for ch in range(chunks - 2, chunks):
+            for cp in copies(ch):
+                cp.wait()
+
+
+def correlate(plan, block, base, spreads, lags, carried, last, owners, windows):
+    own = spreads[3].shape[1]
     nine = COMP * COMP
     stations, pairs = GROUP * own, GROUP * CAP
-    lines = own * nine * pairs + CAP * nine * stations
-    smem = pl.BlockSpec(memory_space=pltpu.SMEM)
     vmem = pl.BlockSpec(memory_space=pltpu.VMEM)
     anywhere = pl.BlockSpec(memory_space=pl.ANY)
     f32, bf16 = jnp.float32, jnp.bfloat16
-    first = carried is None
-    operands = [assign, target, masks, chunk, rows, partners, lags]
-    specs = [smem] * 3 + [vmem] * 4
-    aliases = {}
-    if not first:
-        out_so_far, sums = carried
-        operands += [sums, out_so_far]
-        specs += [vmem, anywhere]
-        aliases = {len(operands) - 1: 0}
-    sum_shape = (own, nine) if last else (own, nine * LANE)
-    chunks = chunk.shape[0] // stations
-    return pl.pallas_call(
-        functools.partial(correlate_kernel, owners, own, windows, base, first, last),
-        out_shape=(
-            jax.ShapeDtypeStruct((own, owners, nine, CAP, LAGS), bf16),
-            jax.ShapeDtypeStruct(sum_shape, f32),
-        ),
+    chunks = block.shape[0] // stations
+    sums, waiting, waiting_base, out_so_far = carried
+    kind = {
+        "last": last,
+        "sums": sums is not None,
+        "waiting": waiting_base,
+        "out_in": out_so_far is not None,
+        "keep": chunks == 1 and not last,
+    }
+    kind["out"] = waiting is not None or out_so_far is not None or not kind["keep"]
+    operands, specs, aliases = [block, *spreads, lags], [vmem] * 6, {}
+    if kind["sums"]:
+        operands.append(sums)
+        specs.append(vmem)
+    if waiting is not None:
+        operands.append(waiting)
+        specs.append(vmem)
+    if kind["out_in"]:
+        aliases = {len(operands): 0}
+        operands.append(out_so_far)
+        specs.append(anywhere)
+    shapes, out_specs = [], []
+    if kind["out"]:
+        shapes.append(jax.ShapeDtypeStruct((own, owners, nine, CAP, LAGS), bf16))
+        out_specs.append(anywhere)
+    if kind["keep"]:
+        shapes.append(jax.ShapeDtypeStruct((own, GROUP, nine, CAP, LAGS), bf16))
+        out_specs.append(vmem)
+    shapes.append(jax.ShapeDtypeStruct((own, nine) if last else (own, nine * LANE), f32))
+    out_specs.append(anywhere if last else vmem)
+    half = CAP * nine * stations
+    results = pl.pallas_call(
+        functools.partial(correlate_kernel, plan, owners, own, windows, base, kind),
+        out_shape=tuple(shapes),
         in_specs=specs,
-        out_specs=(anywhere, vmem),
+        out_specs=tuple(out_specs),
         input_output_aliases=aliases,
         scratch_shapes=[
             pltpu.VMEM((2 * pairs, WIDE), bf16),
-            pltpu.VMEM((CAP * nine * stations, 2 * FREQ), bf16),
-            pltpu.VMEM((CAP * nine * stations, LAGS), f32),
+            pltpu.VMEM((half, 2 * FREQ), bf16),
+            pltpu.VMEM((half, LAGS), f32),
             pltpu.VMEM((own * nine * pairs, 2 * FREQ), bf16),
             pltpu.VMEM((own * nine * pairs, LAGS), f32),
             pltpu.VMEM((2, own, GROUP, nine, CAP, LAGS), bf16),
-            pltpu.SemaphoreType.DMA((2,)),
+            pltpu.VMEM((own, nine), f32),
+            pltpu.SemaphoreType.DMA((4,)),
         ],
-        compiler_params=room(2 * (chunk.size + rows.size + partners.size)),
+        compiler_params=room(2 * (block.size + sum(v.size for v in spreads))),
         cost_estimate=pl.CostEstimate(
-            flops=chunks * 4 * lines * FREQ * LAGS,
-            bytes_accessed=chunks * 2 * lines * LAGS,
+            flops=chunks * 8 * half * FREQ * LAGS,
+            bytes_accessed=chunks * 4 * half * LAGS,
             transcendentals=0,
         ),
         name="correlate",
     )(*operands)
+    results = list(results)
+    out = results.pop(0) if kind["out"] else None
+    kept = results.pop(0) if kind["keep"] else None
+    return results[0], kept, base if kind["keep"] else None, out
 
 
 def steps_of(traces, gaps, assign, target):
     owners = lax.axis_size("pairs")
+    own, windows = gaps.shape
     plan = exchange_plan(owners)
-    masks = jnp.asarray(owner_masks(plan))
     lags = jnp.asarray(lag_table())
 
     def swap(block, masks_of):
@@ -502,7 +555,7 @@
 
     steps = [tuple(m) for m in zip(*plan)]
     held = front(traces, gaps)
-    spreads = spread(held, assign, target, masks)
+    spreads = spread(plan, held, assign, target)
     for step in steps[:2]:
         got = swap(held, step)
         held = jnp.concatenate([held, got], 0)
@@ -517,14 +570,14 @@
     order = []
     for block in blocks + other:
         order.append((block, base))
-        base += block.shape[0] // traces.shape[0]
+        base += block.shape[0] // own
     count = len(blocks)
     ranked = [order[i + side * count] for i in range(count) for side in range(2)]
-    carried = None
+    carried = (None, None, None, None)
     for at, (block, start) in enumerate(ranked):
         last = at == len(ranked) - 1
-        carried = correlate(block, start, spreads, carried, last, assign, target, masks, lags)
-    out, energy = carried
+        carried = correlate(plan, block, start, spreads, lags, carried, last, owners, windows)
+    energy, _, _, out = carried
     return out.transpose(0, 1, 3, 2, 4), energy
 
 

time: 30.8 us -> 27.2 us (0.88)
  Pallas kernels: 12.9 us -> 9.39 us
    pallas_call x5, Pallas kernels: 10.6 us -> 7.08 us  [the longest x4 4.88 us: correlate(): pl.pallas_call(functools.partial(correlate_kernel, plan, owners, own, win...]
  transfers between devices with their start and end apart: 5 -> 5, of which waited for: 3 -> 3; matrix products, arithmetic and copies ran while one was open for 0% -> 0% of each run, Pallas kernels for 26% -> 21%
where the time goes in v5:
time: 27.2 us; the launch traced here: 27.1 us
  Pallas kernels  9.39 us (35%)
  waiting for transfers between devices  8.76 us (32%)
  starting transfers between devices  8.02 us (29%)
  between operations  0.73 us (3%)
    ppermute x5, waiting for transfers between devices, swap(): lax.ppermute(block, 'pairs', [(i, i ^ masks_of[i % 2]) for i in range(own...  8.76 us
    ppermute x5, starting transfers between devices, swap(): lax.ppermute(block, 'pairs', [(i, i ^ masks_of[i % 2]) for i in range(own...  8.02 us
    pallas_call x4, Pallas kernels, correlate(): pl.pallas_call(functools.partial(correlate_kernel, plan, owners, own, win...  4.88 us
    pallas_call x1, Pallas kernels, front(): pl.pallas_call(front_kernel, out_shape=jax.ShapeDtypeStruct((own, windows...  2.31 us
    pallas_call x1, Pallas kernels, spread(): pl.pallas_call(functools.partial(spread_kernel, plan, own), out_shape=(ja...  2.2 us
  transfers between devices with their start and end apart: 5, of which 3 were waited for; matrix products, arithmetic and copies ran while one was open for 0% of the time, Pallas kernels for 21%

profile of v5, /device:TPU:0, one launch (start us, length us, event | category | flops | bytes accessed | tf_op | source)
XLA Modules:
  0.0 27.1 jit_solution(11039006821533410116)
XLA Ops:
  0.6 0.0 copy-start
  0.6 0.0 copy-start.2
  0.7 0.0 copy-start.1
  0.7 2.3 %front.1.self_ref = bf16[4,6400]{1,0:T(4,128)(2,1)S(1)} custom-call(s32[2,4]{1,0:T(2,128)} %bitcast.5, bf16[3,4,4096]{2,1,0:T(4,128)(2,1)} %bitcast.4, bf16[3072,256]{1,0:T(8,128)(2,1)} %constant.7.clone.tab_hbm, bf16[512,512]{1,0:T(8,128)(2,1)} %constant.8.clone.band_hbm), custom_call_target="tpu_custom_call" | custom-call | tf_op jit(solution)/shard_map/front/pallas_call | solution.py:169
  3.0 4.1 %collective-permute-start = (bf16[4,6400]{1,0:T(4,128)(2,1)S(1)}, bf16[4,6400]{1,0:T(4,128)(2,1)S(1)}, u32[]{:S(2)}, u32[]{:S(2)}) collective-permute-start(bf16[4,6400]{1,0:T(4,128)(2,1)S(1)} %front.1.self_ref), channel_id=1, source_target_pairs={{0,8},{1,3},{2,10},{3,1},{4,12},{5,7},{6,14},{7,5},{8,0},{9,11},{1... | collective-permute-start | bytes 153608 | tf_op jit(solution)/shard_map/ppermute | solution.py:554
  7.1 2.1 %collective-permute-done = bf16[4,6400]{1,0:T(4,128)(2,1)S(1)} collective-permute-done((bf16[4,6400]{1,0:T(4,128)(2,1)S(1)}, bf16[4,6400]{1,0:T(4,128)(2,1)S(1)}, u32[]{:S(2)}, u32[]{:S(2)}) %collective-permute-start) | collective-permute-done | bytes 51232 | tf_op jit(solution)/shard_map/ppermute | solution.py:554
  9.2 0.1 pad_maximum_fusion.1
  9.3 2.0 %collective-permute-start.1 = (bf16[8,6400]{1,0:T(8,128)(2,1)S(1)}, bf16[8,6400]{1,0:T(8,128)(2,1)S(1)}, u32[]{:S(2)}, u32[]{:S(2)}) collective-permute-start(bf16[8,6400]{1,0:T(8,128)(2,1)S(1)} %pad_maximum_fusion.1), channel_id=1, source_target_pairs={{0,4},{1,9},{2,6},{3,11},{4,0},{5,13},{6,2},{7,15},{8,12},{9,1},{1... | collective-permute-start | bytes 307208 | tf_op jit(solution)/shard_map/ppermute | solution.py:554
  11.2 2.8 %collective-permute-done.1 = bf16[8,6400]{1,0:T(8,128)(2,1)S(1)} collective-permute-done((bf16[8,6400]{1,0:T(8,128)(2,1)S(1)}, bf16[8,6400]{1,0:T(8,128)(2,1)S(1)}, u32[]{:S(2)}, u32[]{:S(2)}) %collective-permute-start.1) | collective-permute-done | bytes 102432 | tf_op jit(solution)/shard_map/ppermute | solution.py:554
  14.0 0.1 pad_maximum_fusion.chunk_ref
  14.1 1.9 %collective-permute-start.2 = (bf16[16,6400]{1,0:T(8,128)(2,1)S(1)}, bf16[16,6400]{1,0:T(8,128)(2,1)S(1)}, u32[]{:S(2)}, u32[]{:S(2)}) collective-permute-start(bf16[16,6400]{1,0:T(8,128)(2,1)S(1)} %pad_maximum_fusion.chunk_ref), channel_id=1, source_target_pairs={{0,2},{1,5},{2,0},{3,7},{4,6},{5,1},{6,4},{7,3},{8,10},{9,13},{10,... | collective-permute-start | bytes 614408 | tf_op jit(solution)/shard_map/ppermute | solution.py:554
  16.0 0.0 collective-permute-start.4
  16.0 3.9 %collective-permute-done.2.chunk_ref = bf16[16,6400]{1,0:T(8,128)(2,1)S(1)} collective-permute-done((bf16[16,6400]{1,0:T(8,128)(2,1)S(1)}, bf16[16,6400]{1,0:T(8,128)(2,1)S(1)}, u32[]{:S(2)}, u32[]{:S(2)}) %collective-permute-start.2) | collective-permute-done | bytes 204832 | tf_op jit(solution)/shard_map/ppermute | solution.py:554
  19.9 0.0 collective-permute-start.3
  19.9 0.0 copy-done.2
  19.9 0.0 copy-done.1
  19.9 2.2 %spread.1 = (bf16[32,6400]{1,0:T(8,128)(2,1)S(1)}, bf16[4,32,6400]{2,1,0:T(8,128)(2,1)S(1)}, bf16[4,16,16]{2,1,0:T(8,128)(2,1)S(1)}, bf16[4,4,32]{2,1,0:T(4,128)(2,1)S(1)}) custom-call(s32[64]{0:T(128)S(1)} %copy-done.1, s32[16]{0:T(128)S(1)} %copy-done.2, bf16[4,6400]{1,0:T(4,128)(2,1)S(1)} %front.1.self_ref), custom_call_target="tpu_custom_call" | custom-call | flops 8192000 | bytes 2048000 | tf_op jit(solution)/shard_map/spread/pallas_call | solution.py:282
  22.1 0.0 copy-done
  22.1 0.8 %correlate.4 = (bf16[4,4,9,2,256]{4,3,2,1,0:T(2,128)(2,1)S(1)}, f32[4,1152]{1,0:T(4,128)S(1)}) custom-call(bf16[16,6400]{1,0:T(8,128)(2,1)S(1)} %pad_maximum_fusion.chunk_ref, bf16[32,6400]{1,0:T(8,128)(2,1)S(1)} %get-tuple-element.16.refs_0_, bf16[4,32,6400]{2,1,0:T(8,128)(2,1)S(1)} %get-tuple-element.17.refs_1_, ...), custom_call_target="tpu_custom_call" | custom-call | flops 301989888 | bytes 294912 | tf_op jit(solution)/shard_map/correlate/pallas_call | solution.py:517
  22.9 0.0 collective-permute-done.4.chunk_ref
  22.9 1.3 %correlate.5 = (bf16[4,16,9,2,256]{4,3,2,1,0:T(2,128)(2,1)}, bf16[4,4,9,2,256]{4,3,2,1,0:T(2,128)(2,1)S(1)}, f32[4,1152]{1,0:T(4,128)S(1)}) custom-call(bf16[16,6400]{1,0:T(8,128)(2,1)S(1)} %collective-permute-done.4.chunk_ref, bf16[32,6400]{1,0:T(8,128)(2,1)S(1)} %get-tuple-element.16.refs_0_, bf16[4,32,6400]{2,1,0:T(8,128)(2,1)S(1)} %get-tuple-element.17.refs_1_, ...), custom_call_target="tpu_custom_call" | custom-call | flops 301989888 | bytes 294912 | tf_op jit(solution)/shard_map/correlate/pallas_call | solution.py:517
  24.2 1.3 %correlate.6 = (bf16[4,16,9,2,256]{4,3,2,1,0:T(2,128)(2,1)}, bf16[4,4,9,2,256]{4,3,2,1,0:T(2,128)(2,1)S(1)}, f32[4,1152]{1,0:T(4,128)S(1)}) custom-call(bf16[16,6400]{1,0:T(8,128)(2,1)S(1)} %collective-permute-done.2.chunk_ref, bf16[32,6400]{1,0:T(8,128)(2,1)S(1)} %get-tuple-element.16.refs_0_, ...), custom_call_target="tpu_custom_call", output_to_operand_aliasing={{0}: (8, {})} | custom-call | flops 301989888 | bytes 294912 | tf_op jit(solution)/shard_map/correlate/pallas_call | solution.py:517
  25.5 0.0 collective-permute-done.3.chunk_ref
  25.5 1.5 %correlate.7 = (bf16[4,16,9,2,256]{4,3,2,1,0:T(2,128)(2,1)}, f32[4,9]{1,0:T(4,128)}) custom-call(bf16[16,6400]{1,0:T(8,128)(2,1)S(1)} %collective-permute-done.3.chunk_ref, bf16[32,6400]{1,0:T(8,128)(2,1)S(1)} %get-tuple-element.16.refs_0_, bf16[4,32,6400]{2,1,0:T(8,128)(2,1)S(1)} %get-tuple-element.17.refs_1_, ...), custom_call_target="tpu_custom_call", output_to_operand_aliasing={{0}: (8, {})} | custom-call | flops 301989888 | bytes 294912 | tf_op jit(solution)/shard_map/correlate/pallas_call | solution.py:517
Async XLA Ops:
  0.6 21.5 %copy-start = (bf16[1024,256]{1,0:T(8,128)(2,1)S(1)}, bf16[1024,256]{1,0:T(8,128)(2,1)}, u32[]{:S(2)}) copy-start(bf16[1024,256]{1,0:T(8,128)(2,1)} %constant.6.clone.refs_4_) | copy-start | bytes 1572868
  0.6 19.3 %copy-start.2 = (s32[16]{0:T(128)S(1)}, s32[16]{0:T(128)}, u32[]{:S(2)}) copy-start(s32[16]{0:T(128)} %target_ref.1) | copy-start | bytes 196
  0.7 19.3 %copy-start.1 = (s32[64]{0:T(128)S(1)}, s32[64]{0:T(128)}, u32[]{:S(2)}) copy-start(s32[64]{0:T(128)} %assign_ref.1) | copy-start | bytes 772
  3.0 6.2 %collective-permute-start = (bf16[4,6400]{1,0:T(4,128)(2,1)S(1)}, bf16[4,6400]{1,0:T(4,128)(2,1)S(1)}, u32[]{:S(2)}, u32[]{:S(2)}) collective-permute-start(bf16[4,6400]{1,0:T(4,128)(2,1)S(1)} %front.1.self_ref), channel_id=1, source_target_pairs={{0,8},{1,3},{2,10},{3,1},{4,12},{5,7},{6,14},{7,5},{8,0},{9,11},{1... | collective-permute-start | bytes 153608 | tf_op jit(solution)/shard_map/ppermute | solution.py:554
  9.3 4.7 %collective-permute-start.1 = (bf16[8,6400]{1,0:T(8,128)(2,1)S(1)}, bf16[8,6400]{1,0:T(8,128)(2,1)S(1)}, u32[]{:S(2)}, u32[]{:S(2)}) collective-permute-start(bf16[8,6400]{1,0:T(8,128)(2,1)S(1)} %pad_maximum_fusion.1), channel_id=1, source_target_pairs={{0,4},{1,9},{2,6},{3,11},{4,0},{5,13},{6,2},{7,15},{8,12},{9,1},{1... | collective-permute-start | bytes 307208 | tf_op jit(solution)/shard_map/ppermute | solution.py:554
  14.1 5.8 %collective-permute-start.2 = (bf16[16,6400]{1,0:T(8,128)(2,1)S(1)}, bf16[16,6400]{1,0:T(8,128)(2,1)S(1)}, u32[]{:S(2)}, u32[]{:S(2)}) collective-permute-start(bf16[16,6400]{1,0:T(8,128)(2,1)S(1)} %pad_maximum_fusion.chunk_ref), channel_id=1, source_target_pairs={{0,2},{1,5},{2,0},{3,7},{4,6},{5,1},{6,4},{7,3},{8,10},{9,13},{10,... | collective-permute-start | bytes 614408 | tf_op jit(solution)/shard_map/ppermute | solution.py:554
  16.0 6.9 %collective-permute-start.4 = (bf16[16,6400]{1,0:T(8,128)(2,1)S(1)}, bf16[16,6400]{1,0:T(8,128)(2,1)S(1)}, u32[]{:S(2)}, u32[]{:S(2)}) collective-permute-start(bf16[16,6400]{1,0:T(8,128)(2,1)S(1)} %pad_maximum_fusion.chunk_ref), channel_id=1, source_target_pairs={{0,1},{1,0},{2,3},{3,2},{4,5},{5,4},{6,7},{7,6},{8,9},{9,8},{10,11... | collective-permute-start | bytes 614408 | tf_op jit(solution)/shard_map/ppermute | solution.py:554
  19.9 5.6 %collective-permute-start.3 = (bf16[16,6400]{1,0:T(8,128)(2,1)S(1)}, bf16[16,6400]{1,0:T(8,128)(2,1)S(1)}, u32[]{:S(2)}, u32[]{:S(2)}) collective-permute-start(bf16[16,6400]{1,0:T(8,128)(2,1)S(1)} %collective-permute-done.2.chunk_ref), channel_id=1, source_target_pairs={{0,1},{1,0},{2,3},{3,2},{4,5},{5,4},{6,7},{7,6},{8,9},{9,8},{10,11... | collective-permute-start | bytes 614408 | tf_op jit(solution)/shard_map/ppermute | solution.py:554

commit v6 on v5

--- a/solution.py
+++ b/solution.py
@@ -65,7 +65,80 @@
     return jnp.dot(a, b, preferred_element_type=jnp.float32)
 
 
-def front_kernel(gaps_hbm, x_hbm, tab_hbm, band_hbm, out_ref, gaps_ref, x_ref, tab_ref, band_ref, sem):
+def exchange_plan(count):
+    bits = int(count).bit_length() - 1
+    assert count == 1 << bits and bits >= 4
+    chips = [1 << b for b in range(bits - 1, 0, -1)]
+    return chips[:1] + chips[-1:] + chips[1:-1]
+
+
+def owner_at(plan, me, place):
+    mask = place >> len(plan)
+    for i, m in enumerate(plan):
+        mask = mask ^ (m * ((place >> i) & 1))
+    return me ^ mask
+
+
+def room(operand_bytes):
+    return pltpu.CompilerParams(vmem_limit_bytes=(8 << 20) + operand_bytes)
+
+
+def first_two(flags):
+    found = [jnp.int32(NONE)] * CAP
+    seen = jnp.int32(0)
+    for s, flag in enumerate(flags):
+        for c in range(CAP):
+            found[c] = jnp.where(jnp.logical_and(flag, seen == c), s, found[c])
+        seen = seen + flag.astype(jnp.int32)
+    return found
+
+
+def iota(rows, cols, dim):
+    return lax.broadcasted_iota(jnp.int32, (rows, cols), dim)
+
+
+def one_hot(want, cols):
+    return jnp.where(iota(want.shape[0], cols, 1) == want, 1.0, 0.0).astype(jnp.bfloat16)
+
+
+def meet(plan, own, assign_ref, target_ref, pick_ref, mine_ref, weight_ref):
+    me = lax.axis_index("pairs")
+    pairs = GROUP * CAP
+    stations = GROUP * own
+    place = iota(CAP * stations, own, 0)
+    place = (place // stations) * GROUP + (place % stations) // own
+    slot = iota(2 * pairs, stations, 0) % pairs
+    col = iota(own, CAP * stations, 1)
+    col = (col // stations) * GROUP + (col % stations) // own
+    y_row = iota(own, CAP * stations, 0)
+    my_target = target_ref[me]
+
+    def one_group(ch, carry):
+        want = jnp.full(place.shape, NONE, jnp.int32)
+        taken = jnp.full(slot.shape, NONE, jnp.int32)
+        weight = jnp.zeros(col.shape, jnp.float32)
+        for j in range(GROUP):
+            owner = owner_at(plan, me, ch * GROUP + j)
+            wanted = target_ref[owner]
+            mine = first_two([assign_ref[me * own + s] == wanted for s in range(own)])
+            theirs = first_two([assign_ref[owner * own + s] == my_target for s in range(own)])
+            for c in range(CAP):
+                want = jnp.where(place == c * GROUP + j, mine[c], want)
+                hit = jnp.logical_and(col == c * GROUP + j, y_row == mine[c])
+                weight = jnp.where(hit, 1.0, weight)
+                taken = jnp.where(slot == j * CAP + c, theirs[c] + j * own, taken)
+        mine_ref[ch] = one_hot(want, own)
+        pick_ref[ch] = one_hot(taken, stations)
+        weight_ref[ch] = weight.astype(jnp.bfloat16)
+        return carry
+
+    lax.fori_loop(0, pick_ref.shape[0], one_group, 0)
+
+
+def front_kernel(
+    plan, gaps_hbm, assign_hbm, target_hbm, x_hbm, tab_hbm, band_hbm, out_ref, pick_ref, mine_ref,
+    weight_ref, gaps_ref, assign_ref, target_ref, x_ref, tab_ref, band_ref, sem,
+):
     windows, own = gaps_ref.shape
     rows = windows * own
     parts = tab_ref.shape[0] // PART
@@ -82,8 +155,15 @@
         pltpu.make_async_copy(band_hbm, band_ref, sem.at[1 + parts]),
         pltpu.make_async_copy(gaps_hbm, gaps_ref, sem.at[2 + parts]),
     ]
-    for load in loads:
+    names = [
+        pltpu.make_async_copy(assign_hbm, assign_ref, sem.at[3 + parts]),
+        pltpu.make_async_copy(target_hbm, target_ref, sem.at[4 + parts]),
+    ]
+    for load in names + loads:
         load.start()
+    for load in names:
+        load.wait()
+    meet(plan, own, assign_ref, target_ref, pick_ref, mine_ref, weight_ref)
     loads[0].wait()
     quarter = []
     for j in range(RADIX):
@@ -158,157 +238,52 @@
         out_ref[:, start : start + LANE] = flags[w * own : (w + 1) * own].astype(jnp.bfloat16)
 
 
-def front(traces, gaps):
+def front(plan, traces, gaps, assign, target):
     own, comps, length = traces.shape
     windows = gaps.shape[1]
     assert comps == COMP and length == windows * SEG
     table, band = dft_table(), band_table()
-    operands = (gaps.T, traces.transpose(1, 0, 2), jnp.asarray(table), jnp.asarray(band))
+    operands = (gaps.T, assign, target, traces.transpose(1, 0, 2), jnp.asarray(table), jnp.asarray(band))
     hbm = pl.BlockSpec(memory_space=pltpu.HBM)
+    vmem = pl.BlockSpec(memory_space=pltpu.VMEM)
     bf16 = jnp.bfloat16
+    groups, stations = target.shape[0] // GROUP, GROUP * own
     return pl.pallas_call(
-        front_kernel,
-        out_shape=jax.ShapeDtypeStruct((own, windows * (PLANE + LANE)), bf16),
-        in_specs=[hbm] * 4,
-        out_specs=pl.BlockSpec(memory_space=pltpu.VMEM),
+        functools.partial(front_kernel, plan),
+        out_shape=(
+            jax.ShapeDtypeStruct((own, windows * (PLANE + LANE)), bf16),
+            jax.ShapeDtypeStruct((groups, 2 * GROUP * CAP, stations), bf16),
+            jax.ShapeDtypeStruct((groups, CAP * stations, own), bf16),
+            jax.ShapeDtypeStruct((groups, own, CAP * stations), bf16),
+        ),
+        in_specs=[hbm] * 6,
+        out_specs=(vmem,) * 4,
         scratch_shapes=[
             pltpu.SMEM((windows, own), jnp.int32),
+            pltpu.SMEM(assign.shape, jnp.int32),
+            pltpu.SMEM(target.shape, jnp.int32),
             pltpu.VMEM((comps, own, length), bf16),
             pltpu.VMEM(table.shape, bf16),
             pltpu.VMEM(band.shape, bf16),
-            pltpu.SemaphoreType.DMA((3 + table.shape[0] // PART,)),
+            pltpu.SemaphoreType.DMA((5 + table.shape[0] // PART,)),
         ],
         compiler_params=room(0),
         name="front",
     )(*[pltpu.with_memory_space_constraint(v, pltpu.HBM) for v in operands])
 
 
-def exchange_plan(count):
-    bits = int(count).bit_length() - 1
-    assert count == 1 << bits and bits >= 3
-    chips = [1 << b for b in range(bits - 1, 0, -1)]
-    return [chips, chips[-1:] + chips[:-1]]
-
-
-def owner_at(plan, me, place):
-    parity = lax.rem(me, 2)
-    bits = len(plan[0])
-    if isinstance(place, int):
-        found = []
-        for p in range(2):
-            far = place >> bits
-            mask = far
-            for i, m in enumerate(plan[p ^ far]):
-                mask ^= m * ((place >> i) & 1)
-            found.append(mask)
-        return me ^ jnp.where(parity == 0, found[0], found[1])
-    far = place >> bits
-    side = parity ^ far
-    mask = far
-    for i in range(bits):
-        step = jnp.where(side == 0, plan[0][i], plan[1][i])
-        mask = mask ^ (step * ((place >> i) & 1))
-    return me ^ mask
-
-
-def room(operand_bytes):
-    return pltpu.CompilerParams(vmem_limit_bytes=(8 << 20) + operand_bytes)
-
-
-def first_two(flags):
-    found = [jnp.int32(NONE)] * CAP
-    seen = jnp.int32(0)
-    for s, flag in enumerate(flags):
-        for c in range(CAP):
-            found[c] = jnp.where(jnp.logical_and(flag, seen == c), s, found[c])
-        seen = seen + flag.astype(jnp.int32)
-    return found
-
-
-def iota(rows, cols, dim):
-    return lax.broadcasted_iota(jnp.int32, (rows, cols), dim)
-
-
-def one_hot(want, cols):
-    return jnp.where(iota(want.shape[0], cols, 1) == want, 1.0, 0.0).astype(jnp.bfloat16)
-
-
-def spread_kernel(plan, own, assign_ref, target_ref, self_ref, rows_ref, partner_ref, pick_ref, weight_ref):
-    me = lax.axis_index("pairs")
-    pairs = GROUP * CAP
-    stations = GROUP * own
-    mine_rows = self_ref[...]
-    rows_ref[...] = mm(one_hot(iota(own * pairs, own, 0) // pairs, own), mine_rows).astype(
-        jnp.bfloat16
-    )
-    place = iota(CAP * stations, own, 0)
-    place = (place // stations) * GROUP + (place % stations) // own
-    slot = iota(2 * pairs, stations, 0) % pairs
-    col = iota(own, CAP * stations, 1)
-    col = (col // stations) * GROUP + (col % stations) // own
-    y_row = iota(own, CAP * stations, 0)
-    my_target = target_ref[me]
-
-    def one_chunk(ch, carry):
-        want = jnp.full(place.shape, NONE, jnp.int32)
-        taken = jnp.full(slot.shape, NONE, jnp.int32)
-        weight = jnp.zeros(col.shape, jnp.float32)
-        for j in range(GROUP):
-            owner = owner_at(plan, me, ch * GROUP + j)
-            wanted = target_ref[owner]
-            mine = first_two([assign_ref[me * own + s] == wanted for s in range(own)])
-            theirs = first_two([assign_ref[owner * own + s] == my_target for s in range(own)])
-            for c in range(CAP):
-                want = jnp.where(place == c * GROUP + j, mine[c], want)
-                hit = jnp.logical_and(col == c * GROUP + j, y_row == mine[c])
-                weight = jnp.where(hit, 1.0, weight)
-                taken = jnp.where(slot == j * CAP + c, theirs[c] + j * own, taken)
-        partner_ref[ch] = mm(one_hot(want, own), mine_rows).astype(jnp.bfloat16)
-        pick_ref[ch] = one_hot(taken, stations)
-        weight_ref[ch] = weight.astype(jnp.bfloat16)
-        return carry
-
-    lax.fori_loop(0, partner_ref.shape[0], one_chunk, 0)
-
-
-def spread(plan, held, assign, target):
-    own = held.shape[0]
-    chunks = target.shape[0] // GROUP
-    stations, pairs = GROUP * own, GROUP * CAP
-    smem = pl.BlockSpec(memory_space=pltpu.SMEM)
-    vmem = pl.BlockSpec(memory_space=pltpu.VMEM)
-    made = own * pairs + chunks * CAP * stations
-    bf16 = jnp.bfloat16
-    return pl.pallas_call(
-        functools.partial(spread_kernel, plan, own),
-        out_shape=(
-            jax.ShapeDtypeStruct((own * pairs, WIDE), bf16),
-            jax.ShapeDtypeStruct((chunks, CAP * stations, WIDE), bf16),
-            jax.ShapeDtypeStruct((chunks, 2 * pairs, stations), bf16),
-            jax.ShapeDtypeStruct((chunks, own, CAP * stations), bf16),
-        ),
-        in_specs=[smem] * 2 + [vmem],
-        out_specs=(vmem,) * 4,
-        compiler_params=room(2 * made * WIDE),
-        cost_estimate=pl.CostEstimate(
-            flops=2 * made * own * WIDE, bytes_accessed=2 * made * WIDE, transcendentals=0
-        ),
-        name="spread",
-    )(assign, target, held)
-
-
 def correlate_kernel(plan, owners, own, windows, base, kind, chunk_ref, *refs):
     refs = list(refs)
-    rows_ref, partner_ref, pick_ref, weight_ref, lag_ref = refs[:5]
+    self_ref, pick_ref, mine_ref, weight_ref, lag_ref = refs[:5]
     refs = refs[5:]
     sum_in = refs.pop(0) if kind["sums"] else None
-    waiting = refs.pop(0) if kind["waiting"] is not None else None
+    waiting = [(refs.pop(0), place) for place in kind["waiting"]]
     if kind["out_in"]:
         refs.pop(0)
     out_ref = refs.pop(0) if kind["out"] else None
     kept = refs.pop(0) if kind["keep"] else None
     sum_ref = refs.pop(0)
-    picked, cross_e, result_e, cross, result, outv, energy_v, sem = refs
+    rows_ref, picked, cross_e, result_e, cross, result, outv, energy_v, sem = refs
     me = lax.axis_index("pairs")
     pairs = GROUP * CAP
     stations = GROUP * own
@@ -327,7 +302,7 @@
     def copies(ch):
         return flush(outv.at[lax.rem(ch, 2)], base + ch * GROUP, lax.rem(ch, 2))
 
-    before = [] if waiting is None else flush(waiting, kind["waiting"], 2)
+    before = [cp for source, place in waiting for cp in flush(source, place, 2)]
     for cp in before:
         cp.start()
     started = []
@@ -337,6 +312,9 @@
         first_row = ch * stations if isinstance(ch, int) else pl.multiple_of(ch * stations, stations)
         here = pl.ds(first_row, stations)
         number = base // GROUP + ch
+        each = one_hot(iota(own * pairs, own, 0) // pairs, own)
+        spread = jnp.concatenate([each, mine_ref[number]], 0)
+        rows_ref[...] = mm(spread, self_ref[...]).astype(jnp.bfloat16)
         picked[...] = mm(pick_ref[number], chunk_ref[here, :]).astype(jnp.bfloat16)
 
         def product(left, right):
@@ -359,7 +337,7 @@
             return got
 
         def partner(rows, lanes):
-            return partner_ref[number, rows, lanes]
+            return rows_ref[own * pairs + rows.start : own * pairs + rows.stop, lanes]
 
         tiles = FREQ // TILE
 
@@ -476,39 +454,42 @@
                 cp.wait()
 
 
-def correlate(plan, block, base, spreads, lags, carried, last, owners, windows):
-    own = spreads[3].shape[1]
+def correlate(plan, block, base, held, names, lags, carried, last, owners, windows):
+    own = held.shape[0]
     nine = COMP * COMP
     stations, pairs = GROUP * own, GROUP * CAP
     vmem = pl.BlockSpec(memory_space=pltpu.VMEM)
     anywhere = pl.BlockSpec(memory_space=pl.ANY)
     f32, bf16 = jnp.float32, jnp.bfloat16
     chunks = block.shape[0] // stations
-    sums, waiting, waiting_base, out_so_far = carried
+    sums, waiting, out_so_far = carried
+    keep = chunks == 1 and not last
     kind = {
         "last": last,
         "sums": sums is not None,
-        "waiting": waiting_base,
-        "out_in": out_so_far is not None,
-        "keep": chunks == 1 and not last,
+        "waiting": [] if keep else [place for _, place in waiting],
+        "out_in": out_so_far is not None and not keep,
+        "keep": keep,
+        "out": not keep,
     }
-    kind["out"] = waiting is not None or out_so_far is not None or not kind["keep"]
-    operands, specs, aliases = [block, *spreads, lags], [vmem] * 6, {}
+    operands, aliases = [block, held, *names, lags], {}
+    specs = [vmem] * len(operands)
     if kind["sums"]:
         operands.append(sums)
         specs.append(vmem)
-    if waiting is not None:
-        operands.append(waiting)
-        specs.append(vmem)
-    if kind["out_in"]:
-        aliases = {len(operands): 0}
-        operands.append(out_so_far)
-        specs.append(anywhere)
+    if not keep:
+        for source, _ in waiting:
+            operands.append(source)
+            specs.append(vmem)
+        if out_so_far is not None:
+            aliases = {len(operands): 0}
+            operands.append(out_so_far)
+            specs.append(anywhere)
     shapes, out_specs = [], []
     if kind["out"]:
         shapes.append(jax.ShapeDtypeStruct((own, owners, nine, CAP, LAGS), bf16))
         out_specs.append(anywhere)
-    if kind["keep"]:
+    if keep:
         shapes.append(jax.ShapeDtypeStruct((own, GROUP, nine, CAP, LAGS), bf16))
         out_specs.append(vmem)
     shapes.append(jax.ShapeDtypeStruct((own, nine) if last else (own, nine * LANE), f32))
@@ -521,6 +502,7 @@
         out_specs=tuple(out_specs),
         input_output_aliases=aliases,
         scratch_shapes=[
+            pltpu.VMEM((own * pairs + CAP * stations, WIDE), bf16),
             pltpu.VMEM((2 * pairs, WIDE), bf16),
             pltpu.VMEM((half, 2 * FREQ), bf16),
             pltpu.VMEM((half, LAGS), f32),
@@ -530,7 +512,7 @@
             pltpu.VMEM((own, nine), f32),
             pltpu.SemaphoreType.DMA((4,)),
         ],
-        compiler_params=room(2 * (block.size + sum(v.size for v in spreads))),
+        compiler_params=room(2 * sum(v.size for v in operands[:-1])),
         cost_estimate=pl.CostEstimate(
             flops=chunks * 8 * half * FREQ * LAGS,
             bytes_accessed=chunks * 4 * half * LAGS,
@@ -538,10 +520,11 @@
         ),
         name="correlate",
     )(*operands)
-    results = list(results)
-    out = results.pop(0) if kind["out"] else None
-    kept = results.pop(0) if kind["keep"] else None
-    return results[0], kept, base if kind["keep"] else None, out
+    if keep:
+        kept, sums = results
+        return sums, waiting + [(kept, base)], out_so_far
+    out, sums = results
+    return sums, [], out
 
 
 def steps_of(traces, gaps, assign, target):
@@ -550,22 +533,31 @@
     plan = exchange_plan(owners)
     lags = jnp.asarray(lag_table())
 
-    def swap(block, masks_of):
-        return lax.ppermute(block, "pairs", [(i, i ^ masks_of[i % 2]) for i in range(owners)])
-
-    steps = [tuple(m) for m in zip(*plan)]
-    held = front(traces, gaps)
-    spreads = spread(plan, held, assign, target)
-    for step in steps[:2]:
-        got = swap(held, step)
-        held = jnp.concatenate([held, got], 0)
-    blocks = [held]
-    for step in steps[2:]:
-        sent = jnp.concatenate(blocks, 0) if len(blocks) > 1 else held
-        blocks.append(swap(sent, step))
-    other = []
-    for block in blocks:
-        other.append(swap(block, (1, 1)))
+    def swap(block, mask):
+        return lax.ppermute(block, "pairs", [(i, i ^ mask) for i in range(owners)])
+
+    def join(*parts):
+        return jnp.concatenate(parts, 0)
+
+    held, *names = front(plan, traces, gaps, assign, target)
+    wide, near, third = plan[:3]
+    a = swap(held, wide)
+    b0 = swap(held, near)
+    b1 = swap(a, near)
+    c0 = swap(join(held, a), third)
+    c1 = swap(b0, third)
+    c2 = swap(b1, third)
+    blocks = [join(held, a, b0, b1)]
+    other = [swap(blocks[0], 1)]
+    if len(plan) > 3:
+        blocks.append(join(c0, c1, c2))
+        for mask in plan[3:]:
+            blocks.append(swap(join(*blocks), mask))
+        other += [swap(block, 1) for block in blocks[1:]]
+    else:
+        blocks.append(join(c0, c1, c2))
+        far = [swap(c, 1) for c in (c0, c1, c2)]
+        other.append(join(*far))
     base = 0
     order = []
     for block in blocks + other:
@@ -573,11 +565,11 @@
         base += block.shape[0] // own
     count = len(blocks)
     ranked = [order[i + side * count] for i in range(count) for side in range(2)]
-    carried = (None, None, None, None)
+    carried = (None, [], None)
     for at, (block, start) in enumerate(ranked):
         last = at == len(ranked) - 1
-        carried = correlate(plan, block, start, spreads, lags, carried, last, owners, windows)
-    energy, _, _, out = carried
+        carried = correlate(plan, block, start, held, names, lags, carried, last, owners, windows)
+    energy, _, out = carried
     return out.transpose(0, 1, 3, 2, 4), energy
 
 

time: 27.2 us -> 24.1 us (0.89)
  waiting for transfers between devices: 8.76 us -> 4.05 us
  starting transfers between devices: 8.02 us -> 11.5 us
  Pallas kernels: 9.39 us -> 7.38 us
    ppermute x5 -> x10, waiting for transfers between devices: 8.76 us -> 4.05 us  [swap(): return lax.ppermute(block, 'pairs', [(i, i ^ mask) for i in range(owners)])]
    ppermute x5 -> x10, starting transfers between devices: 8.02 us -> 11.5 us  [swap(): return lax.ppermute(block, 'pairs', [(i, i ^ mask) for i in range(owners)])]
    pallas_call x2 -> x1, Pallas kernels: 4.52 us -> 2.57 us  [front(): pl.pallas_call(functools.partial(front_kernel, plan), out_shape=(jax.Shap...]
  transfers between devices with their start and end apart: 5 -> 10, of which waited for: 3 -> 6; matrix products, arithmetic and copies ran while one was open for 0% -> 1% of each run, Pallas kernels for 21% -> 4%
where the time goes in v6:
time: 24.1 us; the launch traced here: 23.9 us
  starting transfers between devices  11.5 us (48%)
  Pallas kernels  7.38 us (31%)
  waiting for transfers between devices  4.05 us (17%)
  between operations  0.71 us (3%)
  other arithmetic  0.29 us (1%)
    ppermute x10, starting transfers between devices, swap(): return lax.ppermute(block, 'pairs', [(i, i ^ mask) for i in range(owners)])  11.5 us
    pallas_call x4, Pallas kernels, correlate(): pl.pallas_call(functools.partial(correlate_kernel, plan, owners, own, win...  4.82 us
    ppermute x10, waiting for transfers between devices, swap(): return lax.ppermute(block, 'pairs', [(i, i ^ mask) for i in range(owners)])  4.05 us
    pallas_call x1, Pallas kernels, front(): pl.pallas_call(functools.partial(front_kernel, plan), out_shape=(jax.Shap...  2.57 us
  transfers between devices with their start and end apart: 10, of which 6 were waited for; matrix products, arithmetic and copies ran while one was open for 1% of the time, Pallas kernels for 4%

profile of v6, /device:TPU:0, one launch (start us, length us, event | category | flops | bytes accessed | tf_op | source)
XLA Modules:
  0.0 23.9 jit_solution(7985349619887207053)
XLA Ops:
  0.6 0.0 copy-start
  0.6 2.6 %front.1 = (bf16[4,6400]{1,0:T(4,128)(2,1)S(1)}, bf16[4,16,16]{2,1,0:T(8,128)(2,1)S(1)}, bf16[4,32,4]{2,1,0:T(8,128)(2,1)S(1)}, bf16[4,4,32]{2,1,0:T(4,128)(2,1)S(1)}) custom-call(s32[2,4]{1,0:T(2,128)} %bitcast.4, s32[64]{0:T(128)} %assign_hbm.1, s32[16]{0:T(128)} %target_hbm.1, bf16[3,4,4096]{2,1,0:T(4,128)(2,1)} %bitcast.3, ...), custom_call_target="tpu_custom_call" | custom-call | tf_op jit(solution)/shard_map/front/pallas_call | solution.py:251
  3.2 4.1 %collective-permute-start = (bf16[4,6400]{1,0:T(4,128)(2,1)S(1)}, bf16[4,6400]{1,0:T(4,128)(2,1)S(1)}, u32[]{:S(2)}, u32[]{:S(2)}) collective-permute-start(bf16[4,6400]{1,0:T(4,128)(2,1)S(1)} %get-tuple-element.14.refs_0_), channel_id=1, source_target_pairs={{0,8},{1,9},{2,10},{3,11},{4,12},{5,13},{6,14},{7,15},{8,0},{9,1},... | collective-permute-start | bytes 153608 | tf_op jit(solution)/shard_map/ppermute | solution.py:537
  7.3 1.5 %collective-permute-start.3 = (bf16[4,6400]{1,0:T(4,128)(2,1)S(1)}, bf16[4,6400]{1,0:T(4,128)(2,1)S(1)}, u32[]{:S(2)}, u32[]{:S(2)}) collective-permute-start(bf16[4,6400]{1,0:T(4,128)(2,1)S(1)} %get-tuple-element.14.refs_0_), channel_id=1, source_target_pairs={{0,2},{1,3},{2,0},{3,1},{4,6},{5,7},{6,4},{7,5},{8,10},{9,11},{10,... | collective-permute-start | bytes 153608 | tf_op jit(solution)/shard_map/ppermute | solution.py:537
  8.9 1.1 %collective-permute-done = bf16[4,6400]{1,0:T(4,128)(2,1)S(1)} collective-permute-done((bf16[4,6400]{1,0:T(4,128)(2,1)S(1)}, bf16[4,6400]{1,0:T(4,128)(2,1)S(1)}, u32[]{:S(2)}, u32[]{:S(2)}) %collective-permute-start) | collective-permute-done | bytes 51232 | tf_op jit(solution)/shard_map/ppermute | solution.py:537
  10.0 1.7 %collective-permute-start.6 = (bf16[4,6400]{1,0:T(4,128)(2,1)S(1)}, bf16[4,6400]{1,0:T(4,128)(2,1)S(1)}, u32[]{:S(2)}, u32[]{:S(2)}) collective-permute-start(bf16[4,6400]{1,0:T(4,128)(2,1)S(1)} %collective-permute-done), channel_id=1, source_target_pairs={{0,2},{1,3},{2,0},{3,1},{4,6},{5,7},{6,4},{7,5},{8,10},{9,11},{10,... | collective-permute-start | bytes 153608 | tf_op jit(solution)/shard_map/ppermute | solution.py:537
  11.7 0.1 pad_maximum_fusion.3
  11.8 1.2 %collective-permute-start.1 = (bf16[8,6400]{1,0:T(8,128)(2,1)S(1)}, bf16[8,6400]{1,0:T(8,128)(2,1)S(1)}, u32[]{:S(2)}, u32[]{:S(2)}) collective-permute-start(bf16[8,6400]{1,0:T(8,128)(2,1)S(1)} %pad_maximum_fusion.3), channel_id=1, source_target_pairs={{0,4},{1,5},{2,6},{3,7},{4,0},{5,1},{6,2},{7,3},{8,12},{9,13},{10,... | collective-permute-start | bytes 307208 | tf_op jit(solution)/shard_map/ppermute | solution.py:537
  13.0 0.0 collective-permute-done.3
  13.0 0.9 %collective-permute-start.4 = (bf16[4,6400]{1,0:T(4,128)(2,1)S(1)}, bf16[4,6400]{1,0:T(4,128)(2,1)S(1)}, u32[]{:S(2)}, u32[]{:S(2)}) collective-permute-start(bf16[4,6400]{1,0:T(4,128)(2,1)S(1)} %collective-permute-done.3), channel_id=1, source_target_pairs={{0,4},{1,5},{2,6},{3,7},{4,0},{5,1},{6,2},{7,3},{8,12},{9,13},{10,... | collective-permute-start | bytes 153608 | tf_op jit(solution)/shard_map/ppermute | solution.py:537
  13.9 0.2 collective-permute-done.6
  14.1 1.4 %collective-permute-start.7 = (bf16[4,6400]{1,0:T(4,128)(2,1)S(1)}, bf16[4,6400]{1,0:T(4,128)(2,1)S(1)}, u32[]{:S(2)}, u32[]{:S(2)}) collective-permute-start(bf16[4,6400]{1,0:T(4,128)(2,1)S(1)} %collective-permute-done.6), channel_id=1, source_target_pairs={{0,4},{1,5},{2,6},{3,7},{4,0},{5,1},{6,2},{7,3},{8,12},{9,13},{10,... | collective-permute-start | bytes 153608 | tf_op jit(solution)/shard_map/ppermute | solution.py:537
  15.5 0.1 pad_maximum_fusion.2.chunk_ref
  15.6 0.1 collective-permute-start.9
  15.7 1.4 %collective-permute-done.4 = bf16[4,6400]{1,0:T(4,128)(2,1)S(1)} collective-permute-done((bf16[4,6400]{1,0:T(4,128)(2,1)S(1)}, bf16[4,6400]{1,0:T(4,128)(2,1)S(1)}, u32[]{:S(2)}, u32[]{:S(2)}) %collective-permute-start.4) | collective-permute-done | bytes 51232 | tf_op jit(solution)/shard_map/ppermute | solution.py:537
  17.1 0.0 collective-permute-start.5
  17.1 0.0 copy-done
  17.1 1.0 %correlate.4 = (bf16[4,4,9,2,256]{4,3,2,1,0:T(2,128)(2,1)S(1)}, f32[4,1152]{1,0:T(4,128)S(1)}) custom-call(bf16[16,6400]{1,0:T(8,128)(2,1)S(1)} %pad_maximum_fusion.2.chunk_ref, bf16[4,6400]{1,0:T(4,128)(2,1)S(1)} %get-tuple-element.14.refs_0_, bf16[4,16,16]{2,1,0:T(8,128)(2,1)S(1)} %get-tuple-element.15.refs_1_, ...), custom_call_target="tpu_custom_call" | custom-call | flops 301989888 | bytes 294912 | tf_op jit(solution)/shard_map/correlate/pallas_call | solution.py:498
  18.1 0.1 collective-permute-done.7
  18.2 0.5 %collective-permute-start.8 = (bf16[4,6400]{1,0:T(4,128)(2,1)S(1)}, bf16[4,6400]{1,0:T(4,128)(2,1)S(1)}, u32[]{:S(2)}, u32[]{:S(2)}) collective-permute-start(bf16[4,6400]{1,0:T(4,128)(2,1)S(1)} %collective-permute-done.7), channel_id=1, source_target_pairs={{0,1},{1,0},{2,3},{3,2},{4,5},{5,4},{6,7},{7,6},{8,9},{9,8},{10,11... | collective-permute-start | bytes 153608 | tf_op jit(solution)/shard_map/ppermute | solution.py:537
  18.7 0.0 collective-permute-done.1
  18.7 0.1 collective-permute-start.2
  18.8 0.1 pad_maximum_fusion.1.chunk_ref
  18.8 0.0 collective-permute-done.5
  18.9 0.7 %collective-permute-done.8 = bf16[4,6400]{1,0:T(4,128)(2,1)S(1)} collective-permute-done((bf16[4,6400]{1,0:T(4,128)(2,1)S(1)}, bf16[4,6400]{1,0:T(4,128)(2,1)S(1)}, u32[]{:S(2)}, u32[]{:S(2)}) %collective-permute-start.8) | collective-permute-done | bytes 51232 | tf_op jit(solution)/shard_map/ppermute | solution.py:537
  19.6 0.4 %collective-permute-done.2 = bf16[8,6400]{1,0:T(8,128)(2,1)S(1)} collective-permute-done((bf16[8,6400]{1,0:T(8,128)(2,1)S(1)}, bf16[8,6400]{1,0:T(8,128)(2,1)S(1)}, u32[]{:S(2)}, u32[]{:S(2)}) %collective-permute-start.2) | collective-permute-done | bytes 102432 | tf_op jit(solution)/shard_map/ppermute | solution.py:537
  20.0 0.1 pad_maximum_fusion.chunk_ref
  20.1 0.0 collective-permute-done.9.chunk_ref
  20.1 1.0 %correlate.5 = (bf16[4,4,9,2,256]{4,3,2,1,0:T(2,128)(2,1)S(1)}, f32[4,1152]{1,0:T(4,128)S(1)}) custom-call(bf16[16,6400]{1,0:T(8,128)(2,1)S(1)} %collective-permute-done.9.chunk_ref, bf16[4,6400]{1,0:T(4,128)(2,1)S(1)} %get-tuple-element.14.refs_0_, bf16[4,16,16]{2,1,0:T(8,128)(2,1)S(1)} %get-tuple-element.15.refs_1_, ...), custom_call_target="tpu_custom_call" | custom-call | flops 301989888 | bytes 294912 | tf_op jit(solution)/shard_map/correlate/pallas_call | solution.py:498
  21.1 1.0 %correlate.6 = (bf16[4,4,9,2,256]{4,3,2,1,0:T(2,128)(2,1)S(1)}, f32[4,1152]{1,0:T(4,128)S(1)}) custom-call(bf16[16,6400]{1,0:T(8,128)(2,1)S(1)} %pad_maximum_fusion.1.chunk_ref, bf16[4,6400]{1,0:T(4,128)(2,1)S(1)} %get-tuple-element.14.refs_0_, bf16[4,16,16]{2,1,0:T(8,128)(2,1)S(1)} %get-tuple-element.15.refs_1_, ...), custom_call_target="tpu_custom_call" | custom-call | flops 301989888 | bytes 294912 | tf_op jit(solution)/shard_map/correlate/pallas_call | solution.py:498
  22.1 1.8 %correlate.7 = (bf16[4,16,9,2,256]{4,3,2,1,0:T(2,128)(2,1)}, f32[4,9]{1,0:T(4,128)}) custom-call(bf16[16,6400]{1,0:T(8,128)(2,1)S(1)} %pad_maximum_fusion.chunk_ref, bf16[4,6400]{1,0:T(4,128)(2,1)S(1)} %get-tuple-element.14.refs_0_, bf16[4,16,16]{2,1,0:T(8,128)(2,1)S(1)} %get-tuple-element.15.refs_1_, bf16[4,32,4]{2,1,0:T(8,128)(2,1)S(1)} %get-tuple-element.16.refs_2_, ...), custom_call_target="tpu_custom_call" | custom-call | flops 301989888 | bytes 294912 | tf_op jit(solution)/shard_map/correlate/pallas_call | solution.py:498
Async XLA Ops:
  0.6 16.5 %copy-start = (bf16[1024,256]{1,0:T(8,128)(2,1)S(1)}, bf16[1024,256]{1,0:T(8,128)(2,1)}, u32[]{:S(2)}) copy-start(bf16[1024,256]{1,0:T(8,128)(2,1)} %constant.6.clone.refs_4_) | copy-start | bytes 1572868
  3.2 6.8 %collective-permute-start = (bf16[4,6400]{1,0:T(4,128)(2,1)S(1)}, bf16[4,6400]{1,0:T(4,128)(2,1)S(1)}, u32[]{:S(2)}, u32[]{:S(2)}) collective-permute-start(bf16[4,6400]{1,0:T(4,128)(2,1)S(1)} %get-tuple-element.14.refs_0_), channel_id=1, source_target_pairs={{0,8},{1,9},{2,10},{3,11},{4,12},{5,13},{6,14},{7,15},{8,0},{9,1},... | collective-permute-start | bytes 153608 | tf_op jit(solution)/shard_map/ppermute | solution.py:537
  7.3 5.6 %collective-permute-start.3 = (bf16[4,6400]{1,0:T(4,128)(2,1)S(1)}, bf16[4,6400]{1,0:T(4,128)(2,1)S(1)}, u32[]{:S(2)}, u32[]{:S(2)}) collective-permute-start(bf16[4,6400]{1,0:T(4,128)(2,1)S(1)} %get-tuple-element.14.refs_0_), channel_id=1, source_target_pairs={{0,2},{1,3},{2,0},{3,1},{4,6},{5,7},{6,4},{7,5},{8,10},{9,11},{10,... | collective-permute-start | bytes 153608 | tf_op jit(solution)/shard_map/ppermute | solution.py:537
  10.0 4.1 %collective-permute-start.6 = (bf16[4,6400]{1,0:T(4,128)(2,1)S(1)}, bf16[4,6400]{1,0:T(4,128)(2,1)S(1)}, u32[]{:S(2)}, u32[]{:S(2)}) collective-permute-start(bf16[4,6400]{1,0:T(4,128)(2,1)S(1)} %collective-permute-done), channel_id=1, source_target_pairs={{0,2},{1,3},{2,0},{3,1},{4,6},{5,7},{6,4},{7,5},{8,10},{9,11},{10,... | collective-permute-start | bytes 153608 | tf_op jit(solution)/shard_map/ppermute | solution.py:537
  11.8 6.9 %collective-permute-start.1 = (bf16[8,6400]{1,0:T(8,128)(2,1)S(1)}, bf16[8,6400]{1,0:T(8,128)(2,1)S(1)}, u32[]{:S(2)}, u32[]{:S(2)}) collective-permute-start(bf16[8,6400]{1,0:T(8,128)(2,1)S(1)} %pad_maximum_fusion.3), channel_id=1, source_target_pairs={{0,4},{1,5},{2,6},{3,7},{4,0},{5,1},{6,2},{7,3},{8,12},{9,13},{10,... | collective-permute-start | bytes 307208 | tf_op jit(solution)/shard_map/ppermute | solution.py:537
  13.0 4.1 %collective-permute-start.4 = (bf16[4,6400]{1,0:T(4,128)(2,1)S(1)}, bf16[4,6400]{1,0:T(4,128)(2,1)S(1)}, u32[]{:S(2)}, u32[]{:S(2)}) collective-permute-start(bf16[4,6400]{1,0:T(4,128)(2,1)S(1)} %collective-permute-done.3), channel_id=1, source_target_pairs={{0,4},{1,5},{2,6},{3,7},{4,0},{5,1},{6,2},{7,3},{8,12},{9,13},{10,... | collective-permute-start | bytes 153608 | tf_op jit(solution)/shard_map/ppermute | solution.py:537
  14.1 4.1 %collective-permute-start.7 = (bf16[4,6400]{1,0:T(4,128)(2,1)S(1)}, bf16[4,6400]{1,0:T(4,128)(2,1)S(1)}, u32[]{:S(2)}, u32[]{:S(2)}) collective-permute-start(bf16[4,6400]{1,0:T(4,128)(2,1)S(1)} %collective-permute-done.6), channel_id=1, source_target_pairs={{0,4},{1,5},{2,6},{3,7},{4,0},{5,1},{6,2},{7,3},{8,12},{9,13},{10,... | collective-permute-start | bytes 153608 | tf_op jit(solution)/shard_map/ppermute | solution.py:537
  15.6 4.5 %collective-permute-start.9 = (bf16[16,6400]{1,0:T(8,128)(2,1)S(1)}, bf16[16,6400]{1,0:T(8,128)(2,1)S(1)}, u32[]{:S(2)}, u32[]{:S(2)}) collective-permute-start(bf16[16,6400]{1,0:T(8,128)(2,1)S(1)} %pad_maximum_fusion.2.chunk_ref), channel_id=1, source_target_pairs={{0,1},{1,0},{2,3},{3,2},{4,5},{5,4},{6,7},{7,6},{8,9},{9,8},{10,11... | collective-permute-start | bytes 614408 | tf_op jit(solution)/shard_map/ppermute | solution.py:537
  17.1 1.7 %collective-permute-start.5 = (bf16[4,6400]{1,0:T(4,128)(2,1)S(1)}, bf16[4,6400]{1,0:T(4,128)(2,1)S(1)}, u32[]{:S(2)}, u32[]{:S(2)}) collective-permute-start(bf16[4,6400]{1,0:T(4,128)(2,1)S(1)} %collective-permute-done.4), channel_id=1, source_target_pairs={{0,1},{1,0},{2,3},{3,2},{4,5},{5,4},{6,7},{7,6},{8,9},{9,8},{10,11... | collective-permute-start | bytes 153608 | tf_op jit(solution)/shard_map/ppermute | solution.py:537
  18.2 1.4 %collective-permute-start.8 = (bf16[4,6400]{1,0:T(4,128)(2,1)S(1)}, bf16[4,6400]{1,0:T(4,128)(2,1)S(1)}, u32[]{:S(2)}, u32[]{:S(2)}) collective-permute-start(bf16[4,6400]{1,0:T(4,128)(2,1)S(1)} %collective-permute-done.7), channel_id=1, source_target_pairs={{0,1},{1,0},{2,3},{3,2},{4,5},{5,4},{6,7},{7,6},{8,9},{9,8},{10,11... | collective-permute-start | bytes 153608 | tf_op jit(solution)/shard_map/ppermute | solution.py:537
  18.7 1.3 %collective-permute-start.2 = (bf16[8,6400]{1,0:T(8,128)(2,1)S(1)}, bf16[8,6400]{1,0:T(8,128)(2,1)S(1)}, u32[]{:S(2)}, u32[]{:S(2)}) collective-permute-start(bf16[8,6400]{1,0:T(8,128)(2,1)S(1)} %collective-permute-done.1), channel_id=1, source_target_pairs={{0,1},{1,0},{2,3},{3,2},{4,5},{5,4},{6,7},{7,6},{8,9},{9,8},{10,11... | collective-permute-start | bytes 307208 | tf_op jit(solution)/shard_map/ppermute | solution.py:537

commit v7 on v6

--- a/solution.py
+++ b/solution.py
@@ -36,21 +36,11 @@
 def dft_table():
     n1 = np.arange(PART)[:, None]
     blocks = []
-    for r in (0, 2, 1, 3):
+    for r in range(RADIX):
         k = FLO + RADIX * np.arange(LANE)[None, :] + r
         phase = np.mod(n1 * k, SEG) * (2.0 * math.pi / SEG)
-        c, s = np.cos(phase), np.sin(phase)
-        blocks.append(np.concatenate([c, -s], 1))
-        if r == 1:
-            blocks.append(np.concatenate([-s, -c], 1))
-        if r == 3:
-            blocks.append(np.concatenate([s, c], 1) * np.array([1.0]))
+        blocks.append(np.concatenate([np.cos(phase), np.sin(phase)], 1))
     return np.concatenate(blocks, 0).astype(jnp.bfloat16)
-
-
-def band_table():
-    f = bin_order()
-    return (np.abs(f[:, None] - f[None, :]) <= HALF).astype(jnp.bfloat16)
 
 
 def lag_table():
@@ -136,8 +126,8 @@
 
 
 def front_kernel(
-    plan, gaps_hbm, assign_hbm, target_hbm, x_hbm, tab_hbm, band_hbm, out_ref, pick_ref, mine_ref,
-    weight_ref, gaps_ref, assign_ref, target_ref, x_ref, tab_ref, band_ref, sem,
+    plan, gaps_hbm, assign_hbm, target_hbm, x_hbm, tab_hbm, out_ref, pick_ref, mine_ref,
+    weight_ref, gaps_ref, assign_ref, target_ref, x_ref, tab_ref, sem,
 ):
     windows, own = gaps_ref.shape
     rows = windows * own
@@ -152,12 +142,11 @@
             pltpu.make_async_copy(tab_hbm.at[part_at(i)], tab_ref.at[part_at(i)], sem.at[1 + i])
             for i in range(parts)
         ],
-        pltpu.make_async_copy(band_hbm, band_ref, sem.at[1 + parts]),
-        pltpu.make_async_copy(gaps_hbm, gaps_ref, sem.at[2 + parts]),
+        pltpu.make_async_copy(gaps_hbm, gaps_ref, sem.at[1 + parts]),
     ]
     names = [
-        pltpu.make_async_copy(assign_hbm, assign_ref, sem.at[3 + parts]),
-        pltpu.make_async_copy(target_hbm, target_ref, sem.at[4 + parts]),
+        pltpu.make_async_copy(assign_hbm, assign_ref, sem.at[2 + parts]),
+        pltpu.make_async_copy(target_hbm, target_ref, sem.at[3 + parts]),
     ]
     for load in names + loads:
         load.start()
@@ -178,45 +167,58 @@
     x0, x1, x2, x3 = quarter
     even, odd = x0 + x2, x1 + x3
 
-    def halves(y):
-        low = y - y.astype(jnp.bfloat16).astype(jnp.float32)
-        return jnp.concatenate([y, low], 0).astype(jnp.bfloat16)
-
-    zero, two = halves(even + odd), halves(even - odd)
-    u, v = halves(x0 - x2), halves(x1 - x3)
+    def halves(*ys):
+        lows = [y - y.astype(jnp.bfloat16).astype(jnp.float32) for y in ys]
+        return jnp.concatenate([*ys, *lows], 0).astype(jnp.bfloat16)
+
+    def band(d):
+        gap = RADIX * (iota(LANE, LANE, 0) - iota(LANE, LANE, 1)) + d
+        return jnp.where(jnp.abs(gap) <= HALF, 1.0, 0.0).astype(jnp.bfloat16)
+
+    bands = {d: band(d) for d in range(1 - RADIX, RADIX)}
+    count = COMP * rows
+    straight = [halves(even + odd), halves(even - odd)]
+    turned = halves(x0 - x2, x1 - x3)
 
     def tab(i):
         loads[1 + i].wait()
         return tab_ref[part_at(i), :]
 
-    both0 = mm(zero, tab(0))
-    both2 = mm(two, tab(1))
-    both1 = mm(u, tab(2)) + mm(v, tab(3))
-    both3 = mm(u, tab(4)) + mm(v, tab(5))
-    both = [both0, both1, both2, both3]
-    count = COMP * rows
-    spec = [d[:count] + d[count:] for d in both]
+    spec = []
+    for r in range(RADIX):
+        if r % 2 == 0:
+            d = mm(straight[r // 2], tab(r))
+            d = d[:count] + d[count:]
+            spec.append((d[:, :LANE], -d[:, LANE:]))
+        else:
+            d = mm(turned, tab(r))
+            u = d[:count] + d[2 * count : 3 * count]
+            v = d[count : 2 * count] + d[3 * count :]
+            sign = 1.0 if r == 1 else -1.0
+            spec.append(
+                (u[:, :LANE] - sign * v[:, LANE:], -u[:, LANE:] - sign * v[:, :LANE])
+            )
     power = []
-    for d in spec:
+    for re, im in spec:
         total = jnp.zeros((rows, LANE), jnp.float32)
         for a in range(COMP):
-            re = d[a * rows : (a + 1) * rows, :LANE]
-            im = d[a * rows : (a + 1) * rows, LANE:]
-            total = total + (re * re + im * im)
+            both = re[a * rows : (a + 1) * rows], im[a * rows : (a + 1) * rows]
+            total = total + (both[0] * both[0] + both[1] * both[1])
         power.append(total)
     power = jnp.concatenate(power, 1)
     p1 = power.astype(jnp.bfloat16).astype(jnp.float32)
     rest = power - p1
     p2 = rest.astype(jnp.bfloat16).astype(jnp.float32)
     p3 = rest - p2
-    loads[1 + parts].wait()
-    sums = mm(jnp.concatenate([p1, p2, p3], 0).astype(jnp.bfloat16), band_ref[...])
+    three = jnp.concatenate([p1, p2, p3], 0).astype(jnp.bfloat16)
+    reach = [jnp.concatenate([bands[q - r] for r in range(RADIX)], 1) for q in range(RADIX)]
+    sums = mm(three, jnp.concatenate(reach, 0))
     spot = iota(rows, FREQ, 1)
     f = RADIX * (spot % LANE) + spot // LANE
     taken = jnp.minimum(f + HALF, FREQ - 1) - jnp.maximum(f - HALF, 0) + 1
     share = 1.0 / (taken.astype(jnp.float32) * float(COMP))
     smooth = (sums[:rows] + sums[rows : 2 * rows] + sums[2 * rows :]) * share
-    loads[2 + parts].wait()
+    loads[1 + parts].wait()
     row_at = lax.broadcasted_iota(jnp.int32, (rows, LANE), 0)
     flags = jnp.zeros((rows, LANE), jnp.float32)
     for w in range(windows):
@@ -226,9 +228,7 @@
     factor = wide_flags / jnp.sqrt(smooth + 1e-06)
     for a in range(COMP):
         for part in range(2):
-            whole = jnp.concatenate(
-                [d[a * rows : (a + 1) * rows, part * LANE : (part + 1) * LANE] for d in spec], 1
-            )
+            whole = jnp.concatenate([d[part][a * rows : (a + 1) * rows] for d in spec], 1)
             white = whole * factor
             for w in range(windows):
                 start = w * PLANE + (2 * a + part) * FREQ
@@ -242,8 +242,8 @@
     own, comps, length = traces.shape
     windows = gaps.shape[1]
     assert comps == COMP and length == windows * SEG
-    table, band = dft_table(), band_table()
-    operands = (gaps.T, assign, target, traces.transpose(1, 0, 2), jnp.asarray(table), jnp.asarray(band))
+    table = dft_table()
+    operands = (gaps.T, assign, target, traces.transpose(1, 0, 2), jnp.asarray(table))
     hbm = pl.BlockSpec(memory_space=pltpu.HBM)
     vmem = pl.BlockSpec(memory_space=pltpu.VMEM)
     bf16 = jnp.bfloat16
@@ -256,7 +256,7 @@
             jax.ShapeDtypeStruct((groups, CAP * stations, own), bf16),
             jax.ShapeDtypeStruct((groups, own, CAP * stations), bf16),
         ),
-        in_specs=[hbm] * 6,
+        in_specs=[hbm] * 5,
         out_specs=(vmem,) * 4,
         scratch_shapes=[
             pltpu.SMEM((windows, own), jnp.int32),
@@ -264,17 +264,54 @@
             pltpu.SMEM(target.shape, jnp.int32),
             pltpu.VMEM((comps, own, length), bf16),
             pltpu.VMEM(table.shape, bf16),
-            pltpu.VMEM(band.shape, bf16),
-            pltpu.SemaphoreType.DMA((5 + table.shape[0] // PART,)),
+            pltpu.SemaphoreType.DMA((4 + table.shape[0] // PART,)),
         ],
         compiler_params=room(0),
         name="front",
     )(*[pltpu.with_memory_space_constraint(v, pltpu.HBM) for v in operands])
 
 
+def spread_kernel(mine_ref, self_ref, rows_ref, partner_ref):
+    own = self_ref.shape[0]
+    pairs = GROUP * CAP
+    mine_rows = self_ref[...]
+    each = one_hot(iota(own * pairs, own, 0) // pairs, own)
+    rows_ref[...] = mm(each, mine_rows).astype(jnp.bfloat16)
+    groups = mine_ref.shape[0]
+
+    def one_group(ch, carry):
+        partner_ref[ch] = mm(mine_ref[ch], mine_rows).astype(jnp.bfloat16)
+        return carry
+
+    lax.fori_loop(0, groups, one_group, 0, unroll=min(groups, 4))
+
+
+def spread(held, mine):
+    own, lanes = held.shape
+    groups, made, _ = mine.shape
+    vmem = pl.BlockSpec(memory_space=pltpu.VMEM)
+    bf16 = jnp.bfloat16
+    rows = own * GROUP * CAP
+    total = rows + groups * made
+    return pl.pallas_call(
+        spread_kernel,
+        out_shape=(
+            jax.ShapeDtypeStruct((rows, lanes), bf16),
+            jax.ShapeDtypeStruct((groups, made, lanes), bf16),
+        ),
+        in_specs=[vmem] * 2,
+        out_specs=(vmem,) * 2,
+        compiler_params=room(2 * total * lanes),
+        cost_estimate=pl.CostEstimate(
+            flops=2 * total * own * lanes, bytes_accessed=2 * total * lanes, transcendentals=0
+        ),
+        name="spread",
+    )(mine, held)
+
+
 def correlate_kernel(plan, owners, own, windows, base, kind, chunk_ref, *refs):
     refs = list(refs)
-    self_ref, pick_ref, mine_ref, weight_ref, lag_ref = refs[:5]
+    rows_ref, partner_ref, pick_ref, weight_ref, lag_ref = refs[:5]
     refs = refs[5:]
     sum_in = refs.pop(0) if kind["sums"] else None
     waiting = [(refs.pop(0), place) for place in kind["waiting"]]
@@ -283,7 +320,7 @@
     out_ref = refs.pop(0) if kind["out"] else None
     kept = refs.pop(0) if kind["keep"] else None
     sum_ref = refs.pop(0)
-    rows_ref, picked, cross_e, result_e, cross, result, outv, energy_v, sem = refs
+    picked, cross_e, result_e, cross, result, outv, energy_v, sem = refs
     me = lax.axis_index("pairs")
     pairs = GROUP * CAP
     stations = GROUP * own
@@ -312,9 +349,6 @@
         first_row = ch * stations if isinstance(ch, int) else pl.multiple_of(ch * stations, stations)
         here = pl.ds(first_row, stations)
         number = base // GROUP + ch
-        each = one_hot(iota(own * pairs, own, 0) // pairs, own)
-        spread = jnp.concatenate([each, mine_ref[number]], 0)
-        rows_ref[...] = mm(spread, self_ref[...]).astype(jnp.bfloat16)
         picked[...] = mm(pick_ref[number], chunk_ref[here, :]).astype(jnp.bfloat16)
 
         def product(left, right):
@@ -337,7 +371,7 @@
             return got
 
         def partner(rows, lanes):
-            return rows_ref[own * pairs + rows.start : own * pairs + rows.stop, lanes]
+            return partner_ref[number, rows, lanes]
 
         tiles = FREQ // TILE
 
@@ -346,26 +380,28 @@
                 start = (2 * lt + part) * TILE
                 ref[at : at + rows, start : start + TILE] = values[part]
 
-        for lt in range(tiles):
-            lefts = [tile(lambda d: chunk_ref[here, d], a, lt) for a in range(COMP)]
-            for c in range(CAP):
-                part_rows = slice(c * stations, (c + 1) * stations)
+        for c in range(CAP):
+            part_rows = slice(c * stations, (c + 1) * stations)
+            for lt in range(tiles):
+                lefts = [tile(lambda d: chunk_ref[here, d], a, lt) for a in range(COMP)]
                 for b in range(COMP):
                     right = tile(lambda d: partner(part_rows, d), b, lt)
                     for a in range(COMP):
                         at = ((c * COMP + a) * COMP + b) * stations
                         keep(cross_e, at, stations, lt, product(lefts[a], right))
-        result_e[...] = mm(cross_e[...], lag_ref[...])
-        for lt in range(tiles):
-            slots = [tile(lambda d: picked[:, d], b, lt) for b in range(COMP)]
-            for yp in range(own // 2):
-                y_rows = slice(yp * 2 * pairs, (yp + 1) * 2 * pairs)
+            lines = slice(c * nine * stations, (c + 1) * nine * stations)
+            result_e[lines, :] = mm(cross_e[lines, :], lag_ref[...])
+        for yp in range(own // 2):
+            y_rows = slice(yp * 2 * pairs, (yp + 1) * 2 * pairs)
+            for lt in range(tiles):
+                slots = [tile(lambda d: picked[:, d], b, lt) for b in range(COMP)]
                 for a in range(COMP):
                     left = tile(lambda d: rows_ref[y_rows, d], a, lt)
                     for b in range(COMP):
                         at = ((yp * COMP + a) * COMP + b) * 2 * pairs
                         keep(cross, at, 2 * pairs, lt, product(left, slots[b]))
-        result[...] = mm(cross[...], lag_ref[...])
+            lines = slice(yp * nine * 2 * pairs, (yp + 1) * nine * 2 * pairs)
+            result[lines, :] = mm(cross[lines, :], lag_ref[...])
 
         def flag_at(w):
             return slice(PLANE * windows + w * LANE, PLANE * windows + (w + 1) * LANE)
@@ -454,8 +490,8 @@
                 cp.wait()
 
 
-def correlate(plan, block, base, held, names, lags, carried, last, owners, windows):
-    own = held.shape[0]
+def correlate(plan, block, base, rows, lags, carried, last, owners, windows):
+    own = rows[3].shape[1]
     nine = COMP * COMP
     stations, pairs = GROUP * own, GROUP * CAP
     vmem = pl.BlockSpec(memory_space=pltpu.VMEM)
@@ -472,7 +508,7 @@
         "keep": keep,
         "out": not keep,
     }
-    operands, aliases = [block, held, *names, lags], {}
+    operands, aliases = [block, *rows, lags], {}
     specs = [vmem] * len(operands)
     if kind["sums"]:
         operands.append(sums)
@@ -502,7 +538,6 @@
         out_specs=tuple(out_specs),
         input_output_aliases=aliases,
         scratch_shapes=[
-            pltpu.VMEM((own * pairs + CAP * stations, WIDE), bf16),
             pltpu.VMEM((2 * pairs, WIDE), bf16),
             pltpu.VMEM((half, 2 * FREQ), bf16),
             pltpu.VMEM((half, LAGS), f32),
@@ -539,7 +574,8 @@
     def join(*parts):
         return jnp.concatenate(parts, 0)
 
-    held, *names = front(plan, traces, gaps, assign, target)
+    held, pick, mine, weight = front(plan, traces, gaps, assign, target)
+    rows = (*spread(held, mine), pick, weight)
     wide, near, third = plan[:3]
     a = swap(held, wide)
     b0 = swap(held, near)
@@ -568,7 +604,7 @@
     carried = (None, [], None)
     for at, (block, start) in enumerate(ranked):
         last = at == len(ranked) - 1
-        carried = correlate(plan, block, start, held, names, lags, carried, last, owners, windows)
+        carried = correlate(plan, block, start, rows, lags, carried, last, owners, windows)
     energy, _, out = carried
     return out.transpose(0, 1, 3, 2, 4), energy
 

time: 24.1 us -> 22.9 us (0.950)
  waiting for transfers between devices: 4.05 us -> 3.45 us
  Pallas kernels: 7.38 us -> 6.84 us
    pallas_call x4, Pallas kernels: 4.82 us -> 3.78 us  [correlate(): pl.pallas_call(functools.partial(correlate_kernel, plan, owners, own, win...]
    pallas_call x0 -> x1, Pallas kernels: none -> 0.66 us  [spread(): pl.pallas_call(spread_kernel, out_shape=(jax.ShapeDtypeStruct((rows, lane...]
    ppermute x10, waiting for transfers between devices: 4.05 us -> 3.45 us  [swap(): return lax.ppermute(block, 'pairs', [(i, i ^ mask) for i in range(owners)])]
  transfers between devices with their start and end apart: 10 -> 10, of which waited for: 6 -> 6; matrix products, arithmetic and copies ran while one was open for 1% -> 1% of each run, Pallas kernels for 4% -> 6%
where the time goes in v7:
time: 22.9 us; the launch traced here: 22.7 us
  starting transfers between devices  11.4 us (50%)
  Pallas kernels  6.84 us (30%)
  waiting for transfers between devices  3.45 us (15%)
  between operations  0.72 us (3%)
  other arithmetic  0.3 us (1%)
    ppermute x10, starting transfers between devices, swap(): return lax.ppermute(block, 'pairs', [(i, i ^ mask) for i in range(owners)])  11.4 us
    pallas_call x4, Pallas kernels, correlate(): pl.pallas_call(functools.partial(correlate_kernel, plan, owners, own, win...  3.78 us
    ppermute x10, waiting for transfers between devices, swap(): return lax.ppermute(block, 'pairs', [(i, i ^ mask) for i in range(owners)])  3.45 us
    pallas_call x1, Pallas kernels, front(): pl.pallas_call(functools.partial(front_kernel, plan), out_shape=(jax.Shap...  2.4 us
    pallas_call x1, Pallas kernels, spread(): pl.pallas_call(spread_kernel, out_shape=(jax.ShapeDtypeStruct((rows, lane...  0.66 us
  transfers between devices with their start and end apart: 10, of which 6 were waited for; matrix products, arithmetic and copies ran while one was open for 1% of the time, Pallas kernels for 6%

profile of v7, /device:TPU:0, one launch (start us, length us, event | category | flops | bytes accessed | tf_op | source)
XLA Modules:
  0.0 22.7 jit_solution(15517564682306914819)
XLA Ops:
  0.6 0.0 copy-start
  0.6 2.4 %front.1 = (bf16[4,6400]{1,0:T(4,128)(2,1)S(1)}, bf16[4,16,16]{2,1,0:T(8,128)(2,1)S(1)}, bf16[4,32,4]{2,1,0:T(8,128)(2,1)S(1)}, bf16[4,4,32]{2,1,0:T(4,128)(2,1)S(1)}) custom-call(s32[2,4]{1,0:T(2,128)} %bitcast.4, s32[64]{0:T(128)} %assign_hbm.1, s32[16]{0:T(128)} %target_hbm.1, bf16[3,4,4096]{2,1,0:T(4,128)(2,1)} %bitcast.3, ...), custom_call_target="tpu_custom_call" | custom-call | tf_op jit(solution)/shard_map/front/pallas_call | solution.py:251
  3.0 4.1 %collective-permute-start = (bf16[4,6400]{1,0:T(4,128)(2,1)S(1)}, bf16[4,6400]{1,0:T(4,128)(2,1)S(1)}, u32[]{:S(2)}, u32[]{:S(2)}) collective-permute-start(bf16[4,6400]{1,0:T(4,128)(2,1)S(1)} %get-tuple-element.16.self_ref), channel_id=1, source_target_pairs={{0,8},{1,9},{2,10},{3,11},{4,12},{5,13},{6,14},{7,15},{8,0},{9,1},... | collective-permute-start | bytes 153608 | tf_op jit(solution)/shard_map/ppermute | solution.py:572
  7.2 1.5 %collective-permute-start.3 = (bf16[4,6400]{1,0:T(4,128)(2,1)S(1)}, bf16[4,6400]{1,0:T(4,128)(2,1)S(1)}, u32[]{:S(2)}, u32[]{:S(2)}) collective-permute-start(bf16[4,6400]{1,0:T(4,128)(2,1)S(1)} %get-tuple-element.16.self_ref), channel_id=1, source_target_pairs={{0,2},{1,3},{2,0},{3,1},{4,6},{5,7},{6,4},{7,5},{8,10},{9,11},{10,... | collective-permute-start | bytes 153608 | tf_op jit(solution)/shard_map/ppermute | solution.py:572
  8.7 0.7 %spread.1 = (bf16[32,6400]{1,0:T(8,128)(2,1)S(1)}, bf16[4,32,6400]{2,1,0:T(8,128)(2,1)S(1)}) custom-call(bf16[4,32,4]{2,1,0:T(8,128)(2,1)S(1)} %get-tuple-element.17.mine_ref, bf16[4,6400]{1,0:T(4,128)(2,1)S(1)} %get-tuple-element.16.self_ref), custom_call_target="tpu_custom_call" | custom-call | flops 8192000 | bytes 2048000 | tf_op jit(solution)/shard_map/spread/pallas_call | solution.py:296
  9.4 0.5 %collective-permute-done = bf16[4,6400]{1,0:T(4,128)(2,1)S(1)} collective-permute-done((bf16[4,6400]{1,0:T(4,128)(2,1)S(1)}, bf16[4,6400]{1,0:T(4,128)(2,1)S(1)}, u32[]{:S(2)}, u32[]{:S(2)}) %collective-permute-start) | collective-permute-done | bytes 51232 | tf_op jit(solution)/shard_map/ppermute | solution.py:572
  9.8 1.7 %collective-permute-start.6 = (bf16[4,6400]{1,0:T(4,128)(2,1)S(1)}, bf16[4,6400]{1,0:T(4,128)(2,1)S(1)}, u32[]{:S(2)}, u32[]{:S(2)}) collective-permute-start(bf16[4,6400]{1,0:T(4,128)(2,1)S(1)} %collective-permute-done), channel_id=1, source_target_pairs={{0,2},{1,3},{2,0},{3,1},{4,6},{5,7},{6,4},{7,5},{8,10},{9,11},{10,... | collective-permute-start | bytes 153608 | tf_op jit(solution)/shard_map/ppermute | solution.py:572
  11.5 0.1 pad_maximum_fusion.3
  11.6 1.2 %collective-permute-start.1 = (bf16[8,6400]{1,0:T(8,128)(2,1)S(1)}, bf16[8,6400]{1,0:T(8,128)(2,1)S(1)}, u32[]{:S(2)}, u32[]{:S(2)}) collective-permute-start(bf16[8,6400]{1,0:T(8,128)(2,1)S(1)} %pad_maximum_fusion.3), channel_id=1, source_target_pairs={{0,4},{1,5},{2,6},{3,7},{4,0},{5,1},{6,2},{7,3},{8,12},{9,13},{10,... | collective-permute-start | bytes 307208 | tf_op jit(solution)/shard_map/ppermute | solution.py:572
  12.8 0.0 collective-permute-done.3
  12.8 0.9 %collective-permute-start.4 = (bf16[4,6400]{1,0:T(4,128)(2,1)S(1)}, bf16[4,6400]{1,0:T(4,128)(2,1)S(1)}, u32[]{:S(2)}, u32[]{:S(2)}) collective-permute-start(bf16[4,6400]{1,0:T(4,128)(2,1)S(1)} %collective-permute-done.3), channel_id=1, source_target_pairs={{0,4},{1,5},{2,6},{3,7},{4,0},{5,1},{6,2},{7,3},{8,12},{9,13},{10,... | collective-permute-start | bytes 153608 | tf_op jit(solution)/shard_map/ppermute | solution.py:572
  13.7 0.2 %collective-permute-done.6 = bf16[4,6400]{1,0:T(4,128)(2,1)S(1)} collective-permute-done((bf16[4,6400]{1,0:T(4,128)(2,1)S(1)}, bf16[4,6400]{1,0:T(4,128)(2,1)S(1)}, u32[]{:S(2)}, u32[]{:S(2)}) %collective-permute-start.6) | collective-permute-done | bytes 51232 | tf_op jit(solution)/shard_map/ppermute | solution.py:572
  13.9 1.4 %collective-permute-start.7 = (bf16[4,6400]{1,0:T(4,128)(2,1)S(1)}, bf16[4,6400]{1,0:T(4,128)(2,1)S(1)}, u32[]{:S(2)}, u32[]{:S(2)}) collective-permute-start(bf16[4,6400]{1,0:T(4,128)(2,1)S(1)} %collective-permute-done.6), channel_id=1, source_target_pairs={{0,4},{1,5},{2,6},{3,7},{4,0},{5,1},{6,2},{7,3},{8,12},{9,13},{10,... | collective-permute-start | bytes 153608 | tf_op jit(solution)/shard_map/ppermute | solution.py:572
  15.3 0.1 pad_maximum_fusion.2.chunk_ref
  15.4 0.1 collective-permute-start.9
  15.5 1.4 %collective-permute-done.4 = bf16[4,6400]{1,0:T(4,128)(2,1)S(1)} collective-permute-done((bf16[4,6400]{1,0:T(4,128)(2,1)S(1)}, bf16[4,6400]{1,0:T(4,128)(2,1)S(1)}, u32[]{:S(2)}, u32[]{:S(2)}) %collective-permute-start.4) | collective-permute-done | bytes 51232 | tf_op jit(solution)/shard_map/ppermute | solution.py:572
  16.9 0.0 collective-permute-start.5
  16.9 0.0 copy-done
  16.9 0.8 %correlate.4 = (bf16[4,4,9,2,256]{4,3,2,1,0:T(2,128)(2,1)S(1)}, f32[4,1152]{1,0:T(4,128)S(1)}) custom-call(bf16[16,6400]{1,0:T(8,128)(2,1)S(1)} %pad_maximum_fusion.2.chunk_ref, bf16[32,6400]{1,0:T(8,128)(2,1)S(1)} %get-tuple-element.18.refs_0_, bf16[4,32,6400]{2,1,0:T(8,128)(2,1)S(1)} %get-tuple-element.19.refs_1_, ...), custom_call_target="tpu_custom_call" | custom-call | flops 301989888 | bytes 294912 | tf_op jit(solution)/shard_map/correlate/pallas_call | solution.py:534
  17.7 0.3 %collective-permute-done.7 = bf16[4,6400]{1,0:T(4,128)(2,1)S(1)} collective-permute-done((bf16[4,6400]{1,0:T(4,128)(2,1)S(1)}, bf16[4,6400]{1,0:T(4,128)(2,1)S(1)}, u32[]{:S(2)}, u32[]{:S(2)}) %collective-permute-start.7) | collective-permute-done | bytes 51232 | tf_op jit(solution)/shard_map/ppermute | solution.py:572
  18.0 0.3 %collective-permute-start.8 = (bf16[4,6400]{1,0:T(4,128)(2,1)S(1)}, bf16[4,6400]{1,0:T(4,128)(2,1)S(1)}, u32[]{:S(2)}, u32[]{:S(2)}) collective-permute-start(bf16[4,6400]{1,0:T(4,128)(2,1)S(1)} %collective-permute-done.7), channel_id=1, source_target_pairs={{0,1},{1,0},{2,3},{3,2},{4,5},{5,4},{6,7},{7,6},{8,9},{9,8},{10,11... | collective-permute-start | bytes 153608 | tf_op jit(solution)/shard_map/ppermute | solution.py:572
  18.3 0.0 collective-permute-done.1
  18.3 0.3 %collective-permute-start.2 = (bf16[8,6400]{1,0:T(8,128)(2,1)S(1)}, bf16[8,6400]{1,0:T(8,128)(2,1)S(1)}, u32[]{:S(2)}, u32[]{:S(2)}) collective-permute-start(bf16[8,6400]{1,0:T(8,128)(2,1)S(1)} %collective-permute-done.1), channel_id=1, source_target_pairs={{0,1},{1,0},{2,3},{3,2},{4,5},{5,4},{6,7},{7,6},{8,9},{9,8},{10,11... | collective-permute-start | bytes 307208 | tf_op jit(solution)/shard_map/ppermute | solution.py:572
  18.6 0.1 pad_maximum_fusion.1.chunk_ref
  18.6 0.0 collective-permute-done.5
  18.6 0.6 %collective-permute-done.8 = bf16[4,6400]{1,0:T(4,128)(2,1)S(1)} collective-permute-done((bf16[4,6400]{1,0:T(4,128)(2,1)S(1)}, bf16[4,6400]{1,0:T(4,128)(2,1)S(1)}, u32[]{:S(2)}, u32[]{:S(2)}) %collective-permute-start.8) | collective-permute-done | bytes 51232 | tf_op jit(solution)/shard_map/ppermute | solution.py:572
  19.3 0.3 %collective-permute-done.2 = bf16[8,6400]{1,0:T(8,128)(2,1)S(1)} collective-permute-done((bf16[8,6400]{1,0:T(8,128)(2,1)S(1)}, bf16[8,6400]{1,0:T(8,128)(2,1)S(1)}, u32[]{:S(2)}, u32[]{:S(2)}) %collective-permute-start.2) | collective-permute-done | bytes 102432 | tf_op jit(solution)/shard_map/ppermute | solution.py:572
  19.6 0.1 pad_maximum_fusion.chunk_ref
  19.7 0.0 collective-permute-done.9.chunk_ref
  19.7 0.7 %correlate.5 = (bf16[4,4,9,2,256]{4,3,2,1,0:T(2,128)(2,1)S(1)}, f32[4,1152]{1,0:T(4,128)S(1)}) custom-call(bf16[16,6400]{1,0:T(8,128)(2,1)S(1)} %collective-permute-done.9.chunk_ref, bf16[32,6400]{1,0:T(8,128)(2,1)S(1)} %get-tuple-element.18.refs_0_, bf16[4,32,6400]{2,1,0:T(8,128)(2,1)S(1)} %get-tuple-element.19.refs_1_, ...), custom_call_target="tpu_custom_call" | custom-call | flops 301989888 | bytes 294912 | tf_op jit(solution)/shard_map/correlate/pallas_call | solution.py:534
  20.4 0.7 %correlate.6 = (bf16[4,4,9,2,256]{4,3,2,1,0:T(2,128)(2,1)S(1)}, f32[4,1152]{1,0:T(4,128)S(1)}) custom-call(bf16[16,6400]{1,0:T(8,128)(2,1)S(1)} %pad_maximum_fusion.1.chunk_ref, bf16[32,6400]{1,0:T(8,128)(2,1)S(1)} %get-tuple-element.18.refs_0_, bf16[4,32,6400]{2,1,0:T(8,128)(2,1)S(1)} %get-tuple-element.19.refs_1_, ...), custom_call_target="tpu_custom_call" | custom-call | flops 301989888 | bytes 294912 | tf_op jit(solution)/shard_map/correlate/pallas_call | solution.py:534
  21.2 1.5 %correlate.7 = (bf16[4,16,9,2,256]{4,3,2,1,0:T(2,128)(2,1)}, f32[4,9]{1,0:T(4,128)}) custom-call(bf16[16,6400]{1,0:T(8,128)(2,1)S(1)} %pad_maximum_fusion.chunk_ref, bf16[32,6400]{1,0:T(8,128)(2,1)S(1)} %get-tuple-element.18.refs_0_, bf16[4,32,6400]{2,1,0:T(8,128)(2,1)S(1)} %get-tuple-element.19.refs_1_, bf16[4,16,16]{2,1,0:T(8,128)(2,1)S(1)} %get-tuple-element.20.refs_2_, ...), custom_call_target="tpu_custom_call" | custom-call | flops 301989888 | bytes 294912 | tf_op jit(solution)/shard_map/correlate/pallas_call | solution.py:534
Async XLA Ops:
  0.6 16.3 %copy-start = (bf16[1024,256]{1,0:T(8,128)(2,1)S(1)}, bf16[1024,256]{1,0:T(8,128)(2,1)}, u32[]{:S(2)}) copy-start(bf16[1024,256]{1,0:T(8,128)(2,1)} %constant.4.clone.refs_4_) | copy-start | bytes 1572868
  3.0 6.8 %collective-permute-start = (bf16[4,6400]{1,0:T(4,128)(2,1)S(1)}, bf16[4,6400]{1,0:T(4,128)(2,1)S(1)}, u32[]{:S(2)}, u32[]{:S(2)}) collective-permute-start(bf16[4,6400]{1,0:T(4,128)(2,1)S(1)} %get-tuple-element.16.self_ref), channel_id=1, source_target_pairs={{0,8},{1,9},{2,10},{3,11},{4,12},{5,13},{6,14},{7,15},{8,0},{9,1},... | collective-permute-start | bytes 153608 | tf_op jit(solution)/shard_map/ppermute | solution.py:572
  7.2 5.6 %collective-permute-start.3 = (bf16[4,6400]{1,0:T(4,128)(2,1)S(1)}, bf16[4,6400]{1,0:T(4,128)(2,1)S(1)}, u32[]{:S(2)}, u32[]{:S(2)}) collective-permute-start(bf16[4,6400]{1,0:T(4,128)(2,1)S(1)} %get-tuple-element.16.self_ref), channel_id=1, source_target_pairs={{0,2},{1,3},{2,0},{3,1},{4,6},{5,7},{6,4},{7,5},{8,10},{9,11},{10,... | collective-permute-start | bytes 153608 | tf_op jit(solution)/shard_map/ppermute | solution.py:572
  9.8 4.1 %collective-permute-start.6 = (bf16[4,6400]{1,0:T(4,128)(2,1)S(1)}, bf16[4,6400]{1,0:T(4,128)(2,1)S(1)}, u32[]{:S(2)}, u32[]{:S(2)}) collective-permute-start(bf16[4,6400]{1,0:T(4,128)(2,1)S(1)} %collective-permute-done), channel_id=1, source_target_pairs={{0,2},{1,3},{2,0},{3,1},{4,6},{5,7},{6,4},{7,5},{8,10},{9,11},{10,... | collective-permute-start | bytes 153608 | tf_op jit(solution)/shard_map/ppermute | solution.py:572
  11.6 6.7 %collective-permute-start.1 = (bf16[8,6400]{1,0:T(8,128)(2,1)S(1)}, bf16[8,6400]{1,0:T(8,128)(2,1)S(1)}, u32[]{:S(2)}, u32[]{:S(2)}) collective-permute-start(bf16[8,6400]{1,0:T(8,128)(2,1)S(1)} %pad_maximum_fusion.3), channel_id=1, source_target_pairs={{0,4},{1,5},{2,6},{3,7},{4,0},{5,1},{6,2},{7,3},{8,12},{9,13},{10,... | collective-permute-start | bytes 307208 | tf_op jit(solution)/shard_map/ppermute | solution.py:572
  12.8 4.1 %collective-permute-start.4 = (bf16[4,6400]{1,0:T(4,128)(2,1)S(1)}, bf16[4,6400]{1,0:T(4,128)(2,1)S(1)}, u32[]{:S(2)}, u32[]{:S(2)}) collective-permute-start(bf16[4,6400]{1,0:T(4,128)(2,1)S(1)} %collective-permute-done.3), channel_id=1, source_target_pairs={{0,4},{1,5},{2,6},{3,7},{4,0},{5,1},{6,2},{7,3},{8,12},{9,13},{10,... | collective-permute-start | bytes 153608 | tf_op jit(solution)/shard_map/ppermute | solution.py:572
  13.9 4.1 %collective-permute-start.7 = (bf16[4,6400]{1,0:T(4,128)(2,1)S(1)}, bf16[4,6400]{1,0:T(4,128)(2,1)S(1)}, u32[]{:S(2)}, u32[]{:S(2)}) collective-permute-start(bf16[4,6400]{1,0:T(4,128)(2,1)S(1)} %collective-permute-done.6), channel_id=1, source_target_pairs={{0,4},{1,5},{2,6},{3,7},{4,0},{5,1},{6,2},{7,3},{8,12},{9,13},{10,... | collective-permute-start | bytes 153608 | tf_op jit(solution)/shard_map/ppermute | solution.py:572
  15.4 4.3 %collective-permute-start.9 = (bf16[16,6400]{1,0:T(8,128)(2,1)S(1)}, bf16[16,6400]{1,0:T(8,128)(2,1)S(1)}, u32[]{:S(2)}, u32[]{:S(2)}) collective-permute-start(bf16[16,6400]{1,0:T(8,128)(2,1)S(1)} %pad_maximum_fusion.2.chunk_ref), channel_id=1, source_target_pairs={{0,1},{1,0},{2,3},{3,2},{4,5},{5,4},{6,7},{7,6},{8,9},{9,8},{10,11... | collective-permute-start | bytes 614408 | tf_op jit(solution)/shard_map/ppermute | solution.py:572
  16.9 1.7 %collective-permute-start.5 = (bf16[4,6400]{1,0:T(4,128)(2,1)S(1)}, bf16[4,6400]{1,0:T(4,128)(2,1)S(1)}, u32[]{:S(2)}, u32[]{:S(2)}) collective-permute-start(bf16[4,6400]{1,0:T(4,128)(2,1)S(1)} %collective-permute-done.4), channel_id=1, source_target_pairs={{0,1},{1,0},{2,3},{3,2},{4,5},{5,4},{6,7},{7,6},{8,9},{9,8},{10,11... | collective-permute-start | bytes 153608 | tf_op jit(solution)/shard_map/ppermute | solution.py:572
  18.0 1.2 %collective-permute-start.8 = (bf16[4,6400]{1,0:T(4,128)(2,1)S(1)}, bf16[4,6400]{1,0:T(4,128)(2,1)S(1)}, u32[]{:S(2)}, u32[]{:S(2)}) collective-permute-start(bf16[4,6400]{1,0:T(4,128)(2,1)S(1)} %collective-permute-done.7), channel_id=1, source_target_pairs={{0,1},{1,0},{2,3},{3,2},{4,5},{5,4},{6,7},{7,6},{8,9},{9,8},{10,11... | collective-permute-start | bytes 153608 | tf_op jit(solution)/shard_map/ppermute | solution.py:572
  18.3 1.3 %collective-permute-start.2 = (bf16[8,6400]{1,0:T(8,128)(2,1)S(1)}, bf16[8,6400]{1,0:T(8,128)(2,1)S(1)}, u32[]{:S(2)}, u32[]{:S(2)}) collective-permute-start(bf16[8,6400]{1,0:T(8,128)(2,1)S(1)} %collective-permute-done.1), channel_id=1, source_target_pairs={{0,1},{1,0},{2,3},{3,2},{4,5},{5,4},{6,7},{7,6},{8,9},{9,8},{10,11... | collective-permute-start | bytes 307208 | tf_op jit(solution)/shard_map/ppermute | solution.py:572

commit v8 on v7

--- a/solution.py
+++ b/solution.py
@@ -91,7 +91,7 @@
     return jnp.where(iota(want.shape[0], cols, 1) == want, 1.0, 0.0).astype(jnp.bfloat16)
 
 
-def meet(plan, own, assign_ref, target_ref, pick_ref, mine_ref, weight_ref):
+def meet(plan, own, assign_ref, target_ref, pick_ref, mine_ref, weight_ref, part, parts):
     me = lax.axis_index("pairs")
     pairs = GROUP * CAP
     stations = GROUP * own
@@ -122,7 +122,13 @@
         weight_ref[ch] = weight.astype(jnp.bfloat16)
         return carry
 
-    lax.fori_loop(0, pick_ref.shape[0], one_group, 0)
+    groups = pick_ref.shape[0]
+    low, high = part * groups // parts, (part + 1) * groups // parts
+    if high - low <= 2:
+        for ch in range(low, high):
+            one_group(ch, 0)
+    else:
+        lax.fori_loop(low, high, one_group, 0)
 
 
 def front_kernel(
@@ -150,10 +156,11 @@
     ]
     for load in names + loads:
         load.start()
+    loads[0].wait()
     for load in names:
         load.wait()
-    meet(plan, own, assign_ref, target_ref, pick_ref, mine_ref, weight_ref)
-    loads[0].wait()
+    who = functools.partial(meet, plan, own, assign_ref, target_ref, pick_ref, mine_ref, weight_ref)
+    who(0, 2)
     quarter = []
     for j in range(RADIX):
         per_comp = []
@@ -180,8 +187,12 @@
     straight = [halves(even + odd), halves(even - odd)]
     turned = halves(x0 - x2, x1 - x3)
 
+    for i in range(parts):
+        loads[1 + i].wait()
+    loads[1 + parts].wait()
+    who(1, 2)
+
     def tab(i):
-        loads[1 + i].wait()
         return tab_ref[part_at(i), :]
 
     spec = []
@@ -218,7 +229,6 @@
     taken = jnp.minimum(f + HALF, FREQ - 1) - jnp.maximum(f - HALF, 0) + 1
     share = 1.0 / (taken.astype(jnp.float32) * float(COMP))
     smooth = (sums[:rows] + sums[rows : 2 * rows] + sums[2 * rows :]) * share
-    loads[1 + parts].wait()
     row_at = lax.broadcasted_iota(jnp.int32, (rows, LANE), 0)
     flags = jnp.zeros((rows, LANE), jnp.float32)
     for w in range(windows):
@@ -427,9 +437,6 @@
                 lines.append(both * share)
             squares.append(jnp.concatenate(lines, 1))
         total = total + mm(weight_ref[number], jnp.concatenate(squares, 0).astype(jnp.bfloat16))
-        if kind["last"] and chunks == 1:
-            finish(total)
-
         if not isinstance(ch, int):
 
             @pl.when(ch >= 2)
@@ -478,8 +485,8 @@
         total = one_chunk(0, total)
     else:
         total = lax.fori_loop(0, chunks, one_chunk, total)
-        if kind["last"]:
-            finish(total)
+    if kind["last"]:
+        finish(total)
     if not kind["last"]:
         sum_ref[...] = total
     for cp in before + started:

time: 22.9 us -> 22.2 us (0.969)
  Pallas kernels: 6.84 us -> 6.17 us
    pallas_call x1, Pallas kernels: 2.4 us -> 1.84 us  [front(): pl.pallas_call(functools.partial(front_kernel, plan), out_shape=(jax.Shap...]
where the time goes in v8:
time: 22.2 us; the launch traced here: 22 us
  starting transfers between devices  11.4 us (51%)
  Pallas kernels  6.17 us (28%)
  waiting for transfers between devices  3.45 us (16%)
  between operations  0.72 us (3%)
  other arithmetic  0.3 us (1%)
    ppermute x10, starting transfers between devices, swap(): return lax.ppermute(block, 'pairs', [(i, i ^ mask) for i in range(owners)])  11.4 us
    pallas_call x4, Pallas kernels, correlate(): pl.pallas_call(functools.partial(correlate_kernel, plan, owners, own, win...  3.67 us
    ppermute x10, waiting for transfers between devices, swap(): return lax.ppermute(block, 'pairs', [(i, i ^ mask) for i in range(owners)])  3.45 us
    pallas_call x1, Pallas kernels, front(): pl.pallas_call(functools.partial(front_kernel, plan), out_shape=(jax.Shap...  1.84 us
    pallas_call x1, Pallas kernels, spread(): pl.pallas_call(spread_kernel, out_shape=(jax.ShapeDtypeStruct((rows, lane...  0.67 us
  transfers between devices with their start and end apart: 10, of which 6 were waited for; matrix products, arithmetic and copies ran while one was open for 1% of the time, Pallas kernels for 6%

profile of v8, /device:TPU:0, one launch (start us, length us, event | category | flops | bytes accessed | tf_op | source)
XLA Modules:
  0.0 22.0 jit_solution(9534879030275062950)
XLA Ops:
  0.6 0.0 copy-start
  0.6 1.8 %front.1 = (bf16[4,6400]{1,0:T(4,128)(2,1)S(1)}, bf16[4,16,16]{2,1,0:T(8,128)(2,1)S(1)}, bf16[4,32,4]{2,1,0:T(8,128)(2,1)S(1)}, bf16[4,4,32]{2,1,0:T(4,128)(2,1)S(1)}) custom-call(s32[2,4]{1,0:T(2,128)} %bitcast.4, s32[64]{0:T(128)} %assign_hbm.1, s32[16]{0:T(128)} %target_hbm.1, bf16[3,4,4096]{2,1,0:T(4,128)(2,1)} %bitcast.3, ...), custom_call_target="tpu_custom_call" | custom-call | tf_op jit(solution)/shard_map/front/pallas_call | solution.py:261
  2.5 4.1 %collective-permute-start = (bf16[4,6400]{1,0:T(4,128)(2,1)S(1)}, bf16[4,6400]{1,0:T(4,128)(2,1)S(1)}, u32[]{:S(2)}, u32[]{:S(2)}) collective-permute-start(bf16[4,6400]{1,0:T(4,128)(2,1)S(1)} %get-tuple-element.16.self_ref), channel_id=1, source_target_pairs={{0,8},{1,9},{2,10},{3,11},{4,12},{5,13},{6,14},{7,15},{8,0},{9,1},... | collective-permute-start | bytes 153608 | tf_op jit(solution)/shard_map/ppermute | solution.py:579
  6.6 1.5 %collective-permute-start.3 = (bf16[4,6400]{1,0:T(4,128)(2,1)S(1)}, bf16[4,6400]{1,0:T(4,128)(2,1)S(1)}, u32[]{:S(2)}, u32[]{:S(2)}) collective-permute-start(bf16[4,6400]{1,0:T(4,128)(2,1)S(1)} %get-tuple-element.16.self_ref), channel_id=1, source_target_pairs={{0,2},{1,3},{2,0},{3,1},{4,6},{5,7},{6,4},{7,5},{8,10},{9,11},{10,... | collective-permute-start | bytes 153608 | tf_op jit(solution)/shard_map/ppermute | solution.py:579
  8.1 0.7 %spread.1 = (bf16[32,6400]{1,0:T(8,128)(2,1)S(1)}, bf16[4,32,6400]{2,1,0:T(8,128)(2,1)S(1)}) custom-call(bf16[4,32,4]{2,1,0:T(8,128)(2,1)S(1)} %get-tuple-element.17.mine_ref, bf16[4,6400]{1,0:T(4,128)(2,1)S(1)} %get-tuple-element.16.self_ref), custom_call_target="tpu_custom_call" | custom-call | flops 8192000 | bytes 2048000 | tf_op jit(solution)/shard_map/spread/pallas_call | solution.py:306
  8.8 0.4 %collective-permute-done = bf16[4,6400]{1,0:T(4,128)(2,1)S(1)} collective-permute-done((bf16[4,6400]{1,0:T(4,128)(2,1)S(1)}, bf16[4,6400]{1,0:T(4,128)(2,1)S(1)}, u32[]{:S(2)}, u32[]{:S(2)}) %collective-permute-start) | collective-permute-done | bytes 51232 | tf_op jit(solution)/shard_map/ppermute | solution.py:579
  9.3 1.7 %collective-permute-start.6 = (bf16[4,6400]{1,0:T(4,128)(2,1)S(1)}, bf16[4,6400]{1,0:T(4,128)(2,1)S(1)}, u32[]{:S(2)}, u32[]{:S(2)}) collective-permute-start(bf16[4,6400]{1,0:T(4,128)(2,1)S(1)} %collective-permute-done), channel_id=1, source_target_pairs={{0,2},{1,3},{2,0},{3,1},{4,6},{5,7},{6,4},{7,5},{8,10},{9,11},{10,... | collective-permute-start | bytes 153608 | tf_op jit(solution)/shard_map/ppermute | solution.py:579
  11.0 0.1 pad_maximum_fusion.3
  11.0 1.2 %collective-permute-start.1 = (bf16[8,6400]{1,0:T(8,128)(2,1)S(1)}, bf16[8,6400]{1,0:T(8,128)(2,1)S(1)}, u32[]{:S(2)}, u32[]{:S(2)}) collective-permute-start(bf16[8,6400]{1,0:T(8,128)(2,1)S(1)} %pad_maximum_fusion.3), channel_id=1, source_target_pairs={{0,4},{1,5},{2,6},{3,7},{4,0},{5,1},{6,2},{7,3},{8,12},{9,13},{10,... | collective-permute-start | bytes 307208 | tf_op jit(solution)/shard_map/ppermute | solution.py:579
  12.3 0.0 collective-permute-done.3
  12.3 0.9 %collective-permute-start.4 = (bf16[4,6400]{1,0:T(4,128)(2,1)S(1)}, bf16[4,6400]{1,0:T(4,128)(2,1)S(1)}, u32[]{:S(2)}, u32[]{:S(2)}) collective-permute-start(bf16[4,6400]{1,0:T(4,128)(2,1)S(1)} %collective-permute-done.3), channel_id=1, source_target_pairs={{0,4},{1,5},{2,6},{3,7},{4,0},{5,1},{6,2},{7,3},{8,12},{9,13},{10,... | collective-permute-start | bytes 153608 | tf_op jit(solution)/shard_map/ppermute | solution.py:579
  13.1 0.2 %collective-permute-done.6 = bf16[4,6400]{1,0:T(4,128)(2,1)S(1)} collective-permute-done((bf16[4,6400]{1,0:T(4,128)(2,1)S(1)}, bf16[4,6400]{1,0:T(4,128)(2,1)S(1)}, u32[]{:S(2)}, u32[]{:S(2)}) %collective-permute-start.6) | collective-permute-done | bytes 51232 | tf_op jit(solution)/shard_map/ppermute | solution.py:579
  13.4 1.4 %collective-permute-start.7 = (bf16[4,6400]{1,0:T(4,128)(2,1)S(1)}, bf16[4,6400]{1,0:T(4,128)(2,1)S(1)}, u32[]{:S(2)}, u32[]{:S(2)}) collective-permute-start(bf16[4,6400]{1,0:T(4,128)(2,1)S(1)} %collective-permute-done.6), channel_id=1, source_target_pairs={{0,4},{1,5},{2,6},{3,7},{4,0},{5,1},{6,2},{7,3},{8,12},{9,13},{10,... | collective-permute-start | bytes 153608 | tf_op jit(solution)/shard_map/ppermute | solution.py:579
  14.7 0.1 pad_maximum_fusion.2.chunk_ref
  14.9 0.1 collective-permute-start.9
  14.9 1.4 %collective-permute-done.4 = bf16[4,6400]{1,0:T(4,128)(2,1)S(1)} collective-permute-done((bf16[4,6400]{1,0:T(4,128)(2,1)S(1)}, bf16[4,6400]{1,0:T(4,128)(2,1)S(1)}, u32[]{:S(2)}, u32[]{:S(2)}) %collective-permute-start.4) | collective-permute-done | bytes 51232 | tf_op jit(solution)/shard_map/ppermute | solution.py:579
  16.4 0.0 collective-permute-start.5
  16.4 0.0 copy-done
  16.4 0.8 %correlate.4 = (bf16[4,4,9,2,256]{4,3,2,1,0:T(2,128)(2,1)S(1)}, f32[4,1152]{1,0:T(4,128)S(1)}) custom-call(bf16[16,6400]{1,0:T(8,128)(2,1)S(1)} %pad_maximum_fusion.2.chunk_ref, bf16[32,6400]{1,0:T(8,128)(2,1)S(1)} %get-tuple-element.18.refs_0_, bf16[4,32,6400]{2,1,0:T(8,128)(2,1)S(1)} %get-tuple-element.19.refs_1_, ...), custom_call_target="tpu_custom_call" | custom-call | flops 301989888 | bytes 294912 | tf_op jit(solution)/shard_map/correlate/pallas_call | solution.py:541
  17.2 0.3 %collective-permute-done.7 = bf16[4,6400]{1,0:T(4,128)(2,1)S(1)} collective-permute-done((bf16[4,6400]{1,0:T(4,128)(2,1)S(1)}, bf16[4,6400]{1,0:T(4,128)(2,1)S(1)}, u32[]{:S(2)}, u32[]{:S(2)}) %collective-permute-start.7) | collective-permute-done | bytes 51232 | tf_op jit(solution)/shard_map/ppermute | solution.py:579
  17.5 0.3 %collective-permute-start.8 = (bf16[4,6400]{1,0:T(4,128)(2,1)S(1)}, bf16[4,6400]{1,0:T(4,128)(2,1)S(1)}, u32[]{:S(2)}, u32[]{:S(2)}) collective-permute-start(bf16[4,6400]{1,0:T(4,128)(2,1)S(1)} %collective-permute-done.7), channel_id=1, source_target_pairs={{0,1},{1,0},{2,3},{3,2},{4,5},{5,4},{6,7},{7,6},{8,9},{9,8},{10,11... | collective-permute-start | bytes 153608 | tf_op jit(solution)/shard_map/ppermute | solution.py:579
  17.7 0.0 collective-permute-done.1
  17.7 0.2 %collective-permute-start.2 = (bf16[8,6400]{1,0:T(8,128)(2,1)S(1)}, bf16[8,6400]{1,0:T(8,128)(2,1)S(1)}, u32[]{:S(2)}, u32[]{:S(2)}) collective-permute-start(bf16[8,6400]{1,0:T(8,128)(2,1)S(1)} %collective-permute-done.1), channel_id=1, source_target_pairs={{0,1},{1,0},{2,3},{3,2},{4,5},{5,4},{6,7},{7,6},{8,9},{9,8},{10,11... | collective-permute-start | bytes 307208 | tf_op jit(solution)/shard_map/ppermute | solution.py:579
  18.0 0.1 pad_maximum_fusion.1.chunk_ref
  18.1 0.0 collective-permute-done.5
  18.1 0.6 %collective-permute-done.8 = bf16[4,6400]{1,0:T(4,128)(2,1)S(1)} collective-permute-done((bf16[4,6400]{1,0:T(4,128)(2,1)S(1)}, bf16[4,6400]{1,0:T(4,128)(2,1)S(1)}, u32[]{:S(2)}, u32[]{:S(2)}) %collective-permute-start.8) | collective-permute-done | bytes 51232 | tf_op jit(solution)/shard_map/ppermute | solution.py:579
  18.7 0.3 %collective-permute-done.2 = bf16[8,6400]{1,0:T(8,128)(2,1)S(1)} collective-permute-done((bf16[8,6400]{1,0:T(8,128)(2,1)S(1)}, bf16[8,6400]{1,0:T(8,128)(2,1)S(1)}, u32[]{:S(2)}, u32[]{:S(2)}) %collective-permute-start.2) | collective-permute-done | bytes 102432 | tf_op jit(solution)/shard_map/ppermute | solution.py:579
  19.1 0.1 pad_maximum_fusion.chunk_ref
  19.1 0.0 collective-permute-done.9.chunk_ref
  19.1 0.7 %correlate.5 = (bf16[4,4,9,2,256]{4,3,2,1,0:T(2,128)(2,1)S(1)}, f32[4,1152]{1,0:T(4,128)S(1)}) custom-call(bf16[16,6400]{1,0:T(8,128)(2,1)S(1)} %collective-permute-done.9.chunk_ref, bf16[32,6400]{1,0:T(8,128)(2,1)S(1)} %get-tuple-element.18.refs_0_, bf16[4,32,6400]{2,1,0:T(8,128)(2,1)S(1)} %get-tuple-element.19.refs_1_, ...), custom_call_target="tpu_custom_call" | custom-call | flops 301989888 | bytes 294912 | tf_op jit(solution)/shard_map/correlate/pallas_call | solution.py:541
  19.9 0.7 %correlate.6 = (bf16[4,4,9,2,256]{4,3,2,1,0:T(2,128)(2,1)S(1)}, f32[4,1152]{1,0:T(4,128)S(1)}) custom-call(bf16[16,6400]{1,0:T(8,128)(2,1)S(1)} %pad_maximum_fusion.1.chunk_ref, bf16[32,6400]{1,0:T(8,128)(2,1)S(1)} %get-tuple-element.18.refs_0_, bf16[4,32,6400]{2,1,0:T(8,128)(2,1)S(1)} %get-tuple-element.19.refs_1_, ...), custom_call_target="tpu_custom_call" | custom-call | flops 301989888 | bytes 294912 | tf_op jit(solution)/shard_map/correlate/pallas_call | solution.py:541
  20.6 1.4 %correlate.7 = (bf16[4,16,9,2,256]{4,3,2,1,0:T(2,128)(2,1)}, f32[4,9]{1,0:T(4,128)}) custom-call(bf16[16,6400]{1,0:T(8,128)(2,1)S(1)} %pad_maximum_fusion.chunk_ref, bf16[32,6400]{1,0:T(8,128)(2,1)S(1)} %get-tuple-element.18.refs_0_, bf16[4,32,6400]{2,1,0:T(8,128)(2,1)S(1)} %get-tuple-element.19.refs_1_, bf16[4,16,16]{2,1,0:T(8,128)(2,1)S(1)} %get-tuple-element.20.refs_2_, ...), custom_call_target="tpu_custom_call" | custom-call | flops 301989888 | bytes 294912 | tf_op jit(solution)/shard_map/correlate/pallas_call | solution.py:541
Async XLA Ops:
  0.6 15.8 %copy-start = (bf16[1024,256]{1,0:T(8,128)(2,1)S(1)}, bf16[1024,256]{1,0:T(8,128)(2,1)}, u32[]{:S(2)}) copy-start(bf16[1024,256]{1,0:T(8,128)(2,1)} %constant.4.clone.refs_4_) | copy-start | bytes 1572868
  2.5 6.8 %collective-permute-start = (bf16[4,6400]{1,0:T(4,128)(2,1)S(1)}, bf16[4,6400]{1,0:T(4,128)(2,1)S(1)}, u32[]{:S(2)}, u32[]{:S(2)}) collective-permute-start(bf16[4,6400]{1,0:T(4,128)(2,1)S(1)} %get-tuple-element.16.self_ref), channel_id=1, source_target_pairs={{0,8},{1,9},{2,10},{3,11},{4,12},{5,13},{6,14},{7,15},{8,0},{9,1},... | collective-permute-start | bytes 153608 | tf_op jit(solution)/shard_map/ppermute | solution.py:579
  6.6 5.6 %collective-permute-start.3 = (bf16[4,6400]{1,0:T(4,128)(2,1)S(1)}, bf16[4,6400]{1,0:T(4,128)(2,1)S(1)}, u32[]{:S(2)}, u32[]{:S(2)}) collective-permute-start(bf16[4,6400]{1,0:T(4,128)(2,1)S(1)} %get-tuple-element.16.self_ref), channel_id=1, source_target_pairs={{0,2},{1,3},{2,0},{3,1},{4,6},{5,7},{6,4},{7,5},{8,10},{9,11},{10,... | collective-permute-start | bytes 153608 | tf_op jit(solution)/shard_map/ppermute | solution.py:579
  9.3 4.1 %collective-permute-start.6 = (bf16[4,6400]{1,0:T(4,128)(2,1)S(1)}, bf16[4,6400]{1,0:T(4,128)(2,1)S(1)}, u32[]{:S(2)}, u32[]{:S(2)}) collective-permute-start(bf16[4,6400]{1,0:T(4,128)(2,1)S(1)} %collective-permute-done), channel_id=1, source_target_pairs={{0,2},{1,3},{2,0},{3,1},{4,6},{5,7},{6,4},{7,5},{8,10},{9,11},{10,... | collective-permute-start | bytes 153608 | tf_op jit(solution)/shard_map/ppermute | solution.py:579
  11.0 6.7 %collective-permute-start.1 = (bf16[8,6400]{1,0:T(8,128)(2,1)S(1)}, bf16[8,6400]{1,0:T(8,128)(2,1)S(1)}, u32[]{:S(2)}, u32[]{:S(2)}) collective-permute-start(bf16[8,6400]{1,0:T(8,128)(2,1)S(1)} %pad_maximum_fusion.3), channel_id=1, source_target_pairs={{0,4},{1,5},{2,6},{3,7},{4,0},{5,1},{6,2},{7,3},{8,12},{9,13},{10,... | collective-permute-start | bytes 307208 | tf_op jit(solution)/shard_map/ppermute | solution.py:579
  12.3 4.1 %collective-permute-start.4 = (bf16[4,6400]{1,0:T(4,128)(2,1)S(1)}, bf16[4,6400]{1,0:T(4,128)(2,1)S(1)}, u32[]{:S(2)}, u32[]{:S(2)}) collective-permute-start(bf16[4,6400]{1,0:T(4,128)(2,1)S(1)} %collective-permute-done.3), channel_id=1, source_target_pairs={{0,4},{1,5},{2,6},{3,7},{4,0},{5,1},{6,2},{7,3},{8,12},{9,13},{10,... | collective-permute-start | bytes 153608 | tf_op jit(solution)/shard_map/ppermute | solution.py:579
  13.4 4.1 %collective-permute-start.7 = (bf16[4,6400]{1,0:T(4,128)(2,1)S(1)}, bf16[4,6400]{1,0:T(4,128)(2,1)S(1)}, u32[]{:S(2)}, u32[]{:S(2)}) collective-permute-start(bf16[4,6400]{1,0:T(4,128)(2,1)S(1)} %collective-permute-done.6), channel_id=1, source_target_pairs={{0,4},{1,5},{2,6},{3,7},{4,0},{5,1},{6,2},{7,3},{8,12},{9,13},{10,... | collective-permute-start | bytes 153608 | tf_op jit(solution)/shard_map/ppermute | solution.py:579
  14.9 4.3 %collective-permute-start.9 = (bf16[16,6400]{1,0:T(8,128)(2,1)S(1)}, bf16[16,6400]{1,0:T(8,128)(2,1)S(1)}, u32[]{:S(2)}, u32[]{:S(2)}) collective-permute-start(bf16[16,6400]{1,0:T(8,128)(2,1)S(1)} %pad_maximum_fusion.2.chunk_ref), channel_id=1, source_target_pairs={{0,1},{1,0},{2,3},{3,2},{4,5},{5,4},{6,7},{7,6},{8,9},{9,8},{10,11... | collective-permute-start | bytes 614408 | tf_op jit(solution)/shard_map/ppermute | solution.py:579
  16.4 1.7 %collective-permute-start.5 = (bf16[4,6400]{1,0:T(4,128)(2,1)S(1)}, bf16[4,6400]{1,0:T(4,128)(2,1)S(1)}, u32[]{:S(2)}, u32[]{:S(2)}) collective-permute-start(bf16[4,6400]{1,0:T(4,128)(2,1)S(1)} %collective-permute-done.4), channel_id=1, source_target_pairs={{0,1},{1,0},{2,3},{3,2},{4,5},{5,4},{6,7},{7,6},{8,9},{9,8},{10,11... | collective-permute-start | bytes 153608 | tf_op jit(solution)/shard_map/ppermute | solution.py:579
  17.5 1.2 %collective-permute-start.8 = (bf16[4,6400]{1,0:T(4,128)(2,1)S(1)}, bf16[4,6400]{1,0:T(4,128)(2,1)S(1)}, u32[]{:S(2)}, u32[]{:S(2)}) collective-permute-start(bf16[4,6400]{1,0:T(4,128)(2,1)S(1)} %collective-permute-done.7), channel_id=1, source_target_pairs={{0,1},{1,0},{2,3},{3,2},{4,5},{5,4},{6,7},{7,6},{8,9},{9,8},{10,11... | collective-permute-start | bytes 153608 | tf_op jit(solution)/shard_map/ppermute | solution.py:579
  17.7 1.3 %collective-permute-start.2 = (bf16[8,6400]{1,0:T(8,128)(2,1)S(1)}, bf16[8,6400]{1,0:T(8,128)(2,1)S(1)}, u32[]{:S(2)}, u32[]{:S(2)}) collective-permute-start(bf16[8,6400]{1,0:T(8,128)(2,1)S(1)} %collective-permute-done.1), channel_id=1, source_target_pairs={{0,1},{1,0},{2,3},{3,2},{4,5},{5,4},{6,7},{7,6},{8,9},{9,8},{10,11... | collective-permute-start | bytes 307208 | tf_op jit(solution)/shard_map/ppermute | solution.py:579
